TPU v7x, 32 devices: a whole 2x2x4 slice. The times are simulated.
32 devices in a mesh: ctx: 16 (over z, x, core), fsdp: 2 (over y).
Axes of the slice: x: 2, y: 2, z: 4, core: 2. Of those that a mesh axis runs over, the one named last changes fastest.
Arguments:
- inputs: bfloat16 [2, 2048, 1280], P('fsdp', 'ctx'), may hold values from -6 to 6
- norm1_gain: bfloat16 [1280], P('fsdp'), may hold values from 0.099609375 to 1.8984375
- w_query: bfloat16 [1280, 1280], P('fsdp'), may hold values from -0.15625 to 0.15625
- w_key: bfloat16 [1280, 1280], P('fsdp'), may hold values from -0.15625 to 0.15625
- w_value: bfloat16 [1280, 1280], P('fsdp'), may hold values from -0.15625 to 0.15625
- w_output: bfloat16 [1280, 1280], P('fsdp'), may hold values from -0.625 to 0.625
- norm2_gain: bfloat16 [1280], P('fsdp'), may hold values from 0.099609375 to 1.8984375
- router: bfloat16 [1280, 16], P('fsdp'), may hold values from -0.083984375 to 0.083984375
- shared_gate_up_weight: bfloat16 [1280, 1792], P('fsdp'), may hold values from -0.15625 to 0.15625
- shared_down_weight: bfloat16 [896, 1280], P('fsdp'), may hold values from -0.1875 to 0.1875
- expert_in: bfloat16 [16, 1280, 1792], P('ctx', 'fsdp'), may hold values from -0.15625 to 0.15625
- expert_out: bfloat16 [16, 896, 1280], P('ctx', 'fsdp'), may hold values from -0.1875 to 0.1875
- picks: int32 [2, 2048, 7], P('fsdp', 'ctx'), may hold values from 0 to 15, all different within a row
- fill_order: int32 [2, 16, 896], P('fsdp', 'ctx'), may hold values from 0 to 895, each once within a row
- grad_out: bfloat16 [2, 2048, 1280], P('fsdp', 'ctx'), may hold values from -6 to 6
Outputs:
- layer_out: bfloat16 [2, 2048, 1280], P('fsdp', 'ctx')
- grad_inputs: float32 [2, 2048, 1280], P('fsdp', 'ctx')
- grad_norm1: float32 [1280], P('fsdp')
- grad_query: float32 [1280, 1280], P('fsdp')
- grad_key: float32 [1280, 1280], P('fsdp')
- grad_value: float32 [1280, 1280], P('fsdp')
- grad_output: float32 [1280, 1280], P('fsdp')
- grad_norm2: float32 [1280], P('fsdp')
- grad_router: float32 [1280, 16], P('fsdp')
- grad_shared_in: float32 [1280, 1792], P('fsdp')
- grad_shared_out: float32 [896, 1280], P('fsdp')
- grad_expert_in: float32 [16, 1280, 1792], P('ctx', 'fsdp')
- grad_expert_out: float32 [16, 896, 1280], P('ctx', 'fsdp')
Inputs may be any that keep to these rules, and one draw needn't show every extreme that they name: Each token's 7 picks name different experts, and every expert is picked by some token. `fill_order`: for each sequence and run c, the 896 entries are a permutation; entry t * 7 + k belongs to token c * 128 + t and its k-th pick.
All inputs are finite; a program needn't handle non-finite values.
Results may differ from a plain program's by a relative error of at most 0.018.
Values may be sent and summed in bfloat16 or wider, within the bound.
No kernel may reach another device: no remote copies, remote signals or barrier semaphores. Data moves between devices by JAX's collectives and lax.ppermute only.
A program may use at most 320 MiB of HBM per device.

v0:
```python
import functools
import math

import jax
import jax.numpy as jnp
from jax import lax
from jax.experimental import pallas as pl
from jax.experimental.layout import Layout, with_layout_constraint
from jax.experimental.pallas import tpu as pltpu
from jax.sharding import PartitionSpec as P

HEADS = 10
HEAD_DIM = 128
EXP_HID = 896
TOP = 7
BLOCK = 256
TILE = 512

epsilon = 1e-06
masked_score = -1000000000.0
score_scale = 1.0 / math.sqrt(HEAD_DIM)
exact = lax.Precision.HIGHEST
f32 = jnp.float32
bf16 = jnp.bfloat16


def dot(a, b):
    return jnp.dot(a, b, preferred_element_type=f32)


def dot_nt(a, b):
    return lax.dot_general(a, b, (((1,), (1,)), ((), ())), preferred_element_type=f32)


def dot_tn(a, b):
    return lax.dot_general(a, b, (((0,), (0,)), ((), ())), preferred_element_type=f32)


def rms_scale(values):
    return lax.rsqrt(jnp.mean(values * values, axis=-1, keepdims=True) + epsilon)


def rotary_tables(starts, count, width):
    half = width // 2
    freqs = jnp.exp(-math.log(10000.0) * jnp.arange(half, dtype=f32) * 2.0 / width)
    first = starts.astype(f32)[:, None] * freqs[None, :]
    second = jnp.arange(count, dtype=f32)[:, None] * freqs[None, :]
    angles = jnp.concatenate([first, second], axis=0)
    cosine, sine = lax.optimization_barrier((jnp.cos(angles), jnp.sin(angles)))
    spans = starts.shape[0]
    cos_a, sin_a = cosine[:spans, None], sine[:spans, None]
    cos_b, sin_b = cosine[None, spans:], sine[None, spans:]
    cosine = (cos_a * cos_b - sin_a * sin_b).reshape(spans * count, half)
    sine = (sin_a * cos_b + cos_a * sin_b).reshape(spans * count, half)
    return (
        jnp.concatenate([cosine, cosine], axis=1),
        jnp.concatenate([-sine, sine], axis=1),
    )


def allowed_tile(rows, columns):
    key_block = lax.broadcasted_iota(jnp.int32, (rows, columns), 0) // BLOCK
    query_block = lax.broadcasted_iota(jnp.int32, (rows, columns), 1) // BLOCK
    return key_block <= query_block


def ring_of(spans):
    if spans != 16:
        return list(range(spans))
    chips = [0, 2, 4, 6, 7, 5, 3, 1]
    return [2 * chip + core for chip in chips for core in (0, 1)]


def pieces(j, tile, length, ring):
    if ring:
        starts = (j * BLOCK, length - BLOCK - j * BLOCK)
        return [pl.ds(pl.multiple_of(at, BLOCK), BLOCK) for at in starts]
    return [pl.ds(pl.multiple_of(j * tile, tile), tile)]


def load(ref, windows, columns=slice(None)):
    parts = [ref[window, columns] for window in windows]
    return parts[0] if len(parts) == 1 else jnp.concatenate(parts, axis=0)


def store(ref, windows, value, columns=slice(None)):
    size = value.shape[0] // len(windows)
    for i, window in enumerate(windows):
        ref[window, columns] = value[i * size : (i + 1) * size]


def attend_kernel(
    ring, q_ref, k_ref, v_ref, context_ref, lse_ref, low_ref, score_ref
):
    length = k_ref.shape[0]
    tile = context_ref.shape[0]
    here = pl.program_id(0)
    queries = load(q_ref, pieces(here, tile, length, ring))

    def raw_scores(j):
        return dot_nt(load(k_ref, pieces(j, tile, length, ring)), queries) * score_scale

    def fold(j, scores, peak):
        score_ref[pl.ds(pl.multiple_of(j * tile, tile), tile), :] = scores
        return jnp.maximum(peak, jnp.max(scores.reshape(tile // 8, 8, tile), axis=0))

    diagonal = jnp.where(allowed_tile(tile, tile), raw_scores(here), masked_score)
    peak = fold(here, diagonal, jnp.full((8, tile), masked_score, f32))
    peak = lax.fori_loop(0, here, lambda j, p: fold(j, raw_scores(j), p), peak)
    top = jnp.max(peak, axis=0, keepdims=True)

    def gather(j, carry):
        total, numer = carry
        weights = jnp.exp(score_ref[pl.ds(pl.multiple_of(j * tile, tile), tile), :] - top)
        total = total + jnp.sum(weights.reshape(tile // 8, 8, tile), axis=0)
        values = load(v_ref, pieces(j, tile, length, ring))
        return total, numer + dot_tn(values, weights.astype(bf16))

    zero = (jnp.zeros((8, tile), f32), jnp.zeros((HEAD_DIM, tile), f32))
    total, numer = lax.fori_loop(0, here + 1, gather, zero)
    total = jnp.sum(total, axis=0, keepdims=True)
    context = (numer / total).T
    context_ref[...] = context
    low_ref[...] = context.astype(bf16)
    lse_ref[...] = top + jnp.log(total)


def attend(query, key, value, ring):
    length = query.shape[0]
    tile = min(TILE, length)
    whole = pl.BlockSpec((length, HEAD_DIM), lambda i: (0, 0))
    part = pl.BlockSpec((tile, HEAD_DIM), lambda i: (i, 0))
    return pl.pallas_call(
        functools.partial(attend_kernel, ring),
        grid=(length // tile,),
        in_specs=[whole] * 3,
        out_specs=[part, pl.BlockSpec((1, tile), lambda i: (0, i)), part],
        out_shape=[
            jax.ShapeDtypeStruct((length, HEAD_DIM), f32),
            jax.ShapeDtypeStruct((1, length), f32),
            jax.ShapeDtypeStruct((length, HEAD_DIM), bf16),
        ],
        scratch_shapes=[pltpu.VMEM((length, tile), f32)],
        name="attend",
        cost_estimate=pl.CostEstimate(
            flops=2 * length * length * HEAD_DIM,
            bytes_accessed=12 * length * HEAD_DIM,
            transcendentals=length * length // 2,
        ),
    )(query, key, value)


def attend_back_kernel(
    ring,
    q_ref,
    k_ref,
    v_ref,
    grad_ref,
    context_ref,
    lse_ref,
    cos_ref,
    sin_ref,
    out_ref,
    out_ring_ref,
    dq_ref,
    delta_ref,
    dk_ref,
    dv_ref,
):
    length = q_ref.shape[0]
    tile = dk_ref.shape[0]
    steps = length // tile
    here = pl.program_id(0)

    def natural(i):
        return pl.ds(pl.multiple_of(i * tile, tile), tile)

    @pl.when(here == 0)
    def _():
        def prepare(i, carry):
            window = natural(i)
            dq_ref[window, :] = jnp.zeros((tile, HEAD_DIM), f32)
            product = grad_ref[window, :].astype(f32) * context_ref[window, :]
            ones = jnp.ones((8, HEAD_DIM), f32)
            delta = lax.dot_general(
                ones, product, (((1,), (1,)), ((), ())), precision=exact, preferred_element_type=f32
            )
            delta_ref[:, window] = delta
            return carry

        lax.fori_loop(0, steps, prepare, 0)

    keys = load(k_ref, pieces(here, tile, length, ring))
    values = load(v_ref, pieces(here, tile, length, ring))

    dk_ref[...] = jnp.zeros_like(dk_ref)
    dv_ref[...] = jnp.zeros_like(dv_ref)

    def visit(i, carry):
        window = natural(i)
        queries = load(q_ref, pieces(i, tile, length, ring))
        grads = grad_ref[window, :]
        weights = jnp.exp(dot_nt(keys, queries) * score_scale - lse_ref[:, window])
        later = jnp.where(i > here, weights[BLOCK:, :BLOCK], 0.0)
        later = jnp.concatenate([later, weights[BLOCK:, BLOCK:]], axis=1)
        weights = jnp.concatenate([weights[:BLOCK], later], axis=0)
        grad_weights = dot_nt(values, grads)
        grad_raw = (weights * (grad_weights - delta_ref[0:1, window]) * score_scale).astype(bf16)
        dq_ref[window, :] += dot_tn(grad_raw, keys)
        dk_ref[...] += dot(grad_raw, queries)
        dv_ref[...] += dot(weights.astype(bf16), grads)
        return carry

    lax.fori_loop(here, steps, visit, 0)

    def write(i, part, value):
        at = slice(part * HEAD_DIM, (part + 1) * HEAD_DIM)
        out_ref[natural(i), at] = value
        store(out_ring_ref, pieces(i, tile, length, ring), value, at)

    def turned_back(i, value):
        windows = pieces(i, tile, length, ring)
        scaled = pltpu.roll(value * load(sin_ref, windows), HEAD_DIM // 2, 1)
        return (value * load(cos_ref, windows) + scaled).astype(bf16)

    write(here, 1, turned_back(here, dk_ref[...]))
    write(here, 2, dv_ref[...].astype(bf16))

    @pl.when(here == steps - 1)
    def _():
        def finish(i, carry):
            write(i, 0, turned_back(i, dq_ref[natural(i), :]))
            return carry

        lax.fori_loop(0, steps, finish, 0)


def attend_back(query, key, value, grad, context, lse, cosine, sine, ring):
    length = query.shape[0]
    tile = min(TILE, length)
    memory = pl.BlockSpec(memory_space=pltpu.VMEM)
    return pl.pallas_call(
        functools.partial(attend_back_kernel, ring),
        grid=(length // tile,),
        in_specs=[memory] * 8,
        out_specs=[memory] * 2,
        out_shape=[jax.ShapeDtypeStruct((length, 3 * HEAD_DIM), bf16)] * 2,
        scratch_shapes=[
            pltpu.VMEM((length, HEAD_DIM), f32),
            pltpu.VMEM((8, length), f32),
            pltpu.VMEM((tile, HEAD_DIM), f32),
            pltpu.VMEM((tile, HEAD_DIM), f32),
        ],
        name="attend_back",
        cost_estimate=pl.CostEstimate(
            flops=5 * length * length * HEAD_DIM,
            bytes_accessed=20 * length * HEAD_DIM,
            transcendentals=length * length // 2,
        ),
    )(query, key, value, grad, context, lse, cosine, sine)


def project_kernel(
    side_ref, x_ref, gain_ref, own_ref, other_ref, cos_ref, sin_ref, normed_ref, q_ref, k_ref, v_ref
):
    own, other = own_ref[...], other_ref[...]
    weight = jnp.where(
        side_ref[0] == 0,
        jnp.concatenate([own, other], axis=0),
        jnp.concatenate([other, own], axis=0),
    )
    resid = x_ref[...].astype(f32)
    normed = (resid * rms_scale(resid) * gain_ref[...]).astype(bf16)
    normed_ref[...] = normed
    projected = dot(normed, weight)
    for out, at in ((q_ref, 0), (k_ref, HEAD_DIM)):
        part = projected[:, at : at + HEAD_DIM]
        turned = pltpu.roll(part, HEAD_DIM // 2, 1)
        out[...] = (part * cos_ref[...] + turned * sin_ref[...]).astype(bf16)
    v_ref[...] = projected[:, 2 * HEAD_DIM :].astype(bf16)


def project(side, x, gain, own, other, cosine, sine):
    length, width = x.shape
    tile = min(TILE // 2, length)
    part = pl.BlockSpec((tile, HEAD_DIM), lambda i: (i, 0))
    wide = pl.BlockSpec((tile, width), lambda i: (i, 0))
    return pl.pallas_call(
        project_kernel,
        grid=(length // tile,),
        in_specs=[
            pl.BlockSpec(memory_space=pltpu.SMEM),
            wide,
            pl.BlockSpec((1, width), lambda i: (0, 0)),
            pl.BlockSpec(own.shape, lambda i: (0, 0)),
            pl.BlockSpec(own.shape, lambda i: (0, 0)),
            part,
            part,
        ],
        out_specs=[wide, part, part, part],
        out_shape=[jax.ShapeDtypeStruct((length, width), bf16)]
        + [jax.ShapeDtypeStruct((length, HEAD_DIM), bf16)] * 3,
        name="project",
        cost_estimate=pl.CostEstimate(
            flops=6 * length * width * HEAD_DIM,
            bytes_accessed=4 * length * width,
            transcendentals=0,
        ),
    )(side.reshape(1), x, gain, own, other, cosine, sine)


def home(head, spans):
    if spans != 16:
        return head
    chip, core = head // 2, head % 2
    return 2 * jnp.where(chip < 4, 2 * chip, 15 - 2 * chip) + core


def head_pair(side, spans, i):
    count = HEADS // 2
    low, high = home(i, spans), home(count + i, spans)
    mine = jnp.where(side == 0, low, high)
    theirs = jnp.where(side == 0, high, low)
    return mine, theirs, pl.ds(pl.multiple_of(i * HEAD_DIM, HEAD_DIM), HEAD_DIM)


def mix_kernel(
    experts,
    spot_ref,
    got_ref,
    own_ref,
    near_ref,
    far_ref,
    x_ref,
    gain_ref,
    router_ref,
    table_ref,
    second_ref,
    low_ref,
    scale_ref,
    gates_ref,
    attended_ref,
    near_sum_ref,
    far_sum_ref,
):
    ring = ring_of(got_ref.shape[0])
    for h in range(HEADS):
        attended_ref[:, h * HEAD_DIM : (h + 1) * HEAD_DIM] = got_ref[ring[h]]
    second = x_ref[...].astype(f32)
    tokens, width = second.shape
    half = near_ref.shape[1]
    second_ref[...] = second
    near_sum_ref[...] = jnp.zeros((tokens, half), f32)
    far_sum_ref[...] = jnp.zeros((tokens, half), f32)

    def visit(i, carry):
        mine, theirs, at = head_pair(spot_ref[0], got_ref.shape[0], i)
        second_ref[...] += dot(got_ref[mine], own_ref[at, :])
        near_sum_ref[...] += dot(got_ref[theirs], near_ref[at, :])
        far_sum_ref[...] += dot(got_ref[theirs], far_ref[at, :])
        return carry

    lax.fori_loop(0, HEADS // 2, visit, 0)
    second, near, far = second_ref[...], near_sum_ref[...], far_sum_ref[...]
    second += jnp.where(
        spot_ref[1] == 0,
        jnp.concatenate([near, far], axis=1),
        jnp.concatenate([far, near], axis=1),
    )
    scale = rms_scale(second)
    second_ref[...] = second
    scale_ref[...] = scale
    normed = (second * scale * gain_ref[...]).astype(bf16)
    logits = dot_nt(normed, router_ref[...])
    picked = table_ref[...] < tokens
    peak = jnp.max(jnp.where(picked, logits, masked_score), axis=-1, keepdims=True)
    chances = jnp.where(picked, jnp.exp(logits - peak), 0.0)
    gates = chances / jnp.sum(chances, axis=-1, keepdims=True)
    gates_ref[...] = gates
    high = gates.astype(bf16).astype(f32)
    rest = pltpu.roll(gates - high, experts, 1)
    low_ref[:, :width] = normed
    low_ref[:, width:] = (high + rest).astype(bf16)


def mix(spot, got, own, near, far, x, gain, router, table, experts):
    smem = pl.BlockSpec(memory_space=pltpu.SMEM)
    memory = pl.BlockSpec(memory_space=pltpu.VMEM)
    tokens, width = x.shape
    spare = table.shape[1]
    return pl.pallas_call(
        functools.partial(mix_kernel, experts),
        in_specs=[smem] + [memory] * 8,
        out_specs=[memory] * 5,
        out_shape=[
            jax.ShapeDtypeStruct(x.shape, f32),
            jax.ShapeDtypeStruct((tokens, width + spare), bf16),
            jax.ShapeDtypeStruct((tokens, 1), f32),
            jax.ShapeDtypeStruct((tokens, spare), f32),
            jax.ShapeDtypeStruct(x.shape, bf16),
        ],
        scratch_shapes=[pltpu.VMEM((tokens, width // 2), f32)] * 2,
        name="mix",
    )(spot, got, own, near, far, x, gain, router, table)


def mix_back_kernel(
    spot_ref,
    sums_ref,
    gates_ref,
    gate_grads_ref,
    router_ref,
    second_ref,
    scale_ref,
    gain_ref,
    g_ref,
    own_ref,
    near_ref,
    far_ref,
    send_ref,
    cuts_ref,
    grad_second_ref,
    out_ref,
):
    tokens, width = second_ref.shape
    second = second_ref[...]
    scale = scale_ref[...]
    gain = gain_ref[...]
    gates = gates_ref[...]
    gate_grads = gate_grads_ref[...]
    out_ref[...] = (second + sums_ref[:, width:].astype(f32)).astype(bf16)
    weighted = gates * gate_grads
    grad_sel = weighted - gates * jnp.sum(weighted, axis=-1, keepdims=True)
    grad_logits = grad_sel.astype(bf16)
    grad_normed = sums_ref[:, :width].astype(f32) + dot(grad_logits, router_ref[...])
    gain_part = jnp.sum(grad_normed * second * scale, axis=0, keepdims=True)
    hat = grad_normed * gain
    mean = jnp.mean(hat * second, axis=-1, keepdims=True)
    grad_second = g_ref[...].astype(f32) + scale * hat - second * (scale * scale * scale) * mean
    grad_second_ref[...] = grad_second
    grad_mixed = grad_second.astype(bf16)
    spans = send_ref.shape[0]
    cut = width // spans
    lane = lax.broadcasted_iota(jnp.int32, (1, HEAD_DIM), 1)
    high = gain_part.astype(bf16).astype(f32)
    row = lax.broadcasted_iota(jnp.int32, (16, width), 0)
    gain_rows = jnp.where(row == 0, high, jnp.where(row == 1, gain_part - high, 0.0))
    shifted = pltpu.roll(grad_logits.astype(f32), cut, 1)
    for k, c in enumerate(ring_of(spans)):
        start = min(c * cut // HEAD_DIM * HEAD_DIM, width - 2 * HEAD_DIM)
        shift = (start - c * cut) % (2 * HEAD_DIM)
        for value, rest, out_rows in (
            (grad_second, shifted, slice(0, tokens)),
            (gain_rows, 0.0, slice(tokens, tokens + 16)),
        ):
            window = pltpu.roll(value[:, start : start + 2 * HEAD_DIM], shift, 1)[:, :HEAD_DIM]
            window = jnp.where(lane < cut, window, 0.0) + rest
            cuts_ref[k, out_rows, :] = window.astype(bf16)
    left, right = grad_mixed[:, : width // 2], grad_mixed[:, width // 2 :]
    at_near = jnp.where(spot_ref[1] == 0, left, right)
    at_far = jnp.where(spot_ref[1] == 0, right, left)
    def visit(i, carry):
        mine, theirs, at = head_pair(spot_ref[0], spans, i)
        send_ref[mine] = dot_nt(grad_mixed, own_ref[at, :]).astype(bf16)
        other = dot_nt(at_near, near_ref[at, :]) + dot_nt(at_far, far_ref[at, :])
        send_ref[theirs] = other.astype(bf16)
        return carry

    lax.fori_loop(0, HEADS // 2, visit, 0)
    for h in ring_of(spans)[HEADS:]:
        send_ref[h] = jnp.zeros((tokens, HEAD_DIM), bf16)


def mix_back(spot, sums, gates, gate_grads, router, second, scale, gain, g, own, near, far, spans):
    tokens, width = second.shape
    smem = pl.BlockSpec(memory_space=pltpu.SMEM)
    memory = pl.BlockSpec(memory_space=pltpu.VMEM)
    return pl.pallas_call(
        mix_back_kernel,
        in_specs=[smem] + [memory] * 11,
        out_specs=[memory] * 4,
        out_shape=[
            jax.ShapeDtypeStruct((spans, tokens, HEAD_DIM), bf16),
            jax.ShapeDtypeStruct((spans, tokens + 16, HEAD_DIM), bf16),
            jax.ShapeDtypeStruct((tokens, width), f32),
            jax.ShapeDtypeStruct((tokens, width), bf16),
        ],
        name="mix_back",
    )(spot, sums, gates, gate_grads, router, second, scale, gain, g, own, near, far)


def inputs_back_kernel(
    side_ref,
    core_ref,
    got_ref,
    wq_ref,
    wk_ref,
    wv_ref,
    near_ref,
    far_ref,
    x_ref,
    gain_ref,
    grad_second_ref,
    out_ref,
    own_sum_ref,
    other_sum_ref,
):
    tokens, width = x_ref.shape
    half = width // 2
    count = HEADS // 2
    own_sum_ref[...] = jnp.zeros((tokens, half), f32)
    other_sum_ref[...] = jnp.zeros((tokens, half), f32)
    spans = got_ref.shape[0]

    def visit(h, carry):
        low, high = home(h, spans), home(count + h, spans)
        mine = jnp.where(core_ref[0] == 0, low, high)
        theirs = jnp.where(core_ref[0] == 0, high, low)
        window = pl.ds(pl.multiple_of(h * HEAD_DIM, HEAD_DIM), HEAD_DIM)
        upper = pl.ds(pl.multiple_of((count + h) * HEAD_DIM, HEAD_DIM), HEAD_DIM)
        for i, weight in enumerate((wq_ref, wk_ref, wv_ref)):
            at = slice(i * HEAD_DIM, (i + 1) * HEAD_DIM)
            rows = slice(i * half, (i + 1) * half)
            grads = jnp.concatenate([got_ref[low, :, at], got_ref[high, :, at]], axis=1)
            weights = jnp.concatenate([weight[:, window], weight[:, upper]], axis=1)
            own_sum_ref[...] += dot_nt(grads, weights)
            grads = jnp.concatenate([got_ref[mine, :, at], got_ref[theirs, :, at]], axis=1)
            weights = jnp.concatenate([near_ref[rows, window], far_ref[rows, window]], axis=1)
            other_sum_ref[...] += dot_nt(grads, weights)
        return carry

    lax.fori_loop(0, count, visit, 0)
    own_part, other_part = own_sum_ref[...], other_sum_ref[...]
    grad_normed = jnp.where(
        side_ref[0] == 0,
        jnp.concatenate([own_part, other_part], axis=1),
        jnp.concatenate([other_part, own_part], axis=1),
    )
    resid = x_ref[...].astype(f32)
    scale = rms_scale(resid)
    hat = grad_normed * gain_ref[...]
    mean = jnp.mean(hat * resid, axis=-1, keepdims=True)
    out_ref[...] = grad_second_ref[...] + scale * hat - resid * (scale * scale * scale) * mean


def inputs_back(side, core, got, w_query, w_key, w_value, near, far, x, gain, grad_second):
    smem = pl.BlockSpec(memory_space=pltpu.SMEM)
    memory = pl.BlockSpec(memory_space=pltpu.VMEM)
    return pl.pallas_call(
        inputs_back_kernel,
        in_specs=[smem] * 2 + [memory] * 9,
        out_specs=memory,
        out_shape=jax.ShapeDtypeStruct(x.shape, f32),
        scratch_shapes=[pltpu.VMEM((x.shape[0], x.shape[1] // 2), f32)] * 2,
        name="inputs_back",
    )(
        side.reshape(1),
        core.reshape(1),
        got,
        w_query,
        w_key,
        w_value,
        near,
        far,
        x,
        gain,
        grad_second,
    )


def place_heads_kernel(
    cut,
    side_ref,
    heads_ref,
    rest_ref,
    gain_rows_ref,
    gain_ref,
    q_ref,
    k_ref,
    v_ref,
    output_ref,
    norm_ref,
    norm2_ref,
):
    for h in range(HEADS):
        at = slice(h * HEAD_DIM, (h + 1) * HEAD_DIM)
        for i, out in enumerate((q_ref, k_ref, v_ref)):
            out[:, at] = heads_ref[h, :, i * HEAD_DIM : (i + 1) * HEAD_DIM].astype(f32)
    sums = rest_ref[0].astype(f32)
    for h in range(1, HEADS):
        sums += rest_ref[h].astype(f32)
    lane = lax.broadcasted_iota(jnp.int32, (8, HEAD_DIM), 1)
    pair = jnp.where((lane == cut) | (lane == cut + 1), 1.0, 0.0)
    row = lax.dot_general(
        pair, sums, (((1,), (1,)), ((), ())), precision=exact, preferred_element_type=f32
    )
    block = rest_ref.shape[1]
    for i in range(norm_ref.shape[1] // block):

        @pl.when(pl.program_id(0) == i)
        def _(at=slice(i * block, (i + 1) * block)):
            norm_ref[:, at] = row[0:1] / gain_ref[:, at]

    spans = rest_ref.shape[0]

    @pl.when(pl.program_id(0) == 0)
    def _():
        for i in range(spans // 2):
            low, high = ring_position(i, spans), ring_position(spans // 2 + i, spans)
            rows = gain_rows_ref[jnp.where(side_ref[0] == 0, low, high)].astype(f32)
            norm2_ref[:, i * cut : (i + 1) * cut] = (rows[0:1] + rows[1:2])[:, :cut]

    for c in range(spans):
        piece = rest_ref[ring_position(c, spans), :, :cut].astype(f32)
        output_ref[:, c * cut : (c + 1) * cut] = piece


def ring_position(index, spans):
    if spans != 16:
        return index
    chip, core = index // 2, index % 2
    level, column = chip // 2, chip % 2
    return (level + column * (7 - 2 * level)) * 2 + core


def place_heads(side, got, gain, width):
    spans, _, packed = got.shape
    half = width // 2
    cut = width // spans
    block = half // 8
    part = pl.BlockSpec((block, width), lambda r: (r, 0))
    line = pl.BlockSpec((1, half), lambda r: (0, 0))
    return pl.pallas_call(
        functools.partial(place_heads_kernel, cut),
        grid=(8,),
        in_specs=[
            pl.BlockSpec(memory_space=pltpu.SMEM),
            pl.BlockSpec((HEADS, block, 3 * HEAD_DIM), lambda r: (0, r, 0)),
            pl.BlockSpec((spans, block, HEAD_DIM), lambda r: (0, r, 3)),
            pl.BlockSpec((spans, 16, HEAD_DIM), lambda r: (0, half // 16, 3)),
            line,
        ],
        out_specs=[part] * 4 + [line] * 2,
        out_shape=[jax.ShapeDtypeStruct((half, width), f32)] * 4
        + [jax.ShapeDtypeStruct((1, half), f32)] * 2,
        name="place_heads",
    )(side.reshape(1), got, got, got, gain.reshape(1, half))


def place_shared_kernel(side_ref, got_ref, in_ref, out_ref, rows_ref):
    spans = got_ref.shape[0]
    units = got_ref.shape[1] // 4
    half = got_ref.shape[2]
    hidden = spans * units

    for part in range(2):
        for c in range(spans):
            spot = ring_position(c, spans)
            piece = got_ref[spot, part * units : (part + 1) * units, :]
            rows_ref[c * units : (c + 1) * units, :] = piece.astype(f32)

        def turn(i, carry):
            window = pl.ds(pl.multiple_of(i * HEAD_DIM, HEAD_DIM), HEAD_DIM)
            at = pl.ds(pl.multiple_of(part * hidden + i * HEAD_DIM, HEAD_DIM), HEAD_DIM)
            in_ref[:, at] = rows_ref[window, :].T
            return carry

        lax.fori_loop(0, hidden // HEAD_DIM, turn, 0)
    first = side_ref[0] * (spans // 2)
    for c in range(spans // 2):
        spot = ring_position(first + c, spans)
        for part in range(2):
            piece = got_ref[spot, (2 + part) * units : (3 + part) * units, :]
            out_ref[c * units : (c + 1) * units, part * half : (part + 1) * half] = piece.astype(f32)


def place_shared(got, side):
    spans, quad, half = got.shape
    hidden = spans * quad // 4
    memory = pl.BlockSpec(memory_space=pltpu.VMEM)
    return pl.pallas_call(
        place_shared_kernel,
        in_specs=[pl.BlockSpec(memory_space=pltpu.SMEM), memory],
        out_specs=[memory, memory],
        out_shape=[
            jax.ShapeDtypeStruct((half, 2 * hidden), f32),
            jax.ShapeDtypeStruct((hidden // 2, 2 * half), f32),
        ],
        scratch_shapes=[pltpu.VMEM((hidden, half), f32)],
        name="place_shared",
    )(side.reshape(1), got)


def after(value, *others):
    return lax.optimization_barrier((value, *others))[0]


def tied(*values):
    return lax.optimization_barrier(values)


def one_hot_rows(lanes, *targets):
    row = lax.broadcasted_iota(jnp.int32, (8, lanes), 0)
    lane = lax.broadcasted_iota(jnp.int32, (8, lanes), 1)
    rows = jnp.zeros((8, lanes), f32)
    for i, target in enumerate(targets):
        rows = jnp.where((row == i) & (lane == target), 1.0, rows)
    return rows.astype(bf16)


def slot_keys(shape, axis, capacity):
    index = lax.broadcasted_iota(jnp.int32, shape, axis)
    return (index % capacity + 1024 * (index // capacity)).astype(f32)


def run_keys(shape, axis, tokens):
    return (1024 * (lax.broadcasted_iota(jnp.int32, shape, axis) // tokens)).astype(f32)


def group_runs(capacity):
    return min(8, 224 // capacity)


def pick_slots_kernel(capacity, tokens, here_ref, g_ref, out_ref):
    many = g_ref.shape[0]
    width = out_ref.shape[1]
    extras = g_ref[:, width:]
    rows = one_hot_rows(extras.shape[1], here_ref[0])
    slots = dot_nt(rows, extras)[0:1] + run_keys((1, many), 1, tokens)
    takes = slot_keys((out_ref.shape[0], 1), 0, capacity) == slots
    select = jnp.where(takes, 1.0, 0.0).astype(bf16)
    out_ref[...] = dot(select, g_ref[:, :width]).astype(bf16)


def pick_slots(here, g_wide, width, capacity, tokens):
    length, wide = g_wide.shape
    runs = group_runs(capacity)
    steps = length // (runs * tokens)
    return pl.pallas_call(
        functools.partial(pick_slots_kernel, capacity, tokens),
        grid=(steps,),
        in_specs=[
            pl.BlockSpec(memory_space=pltpu.SMEM),
            pl.BlockSpec((runs * tokens, wide), lambda i: (i, 0)),
        ],
        out_specs=pl.BlockSpec((runs * capacity, width), lambda i: (i, 0)),
        out_shape=jax.ShapeDtypeStruct((steps * runs * capacity, width), bf16),
        name="pick_slots",
        cost_estimate=pl.CostEstimate(
            flops=2 * length * runs * capacity * width,
            bytes_accessed=3 * length * wide,
            transcendentals=0,
        ),
    )(here.reshape(1), g_wide)


def sigmoid(value):
    return 1.0 / (1.0 + jnp.exp(-value))


def experts_kernel(
    capacity,
    tokens,
    experts,
    here_ref,
    normed_ref,
    g_ref,
    grad_slots_ref,
    own_in_ref,
    first_in_ref,
    rest_in_ref,
    own_down_ref,
    other_down_ref,
    own_shared_in_ref,
    other_shared_in_ref,
    own_shared_out_ref,
    other_shared_out_ref,
    dispatched_ref,
    hidden_ref,
    grad_result_ref,
    grad_proj_ref,
    shared_hidden_ref,
    shared_grad_ref,
    parts_ref,
    gate_dot_ref,
    in_ref,
    down_ref,
    shared_in_ref,
    shared_out_ref,
    grad_dispatched_ref,
    scaled_ref,
):
    @pl.when(pl.program_id(0) == 0)
    def _():
        side = here_ref[1]
        rows = own_in_ref.shape[0]
        first = first_in_ref.shape[0]
        at = (1 - side) * rows
        in_ref[pl.ds(pl.multiple_of(side * rows, 64), rows), :] = own_in_ref[...]
        in_ref[pl.ds(pl.multiple_of(at, 16), first), :] = first_in_ref[...]
        in_ref[pl.ds(pl.multiple_of(at + first, 16), rows - first), :] = rest_in_ref[...]
        rows = own_down_ref.shape[0]
        down_ref[pl.ds(pl.multiple_of(side * rows, 64), rows), :] = own_down_ref[...]
        down_ref[pl.ds(pl.multiple_of((1 - side) * rows, 64), rows), :] = other_down_ref[...]
        rows = own_shared_in_ref.shape[0]
        units = own_shared_out_ref.shape[0]
        shared_in_ref[...] = jnp.zeros_like(shared_in_ref)
        shared_out_ref[...] = jnp.zeros_like(shared_out_ref)
        for place, ref in ((side, own_shared_in_ref), (1 - side, other_shared_in_ref)):
            window = pl.ds(pl.multiple_of(place * rows, 64), rows)
            shared_in_ref[window, :units] = ref[:, :units]
            shared_in_ref[window, HEAD_DIM : HEAD_DIM + units] = ref[:, units:]
        shared_out_ref[:units, :] = jnp.where(
            here_ref[2] == side, own_shared_out_ref[...], other_shared_out_ref[...]
        )

    many, slots = normed_ref.shape[0], dispatched_ref.shape[0]
    width = dispatched_ref.shape[1]
    here = here_ref[0]
    spare = normed_ref.shape[1] - width
    gate_rows = dot_nt(one_hot_rows(spare, here, experts + here), normed_ref[:, width:])
    gate_row = gate_rows[0:1] + gate_rows[1:2]
    slot_pick = one_hot_rows(spare, here)
    group = group_runs(capacity)
    chunk, picks = group * tokens, group * capacity
    takes = []
    for at in range(0, many, chunk):
        extras = g_ref[at : at + chunk, width:]
        slot_row = dot_nt(slot_pick, extras)[0:1] + run_keys((1, chunk), 1, tokens)
        hit = slot_keys((picks, 1), 0, capacity) == slot_row
        takes.append(hit)
        select = jnp.where(hit, 1.0, 0.0).astype(bf16)
        at_slots = slice(at // tokens * capacity, (at // tokens + group) * capacity)
        dispatched_ref[at_slots, :] = dot(select, normed_ref[at : at + chunk, :width]).astype(bf16)
    slot_gate = jnp.concatenate(
        [
            jnp.sum(
                jnp.where(hit, gate_row[:, i * chunk : (i + 1) * chunk], 0.0), axis=1, keepdims=True
            )
            for i, hit in enumerate(takes)
        ],
        axis=0,
    )
    dispatched = dispatched_ref[...]
    grad_slots = grad_slots_ref[...].astype(f32)
    grad_result = (grad_slots * slot_gate).astype(bf16)
    grad_result_ref[...] = grad_result

    projected = dot(dispatched, in_ref[...])
    gate, up = projected[:, :EXP_HID], projected[:, EXP_HID:]
    chance = sigmoid(gate)
    silu = gate * chance
    hidden = (silu * up).astype(bf16)
    hidden_ref[...] = hidden
    grad_hidden = dot_nt(grad_result, down_ref[...])
    grad_proj_ref[:, :EXP_HID] = (
        grad_hidden * up * chance * (1.0 + gate * (1.0 - chance))
    ).astype(bf16)
    grad_proj_ref[:, EXP_HID:] = (grad_hidden * silu).astype(bf16)
    result = dot(hidden, down_ref[...]).astype(bf16).astype(f32)
    slot_dot = jnp.sum(grad_slots * result, axis=1, keepdims=True)
    for i, hit in enumerate(takes):
        dots = slot_dot[i * picks : (i + 1) * picks]
        gate_dot = jnp.sum(jnp.where(hit, dots, 0.0), axis=0, keepdims=True)
        gate_dot_ref[:, i * chunk : (i + 1) * chunk] = jnp.broadcast_to(gate_dot, (8, chunk))
    scaled = (result * slot_gate).astype(bf16)
    grad_dispatched = dot_nt(grad_proj_ref[...], in_ref[...]).astype(bf16)

    grad_dispatched_ref[...] = grad_dispatched
    scaled_ref[...] = scaled
    lanes = shared_out_ref.shape[0]
    size = min(2 * HEAD_DIM, chunk)

    def visit(i, carry):
        at = pl.ds(pl.multiple_of(i * size, size), size)
        which = i * size // chunk
        filled = pl.ds(pl.multiple_of(which * picks, 16), picks)
        shared = dot(normed_ref[at, :width], shared_in_ref[...])
        shared_gate, shared_up = shared[:, :lanes], shared[:, lanes:]
        shared_chance = sigmoid(shared_gate)
        shared_silu = shared_gate * shared_chance
        shared_hidden = (shared_silu * shared_up).astype(bf16)
        shared_hidden_ref[at, :] = shared_hidden
        grad_shared = dot_nt(g_ref[at, :width], shared_out_ref[...])
        slope = shared_chance * (1.0 + shared_gate * (1.0 - shared_chance))
        shared_grad = jnp.concatenate(
            [(grad_shared * shared_up * slope).astype(bf16), (grad_shared * shared_silu).astype(bf16)],
            axis=1,
        )
        shared_grad_ref[at, :] = shared_grad
        slot_column = dot_nt(g_ref[at, width:], slot_pick)[:, 0:1]
        run = (i * size - which * chunk + lax.broadcasted_iota(jnp.int32, (size, 1), 0)) // tokens
        key = slot_column + (1024 * run).astype(f32)
        back = jnp.where(key == slot_keys((1, picks), 1, capacity), 1.0, 0.0).astype(bf16)
        parts_ref[at, :width] = (
            dot(back, grad_dispatched_ref[filled, :]) + dot_nt(shared_grad, shared_in_ref[...])
        ).astype(bf16)
        parts_ref[at, width:] = (
            dot(back, scaled_ref[filled, :]) + dot(shared_hidden, shared_out_ref[...])
        ).astype(bf16)
        return carry

    lax.fori_loop(0, many // size, visit, 0)


def run_experts(
    places, normed_wide, g_wide, grad_slots, weights, tokens, capacity
):
    length, wide = normed_wide.shape
    width = grad_slots.shape[1]
    experts = length // tokens
    runs = group_runs(capacity)
    steps = length // (runs * tokens)
    many, slots = runs * tokens, runs * capacity
    lanes = HEAD_DIM

    def block(rows, columns):
        return pl.BlockSpec((rows, columns), lambda i: (i, 0))

    def fixed(value):
        return pl.BlockSpec(value.shape, lambda i: (0, 0), pipeline_mode=pl.Buffered(1))

    def shape(rows, columns, kind=bf16):
        return jax.ShapeDtypeStruct((rows, columns), kind)

    return pl.pallas_call(
        functools.partial(experts_kernel, capacity, tokens, experts),
        grid=(steps,),
        in_specs=[
            pl.BlockSpec(memory_space=pltpu.SMEM),
            block(many, wide),
            block(many, wide),
            block(slots, width),
            *[fixed(weight) for weight in weights],
        ],
        out_specs=[
            block(slots, width),
            block(slots, EXP_HID),
            block(slots, width),
            block(slots, 2 * EXP_HID),
            block(many, lanes),
            block(many, 2 * lanes),
            block(many, 2 * width),
            pl.BlockSpec((8, many), lambda i: (0, i)),
        ],
        out_shape=[
            shape(steps * slots, width),
            shape(steps * slots, EXP_HID),
            shape(steps * slots, width),
            shape(steps * slots, 2 * EXP_HID),
            shape(length, lanes),
            shape(length, 2 * lanes),
            shape(length, 2 * width),
            shape(8, length, f32),
        ],
        scratch_shapes=[
            pltpu.VMEM((width, 2 * EXP_HID), bf16),
            pltpu.VMEM((EXP_HID, width), bf16),
            pltpu.VMEM((width, 2 * lanes), bf16),
            pltpu.VMEM((lanes, width), bf16),
            pltpu.VMEM((slots, width), bf16),
            pltpu.VMEM((slots, width), bf16),
        ],
        name="experts",
        cost_estimate=pl.CostEstimate(
            flops=20 * 10**9, bytes_accessed=40 * 10**6, transcendentals=2 * 10**6
        ),
    )(
        places,
        normed_wide,
        g_wide,
        grad_slots,
        *weights,
    )


def slot_grads_kernel(side_ref, left_ref, right_ref, own_ref, other_ref, turned_ref):
    @pl.when(pl.program_id(0) == 0)
    def _():
        turned_ref[...] = left_ref[...].T

    rows = own_ref.shape[0]
    size = rows // 5 if rows % 80 == 0 else rows // 4
    side = side_ref[0]

    def visit(i, carry):
        def part(place):
            at = pl.ds(pl.multiple_of(place * rows + i * size, 16), size)
            return dot(turned_ref[at, :], right_ref[...])

        at = pl.ds(pl.multiple_of(i * size, 16), size)
        own_ref[at, :] = part(side)
        other_ref[at, :] = part(1 - side).astype(bf16)
        return carry

    lax.fori_loop(0, rows // size, visit, 0)


def slot_grads(side, left, right):
    slots, tall = left.shape
    wide = right.shape[1]
    block = pl.BlockSpec((tall // 2, 2 * HEAD_DIM), lambda i: (0, i))
    return pl.pallas_call(
        slot_grads_kernel,
        grid=(wide // (2 * HEAD_DIM),),
        in_specs=[
            pl.BlockSpec(memory_space=pltpu.SMEM),
            pl.BlockSpec((slots, tall), lambda i: (0, 0), pipeline_mode=pl.Buffered(1)),
            pl.BlockSpec((slots, 2 * HEAD_DIM), lambda i: (0, i)),
        ],
        out_specs=[block, block],
        out_shape=[
            jax.ShapeDtypeStruct((tall // 2, wide), f32),
            jax.ShapeDtypeStruct((tall // 2, wide), bf16),
        ],
        scratch_shapes=[pltpu.VMEM((tall, slots), bf16)],
        name="slot_grads",
        cost_estimate=pl.CostEstimate(
            flops=2 * slots * tall * wide,
            bytes_accessed=2 * slots * (tall + wide) + 3 * tall * wide,
            transcendentals=0,
        ),
    )(side.reshape(1), left, right)


def turned_product_kernel(side_ref, left_ref, right_ref, out_ref, sum_ref):
    step = pl.program_id(0)

    @pl.when(step == 0)
    def _():
        sum_ref[...] = jnp.zeros_like(sum_ref)

    sum_ref[...] += dot_tn(right_ref[...], left_ref[...])

    @pl.when(step == pl.num_programs(0) - 1)
    def _():
        count = out_ref.shape[0] // HEAD_DIM
        near = count // 2

        def turn(i, carry):
            window = pl.ds(pl.multiple_of(i * HEAD_DIM, HEAD_DIM), HEAD_DIM)
            place = jnp.where(i // near == side_ref[0], 0, near) + i % near
            at = pl.ds(pl.multiple_of(place * HEAD_DIM, HEAD_DIM), HEAD_DIM)
            out_ref[at, :] = sum_ref[:, window].T
            return carry

        lax.fori_loop(0, count, turn, 0)


def turned_product(side, left, right, wide):
    length, lanes = right.shape
    tile = 2 * HEAD_DIM
    return pl.pallas_call(
        turned_product_kernel,
        grid=(length // tile,),
        in_specs=[
            pl.BlockSpec(memory_space=pltpu.SMEM),
            pl.BlockSpec((tile, wide), lambda i: (i, 0)),
            pl.BlockSpec((tile, lanes), lambda i: (i, 0)),
        ],
        out_specs=pl.BlockSpec((wide, lanes), lambda i: (0, 0)),
        out_shape=jax.ShapeDtypeStruct((wide, lanes), f32),
        scratch_shapes=[pltpu.VMEM((lanes, wide), f32)],
        name="turned_product",
        cost_estimate=pl.CostEstimate(
            flops=2 * length * lanes * wide,
            bytes_accessed=2 * length * wide,
            transcendentals=0,
        ),
    )(side.reshape(1), left, right)


def slot_table(span_picks, span_order, experts):
    tokens = span_picks.shape[0]
    order = span_order.reshape(tokens, TOP)
    onehot = span_picks[:, :, None] == jnp.arange(experts, dtype=jnp.int32)
    picked = jnp.any(onehot, axis=1)
    rank_key = jnp.sum(jnp.where(onehot, order[:, :, None], 0), axis=1)
    rank_key = jnp.where(picked, rank_key, tokens * TOP)
    before = rank_key[:, None, :] < rank_key[None, :, :]
    slots = jnp.sum(before.astype(jnp.int32), axis=0)
    return jnp.where(picked, slots, 2 * tokens)


def on_device(
    inputs,
    norm1_gain,
    w_query,
    w_key,
    w_value,
    w_output,
    norm2_gain,
    router,
    shared_gate_up_weight,
    shared_down_weight,
    expert_in,
    expert_out,
    picks,
    fill_order,
    grad_out,
):
    spans = lax.axis_size("ctx")
    here = lax.axis_index("ctx")
    side = lax.axis_index("fsdp")
    core = here % 2
    tokens, width = inputs.shape[1:]
    half = width // 2
    length = spans * tokens
    experts = spans * expert_in.shape[0]
    capacity = tokens * TOP // experts
    head = jnp.minimum(ring_position(here, spans), HEADS - 1)
    units = EXP_HID // spans
    ring = ring_of(spans)
    is_ring = spans == 16
    groups = [ring] if is_ring else None
    swap_core = [(i, i ^ 1) for i in range(spans)]

    def across(value):
        return lax.ppermute(value, "fsdp", [(0, 1), (1, 0)])

    def ordered(own, other, axis):
        return jnp.where(
            side == 0,
            jnp.concatenate([own, other], axis=axis),
            jnp.concatenate([other, own], axis=axis),
        )

    def everyone(value):
        return lax.all_gather(value, "ctx", axis=0, tiled=True, axis_index_groups=groups)

    def columns(value, start, count):
        return lax.dynamic_slice_in_dim(value, start, count, 1)

    def rows(value, start, count):
        return lax.dynamic_slice_in_dim(value, start, count, 0)

    def halves(value, axis=0):
        size = value.shape[axis] // 2
        mine = lax.dynamic_slice_in_dim(value, side * size, size, axis)
        theirs = lax.dynamic_slice_in_dim(value, (1 - side) * size, size, axis)
        return mine, theirs

    def reduced(value, axis=0):
        mine, theirs = halves(value, axis)
        return mine + across(theirs.astype(bf16)).astype(f32)

    def swapped(value):
        return lax.all_to_all(value, "ctx", split_axis=0, concat_axis=0, tiled=True)

    def row_major(value):
        return with_layout_constraint(value, Layout(tuple(range(value.ndim))))

    x = inputs[0]
    g = grad_out[0]
    x_all = everyone(x)
    spare = -(-2 * experts // HEAD_DIM) * HEAD_DIM
    own_table = slot_table(picks[0], fill_order[0, 0], experts)
    own_table = jnp.pad(
        own_table.astype(f32), ((0, 0), (0, spare - experts)), constant_values=2.0 * tokens
    )
    g_wide = jnp.concatenate([g, own_table.astype(bf16)], axis=1)
    head_own = jnp.concatenate(
        [columns(w, head * HEAD_DIM, HEAD_DIM) for w in (w_query, w_key, w_value)], axis=1
    )
    head_other = across(head_own)
    small = jnp.concatenate([router.T, norm1_gain[None], norm2_gain[None]], axis=0)
    small_other = across(small)
    output_near = across(columns(w_output, core * half, half))
    lanes = HEAD_DIM
    shared_in_own = jnp.concatenate(
        [columns(shared_gate_up_weight, at + here * units, units) for at in (0, EXP_HID)], axis=1
    )
    shared_rows = shared_down_weight.shape[0]
    shared_out_own = rows(shared_down_weight, here * units % shared_rows, units)
    cosine, sine = rotary_tables(jnp.asarray(ring, jnp.int32) * tokens, tokens, HEAD_DIM)
    small = ordered(small, small_other, 1)
    router_w = small[:experts]
    gain_one = small[experts : experts + 1].astype(f32)
    gain_two = small[experts + 1 :].astype(f32)
    quarter = half // 8
    chunks = [expert_in[0, :quarter], expert_in[0, quarter:]]
    head_other, *chunks = tied(head_other, *chunks)
    chunks = [across(chunk) for chunk in chunks]
    x_all, cosine, sine, head_other, gain_one, output_near, chunks[0] = tied(
        x_all, cosine, sine, head_other, gain_one, output_near, chunks[0]
    )
    output_far = lax.ppermute(output_near, "ctx", swap_core)
    g_wide_all = everyone(after(g_wide, x_all))
    g_all = g_wide_all[:, :width]
    table = g_wide_all[:, width : width + experts]

    normed1_all, query, key, value = project(
        side, x_all, gain_one, head_own, head_other, cosine, sine
    )
    context, lse, attended = attend(query, key, value, is_ring)
    attended, output_far = tied(attended, output_far)
    down_other = across(after(expert_out[0], attended))
    got = swapped(attended.reshape(spans, tokens, HEAD_DIM))
    got, chunks[1] = tied(got, chunks[1])
    spot = jnp.stack([side, core]).astype(jnp.int32)
    router_pad = jnp.pad(router_w, ((0, spare - experts), (0, 0)))
    second, normed2_wide, scale_two, own_gates, attended = mix(
        spot,
        got,
        w_output,
        output_near,
        output_far,
        x,
        gain_two,
        router_pad,
        own_table,
        experts,
    )
    normed2_wide, g_wide_all = tied(normed2_wide, g_wide_all)
    normed2_wide = everyone(normed2_wide)
    grad_slots = pick_slots(here, g_wide_all, width, capacity, tokens)
    shared_in_other = across(after(shared_in_own, grad_slots))
    shared_out_other = across(after(shared_out_own, grad_slots))
    normed2_wide, grad_slots, down_other, shared_in_other, shared_out_other = tied(
        normed2_wide, grad_slots, down_other, shared_in_other, shared_out_other
    )
    normed2_all = normed2_wide[:, :width]
    attended_all = everyone(after(attended, normed2_wide))
    dense = [
        columns(after(w, grad_slots), core * half, half) for w in (w_query, w_key, w_value)
    ]
    dense = jnp.concatenate(dense, axis=0)
    near = [across(dense[: dense.shape[0] // 2]), across(dense[dense.shape[0] // 2 :])]
    spots = [ring_position(i, spans) for i in range(spans)]
    (
        dispatched,
        expert_hidden,
        grad_result,
        grad_proj,
        shared_hidden,
        grad_sproj,
        parts,
        gate_dot,
    ) = run_experts(
        jnp.stack([here, side, here * units // shared_rows]).astype(jnp.int32),
        normed2_wide,
        g_wide_all,
        grad_slots,
        (
            expert_in[0],
            chunks[0],
            chunks[1],
            expert_out[0],
            down_other,
            shared_in_own,
            shared_in_other,
            shared_out_own,
            shared_out_other,
        ),
        tokens,
        capacity,
    )
    parts, near[0], attended_all = tied(parts, near[0], attended_all)
    sums = lax.psum_scatter(
        parts, "ctx", scatter_dimension=0, tiled=True, axis_index_groups=groups
    )
    gate_dot = gate_dot[0].reshape(spans, tokens)
    grad_shared_in = dot_tn(grad_sproj, normed2_all)
    grad_shared_in = jnp.concatenate(
        [grad_shared_in[:units], grad_shared_in[lanes : lanes + units]], axis=0
    )
    grad_shared_in = reduced(grad_shared_in, 1).astype(bf16)
    grad_shared_out = dot_tn(shared_hidden, g_all)[:units].astype(bf16)
    grad_shared_out = grad_shared_out.astype(f32) + across(grad_shared_out).astype(f32)
    grad_shared_out = grad_shared_out.astype(bf16)
    shared_grads = jnp.concatenate(
        [grad_shared_in, grad_shared_out[:, :half], grad_shared_out[:, half:]], axis=0
    )
    gate_dot = jnp.concatenate([gate_dot[i : i + 1] for i in spots], axis=0)
    gate_grads = swapped(after(gate_dot, parts)[:, None, :])[:, 0, :].T

    own_down, down_theirs = slot_grads(side, expert_hidden, grad_result)
    own_in, in_theirs = slot_grads(side, dispatched, grad_proj)
    down_theirs = across(after(down_theirs, parts))
    sums, in_theirs, shared_grads, gate_grads = tied(
        sums,
        in_theirs,
        row_major(shared_grads),
        gate_grads,
    )
    split = half * 3 // 8
    in_upper = across(in_theirs[:split])

    sent, cuts, grad_second, layer_out = mix_back(
        spot,
        sums,
        own_gates,
        jnp.pad(gate_grads, ((0, 0), (0, spare - experts))),
        router_pad,
        second,
        scale_two,
        gain_two,
        g,
        w_output,
        output_near,
        output_far,
        spans,
    )
    arrived = swapped(sent).reshape(length, HEAD_DIM)
    arrived, shared_grads, cuts, near[1], down_theirs = tied(
        arrived, shared_grads, cuts, near[1], down_theirs
    )
    cuts = lax.all_to_all(
        cuts, "ctx", split_axis=0, concat_axis=0, tiled=True, axis_index_groups=groups
    )
    extras = cuts[:, :tokens].reshape(length, HEAD_DIM)
    shared_grads = everyone(shared_grads[None])
    grad_heads, grad_heads_ring = attend_back(
        query, key, value, arrived, context, lse, cosine, sine, is_ring
    )
    grad_heads, grad_heads_ring, in_upper = tied(grad_heads, grad_heads_ring, in_upper)
    cut = width // spans
    gain_rows = cuts[:, tokens : tokens + 2, :cut].astype(f32)
    gain_rows = jnp.sum(gain_rows, axis=(0, 1))
    gain_rows = jnp.pad(gain_rows.reshape(1, cut), ((0, 15), (0, HEAD_DIM - cut)))
    grad_router = turned_product(side, normed2_wide, extras, width)[:, cut : cut + experts]
    grad_router = grad_router[:half] + across(grad_router[half:])
    products = turned_product(side, attended_all, extras, width)
    mine, theirs = products[:half], products[half:]
    gain_high = gain_rows.astype(bf16)
    gain_low = jnp.roll((gain_rows - gain_high.astype(f32)).astype(bf16), 1, axis=0)
    theirs = jnp.concatenate([theirs.astype(bf16), gain_high + gain_low], axis=0)
    grad_heads_ring, theirs = tied(grad_heads_ring, theirs)
    theirs = across(theirs).astype(f32)
    grad_output = mine + theirs[:half]
    gain_rows = gain_rows[:1] + theirs[half : half + 1] + theirs[half + 1 : half + 2]
    gain_high = gain_rows.astype(bf16)
    gain_low = (gain_rows - gain_high.astype(f32)).astype(bf16)
    gain_rows = jnp.pad(
        jnp.concatenate([gain_high, gain_low], axis=0), ((0, 14), (3 * HEAD_DIM, 0))
    )
    head_mine, head_theirs = halves(dot_tn(normed1_all, grad_heads_ring))
    head_theirs = head_theirs.astype(bf16)
    got = swapped(grad_heads.reshape(spans, tokens, 3 * HEAD_DIM))
    grad_head_w = (head_mine + across(head_theirs).astype(f32)).astype(bf16)
    part = jnp.sum(grad_head_w.astype(f32) * head_own.astype(f32), axis=1, keepdims=True)
    part_high = part.astype(bf16).astype(f32)
    lane = lax.broadcasted_iota(jnp.int32, (half, HEAD_DIM), 1)
    grad_output = jnp.where(lane < cut, grad_output, 0.0)
    grad_output = jnp.where(lane == cut, part_high, grad_output)
    grad_output = jnp.where(lane == cut + 1, part - part_high, grad_output)
    head_grads = jnp.concatenate([grad_head_w, grad_output.astype(bf16)], axis=1)
    head_grads = jnp.concatenate([head_grads, gain_rows], axis=0)
    in_lower = across(after(in_theirs[split:], head_grads))
    head_grads, got = tied(row_major(head_grads), got)
    head_grads = everyone(head_grads[None])
    near = jnp.concatenate(near, axis=0)
    far = lax.ppermute(near, "ctx", swap_core)

    grad_inputs = inputs_back(
        side, core, got, w_query, w_key, w_value, near, far, x, gain_one, grad_second
    )
    grad_inputs, in_lower = tied(grad_inputs, in_lower)
    grad_query, grad_key, grad_value, grad_output, grad_norm1, grad_norm2 = place_heads(
        side, head_grads, norm1_gain.astype(f32), width
    )
    grad_expert_in = jnp.concatenate(
        [
            own_in[:split] + in_upper.astype(f32),
            own_in[split:] + in_lower.astype(f32),
        ],
        axis=0,
    )
    grad_shared_in, grad_shared_out = place_shared(shared_grads, side)
    return (
        layer_out[None],
        grad_inputs[None],
        grad_norm1.reshape(half),
        grad_query,
        grad_key,
        grad_value,
        grad_output,
        grad_norm2.reshape(half),
        grad_router,
        grad_shared_in,
        grad_shared_out,
        grad_expert_in[None],
        (own_down + down_theirs.astype(f32))[None],
    )


def solution(mesh):
    placed = (
        P("fsdp", "ctx", None),
        P("fsdp"),
        P("fsdp", None),
        P("fsdp", None),
        P("fsdp", None),
        P("fsdp", None),
        P("fsdp"),
        P("fsdp", None),
        P("fsdp", None),
        P("fsdp", None),
        P("ctx", "fsdp", None),
        P("ctx", "fsdp", None),
        P("fsdp", "ctx", None),
        P("fsdp", "ctx", None),
        P("fsdp", "ctx", None),
    )
    return jax.shard_map(
        on_device,
        mesh=mesh,
        in_specs=placed,
        out_specs=(
            P("fsdp", "ctx", None),
            P("fsdp", "ctx", None),
            P("fsdp"),
            P("fsdp", None),
            P("fsdp", None),
            P("fsdp", None),
            P("fsdp", None),
            P("fsdp"),
            P("fsdp", None),
            P("fsdp", None),
            P("fsdp", None),
            P("ctx", "fsdp", None),
            P("ctx", "fsdp", None),
        ),
        check_vma=False,
    )
```

profile of v0, /device:TPU:0, one launch (start us, length us, event | category | flops | bytes accessed | tf_op | source)
XLA Modules:
  0.0 436.6 jit_solution(5099039176161462927)
XLA Ops:
  10.8 3.0 collective-permute-start
  14.9 2.1 collective-permute-start.1
  18.9 1.9 pad_maximum_fusion.2
  20.8 1.4 slice_bitcast_fusion
  23.0 20.3 %collective-permute-done.1 = bf16[18,640]{1,0:T(8,128)(2,1)S(1)} collective-permute-done((bf16[18,640]{1,0:T(8,128)(2,1)S(1)}, bf16[18,640]{1,0:T(8,128)(2,1)S(1)}, u32[]{:S(2)}, u32[]{:S(2)}) %collective-permute-start.1) | collective-permute-done | bytes 23072 | tf_op jit(solution)/shard_map/ppermute | solution.py:1119
  43.4 1.8 collective-permute-start.3
  45.8 5.7 %collective-permute-done.3.first_in_ref = bf16[80,1792]{1,0:T(8,128)(2,1)S(1)} collective-permute-done((bf16[80,1792]{1,0:T(8,128)(2,1)S(1)}, bf16[80,1792]{1,0:T(8,128)(2,1)S(1)}, u32[]{:S(2)}, u32[]{:S(2)}) %collective-permute-start.3) | collective-permute-done | bytes 286752 | tf_op jit(solution)/shard_map/ppermute | solution.py:1119
  52.3 1.5 collective-permute-start.5
  53.7 9.8 %project.1 = (bf16[2048,1280]{1,0:T(8,128)(2,1)}, bf16[2048,128]{1,0:T(8,128)(2,1)}, bf16[2048,128]{1,0:T(8,128)(2,1)}, bf16[2048,128]{1,0:T(8,128)(2,1)}) custom-call(s32[1]{0:T(128)} %bitcast.side_ref, bf16[2048,1280]{1,0:T(8,128)(2,1)} %bitcast.48, f32[1,1280]{1,0:T(1,128)} %get-tuple-element.111.gain_ref, bf16[640,384]{1,0:T(8,128)(2,1)} %copy-done.13, ...), custom_call_target="tpu_custom_call" | custom-call | flops 2013265920 | bytes 10485760 | tf_op jit(solution)/shard_map/project/pallas_call | solution.py:288
  63.5 9.5 %attend.1 = (f32[2048,128]{1,0:T(8,128)}, f32[1,2048]{1,0:T(1,128)}, bf16[2048,128]{1,0:T(8,128)(2,1)}) custom-call(bf16[2048,128]{1,0:T(8,128)(2,1)} %get-tuple-element.115.q_ref, bf16[2048,128]{1,0:T(8,128)(2,1)} %get-tuple-element.116.k_ref, bf16[2048,128]{1,0:T(8,128)(2,1)} %get-tuple-element.117.v_ref), custom_call_target="tpu_custom_call" | custom-call | flops 1073741824 | bytes 3145728 | tf_op jit(solution)/shard_map/attend/pallas_call | solution.py:133
  73.1 6.0 %all-to-all-start = ((bf16[16,128,128]{2,1,0:T(8,128)(2,1)}), bf16[16,128,128]{2,1,0:T(8,128)(2,1)S(1)}, u32[]{:S(2)}, u32[]{:S(2)}) async-start(bf16[16,128,128]{2,1,0:T(8,128)(2,1)} %bitcast.61), calls=%async_computation | async-start | bytes 1048576 | tf_op jit(solution)/shard_map/all_to_all | solution.py:1148
  81.2 15.5 %collective-permute-done.5.rest_in_ref = bf16[560,1792]{1,0:T(8,128)(2,1)} collective-permute-done((bf16[560,1792]{1,0:T(8,128)(2,1)}, bf16[560,1792]{1,0:T(8,128)(2,1)}, u32[]{:S(2)}, u32[]{:S(2)}) %collective-permute-start.5) | collective-permute-done | bytes 2007072 | tf_op jit(solution)/shard_map/ppermute | solution.py:1119
  96.6 3.1 all-to-all-done.got_ref
  100.6 5.4 %mix.1 = (f32[128,1280]{1,0:T(8,128)}, bf16[128,1408]{1,0:T(8,128)(2,1)}, f32[128,1]{1,0:T(8,128)}, f32[128,128]{1,0:T(8,128)}, bf16[128,1280]{1,0:T(8,128)(2,1)}) custom-call(s32[2]{0:T(128)} %pad_add_fusion.spot_ref, bf16[16,128,128]{2,1,0:T(8,128)(2,1)} %copy-done.11, bf16[640,1280]{1,0:T(8,128)(2,1)} %own_ref.3, bf16[640,640]{1,0:T(8,128)(2,1)} %copy-done.5, ...), custom_call_target="tpu_custom_call" | custom-call | tf_op jit(solution)/shard_map/mix/pallas_call | solution.py:391
  106.1 1.6 collective-permute-start.6
  107.6 1.2 constant_dynamic-slice_fusion.5
  109.1 5.8 %pick_slots.1.grad_slots_ref = bf16[896,1280]{1,0:T(8,128)(2,1)} custom-call(s32[1]{0:T(128)} %bitcast.2.here_ref, bf16[2048,1408]{1,0:T(8,128)(2,1)} %all-gather.10.cloned.1.call-done.g_ref), custom_call_target="tpu_custom_call" | custom-call | flops 1174405120 | bytes 8650752 | tf_op jit(solution)/shard_map/pick_slots/pallas_call | solution.py:739
  115.6 1.3 collective-permute-start.8
  116.9 17.7 %collective-permute-done.6.other_down_ref = bf16[448,1280]{1,0:T(8,128)(2,1)} collective-permute-done((bf16[448,1280]{1,0:T(8,128)(2,1)}, bf16[448,1280]{1,0:T(8,128)(2,1)}, u32[]{:S(2)}, u32[]{:S(2)}) %collective-permute-start.6) | collective-permute-done | bytes 1146912 | tf_op jit(solution)/shard_map/ppermute | solution.py:1119
  134.6 3.4 collective-permute-done.7.other_shared_in_ref
  138.0 1.9 collective-permute-done.8.other_shared_out_ref
  139.9 2.7 all-gather.12.cloned.1.call-done.normed_ref.left_ref
  143.6 1.2 constant_dynamic-slice_fusion.1
  144.9 1.2 constant_dynamic-slice_fusion.2
  146.1 1.6 pad_maximum_fusion
  147.7 1.4 collective-permute-start.9
  149.1 36.0 %experts.1 = (bf16[896,1280]{1,0:T(8,128)(2,1)}, bf16[896,896]{1,0:T(8,128)(2,1)}, bf16[896,1280]{1,0:T(8,128)(2,1)}, bf16[896,1792]{1,0:T(8,128)(2,1)}, bf16[20...) custom-call(s32[3]{0:T(128)} %pad_add_fusion.1.here_ref, ...), custom_call_target="tpu_custom_call" | custom-call | flops 20000000000 | bytes 40000000 | tf_op jit(solution)/shard_map/experts/pallas_call | solution.py:926
  187.4 4.2 fusion.2
  193.3 1.4 collective-permute-start.11
  196.2 1.2 concatenate.77
  197.4 14.4 %slot_grads.2 = (f32[640,1792]{1,0:T(8,128)}, bf16[640,1792]{1,0:T(8,128)(2,1)}) custom-call(s32[1]{0:T(128)} %bitcast.side_ref, bf16[896,1280]{1,0:T(8,128)(2,1)} %get-tuple-element.144.left_ref, bf16[896,1792]{1,0:T(8,128)(2,1)} %get-tuple-element.145.right_ref), custom_call_target="tpu_custom_call" | custom-call | flops 4110417920 | bytes 12386304 | tf_op jit(solution)/shard_map/slot_grads/pallas_call | solution.py:1003
  211.8 9.2 %slot_grads.3 = (f32[448,1280]{1,0:T(8,128)}, bf16[448,1280]{1,0:T(8,128)(2,1)}) custom-call(s32[1]{0:T(128)} %bitcast.side_ref, bf16[896,896]{1,0:T(8,128)(2,1)} %get-tuple-element.162.left_ref, bf16[896,1280]{1,0:T(8,128)(2,1)} %get-tuple-element.163.right_ref), custom_call_target="tpu_custom_call" | custom-call | flops 2055208960 | bytes 7340032 | tf_op jit(solution)/shard_map/slot_grads/pallas_call | solution.py:1003
  221.1 1.4 collective-permute-start.13
  222.6 4.0 all-to-all-start.1
  227.3 5.7 %all-to-all-done.1 = f32[16,1,128]{2,1,0:T(1,128)S(1)} async-done(((f32[16,1,128]{2,1,0:T(1,128)}), f32[16,1,128]{2,1,0:T(1,128)S(1)}, u32[]{:S(2)}, u32[]{:S(2)}) %all-to-all-start.1) | async-done | bytes 8224 | tf_op jit(solution)/shard_map/all_to_all | solution.py:1148
  233.1 13.7 %reduce-scatter.2.cloned.1.call-done.sums_ref = bf16[128,2560]{1,0:T(8,128)(2,1)} async-done(((bf16[2048,2560]{1,0:T(8,128)(2,1)}), bf16[128,2560]{1,0:T(8,128)(2,1)}) %reduce-scatter.2.cloned.1.call-update) | async-done | bytes 655376 | tf_op jit(solution)/shard_map/reduce_scatter | solution.py:1259
  247.4 6.5 %mix_back.1 = (bf16[16,128,128]{2,1,0:T(8,128)(2,1)}, bf16[16,144,128]{2,1,0:T(8,128)(2,1)}, f32[128,1280]{1,0:T(8,128)}, bf16[128,1280]{1,0:T(8,128)(2,1)}) custom-call(s32[2]{0:T(128)} %pad_add_fusion.spot_ref, bf16[128,2560]{1,0:T(8,128)(2,1)} %reduce-scatter.2.cloned.1.call-done.sums_ref, f32[128,128]{1,0:T(8,128)} %get-tuple-element.152.gates_ref, ...), custom_call_target="tpu_custom_call" | custom-call | tf_op jit(solution)/shard_map/mix_back/pallas_call | solution.py:478
  254.0 5.1 %all-to-all-start.2 = ((bf16[16,128,128]{2,1,0:T(8,128)(2,1)}), bf16[16,128,128]{2,1,0:T(8,128)(2,1)S(1)}, u32[]{:S(2)}, u32[]{:S(2)}) async-start(bf16[16,128,128]{2,1,0:T(8,128)(2,1)} %get-tuple-element.158), calls=%async_computation.3 | async-start | bytes 1048576 | tf_op jit(solution)/shard_map/all_to_all | solution.py:1148
  259.2 14.4 %all-to-all-done.2 = bf16[16,128,128]{2,1,0:T(8,128)(2,1)S(1)} async-done(((bf16[16,128,128]{2,1,0:T(8,128)(2,1)}), bf16[16,128,128]{2,1,0:T(8,128)(2,1)S(1)}, u32[]{:S(2)}, u32[]{:S(2)}) %all-to-all-start.2) | async-done | bytes 524320 | tf_op jit(solution)/shard_map/all_to_all | solution.py:1148
  273.6 4.1 all-to-all-start.3
  277.8 2.1 slice.226
  279.9 1.5 collective-permute-start.14
  281.4 17.6 %attend_back.1 = (bf16[2048,384]{1,0:T(8,128)(2,1)}, bf16[2048,384]{1,0:T(8,128)(2,1)}) custom-call(bf16[2048,128]{1,0:T(8,128)(2,1)} %get-tuple-element.115.q_ref, bf16[2048,128]{1,0:T(8,128)(2,1)} %get-tuple-element.116.k_ref, bf16[2048,128]{1,0:T(8,128)(2,1)} %get-tuple-element.117.v_ref, bf16[2048,128]{1,0:T(8,128)(2,1)} %bitcast.60, ...), custom_call_target="tpu_custom_call" | custom-call | flops 2684354560 | bytes 5242880 | tf_op jit(solution)/shard_map/attend_back/pallas_call | solution.py:242
  299.0 2.6 collective-permute-done.14
  302.5 5.7 %all-to-all-start.4 = ((bf16[16,128,384]{2,1,0:T(8,128)(2,1)}), bf16[16,128,384]{2,1,0:T(8,128)(2,1)S(1)}, u32[]{:S(2)}, u32[]{:S(2)}) async-start(bf16[16,128,384]{2,1,0:T(8,128)(2,1)} %bitcast.56), calls=%async_computation.5 | async-start | bytes 3145728 | tf_op jit(solution)/shard_map/all_to_all | solution.py:1148
  309.2 7.8 %turned_product.2 = f32[1280,128]{1,0:T(8,128)} custom-call(s32[1]{0:T(128)} %bitcast.side_ref, bf16[2048,1280]{1,0:T(8,128)(2,1)} %all-gather.14.cloned.1.call-done.left_ref, bf16[2048,128]{1,0:T(8,128)(2,1)} %bitcast.49), custom_call_target="tpu_custom_call" | custom-call | flops 671088640 | bytes 5242880 | tf_op jit(solution)/shard_map/turned_product/pallas_call | solution.py:1053
  318.1 1.5 collective-permute-start.16
  319.6 5.4 %fusion.32 = f32[1280,384]{1,0:T(8,128)S(1)} fusion(bf16[2048,1280]{1,0:T(8,128)(2,1)} %get-tuple-element.157, bf16[2048,384]{1,0:T(8,128)(2,1)} %get-tuple-element.175), kind=kOutput, calls=%fused_computation.103 | convolution fusion | flops 2013265920 | bytes 8781824 | tf_op jit(solution)/shard_map/dot_general | solution.py:36
  325.8 12.6 %collective-permute-done.15 = bf16[640,384]{1,0:T(8,128)(2,1)S(1)} collective-permute-done((bf16[640,384]{1,0:T(8,128)(2,1)S(1)}, bf16[640,384]{1,0:T(8,128)(2,1)S(1)}, u32[]{:S(2)}, u32[]{:S(2)}) %collective-permute-start.15) | collective-permute-done | bytes 491552 | tf_op jit(solution)/shard_map/ppermute | solution.py:1119
  339.9 4.4 all-to-all-done.4.got_ref
  344.3 3.0 constant_dynamic-update-slice_fusion.1
  347.3 2.6 constant_dynamic-update-slice_fusion.near_ref
  351.8 1.5 collective-permute-start.18
  353.3 1.7 add_bitcast_fusion
  355.0 7.8 %turned_product.3 = f32[1280,128]{1,0:T(8,128)} custom-call(s32[1]{0:T(128)} %bitcast.side_ref, bf16[2048,1408]{1,0:T(8,128)(2,1)} %all-gather.12.cloned.1.call-done.normed_ref.left_ref, bf16[2048,128]{1,0:T(8,128)(2,1)} %bitcast.50), custom_call_target="tpu_custom_call" | custom-call | flops 671088640 | bytes 5242880 | tf_op jit(solution)/shard_map/turned_product/pallas_call | solution.py:1053
  364.7 1.9 convert_add_fusion.1
  366.6 26.1 %collective-permute-done.19 = f32[640,16]{1,0:T(8,128)S(1)} collective-permute-done((f32[640,16]{1,0:T(8,128)S(1)}, f32[640,16]{1,0:T(8,128)S(1)}, u32[]{:S(2)}, u32[]{:S(2)}) %collective-permute-start.19) | collective-permute-done | bytes 40992 | tf_op jit(solution)/shard_map/ppermute | solution.py:1119
  393.6 9.5 %inputs_back.1 = f32[128,1280]{1,0:T(8,128)} custom-call(s32[1]{0:T(128)} %bitcast.side_ref, s32[1]{0:T(128)} %bitcast.1.core_ref, bf16[16,128,384]{2,1,0:T(8,128)(2,1)} %copy-done.3, bf16[640,1280]{1,0:T(8,128)(2,1)} %wq_ref.1, bf16[640,1280]{1,0:T(8,128)(2,1)} %wk_ref.1, bf16[640,1280]{1,0:T(8,128)(2,1)} %wv_ref.1, ...), custom_call_target="tpu_custom_call" | custom-call | tf_op jit(solution)/shard_map/inputs_back/pallas_call | solution.py:549
  403.1 2.5 convert_add_fusion
  405.6 2.4 maximum_bitcast_fusion
  408.1 8.0 %place_shared.1 = (f32[640,1792]{1,0:T(8,128)}, f32[448,1280]{1,0:T(8,128)}) custom-call(s32[1]{0:T(128)} %bitcast.side_ref, bf16[16,224,640]{2,1,0:T(8,128)(2,1)} %bitcast.51), custom_call_target="tpu_custom_call" | custom-call | tf_op jit(solution)/shard_map/place_shared/pallas_call | solution.py:681
  416.1 11.2 %place_heads.1 = (f32[640,1280]{1,0:T(8,128)}, f32[640,1280]{1,0:T(8,128)}, f32[640,1280]{1,0:T(8,128)}, f32[640,1280]{1,0:T(8,128)}, f32[1,640]{1,0:T(1,128)}, /*index=5*/f32[1,640]{1,0:T(1,128)}) custom-call(s32[1]{0:T(128)} %bitcast.side_ref, bf16[16,656,512]{2,1,0:T(8,128)(2,1)} %bitcast.42, bf16[16,656,512]{2,1,0:T(8,128)(2,1)} %bitcast.43, ...), custom_call_target="tpu_custom_call" | custom-call | tf_op jit(solution)/shard_map/place_heads/pallas_call | solution.py:633
  427.2 1.3 reduce.1
  428.5 1.3 reduce.2
  (200 shorter events, 30.0 us)
Async XLA Ops:
  7.2 101.8 %copy-start = (bf16[448,1280]{1,0:T(8,128)(2,1)S(1)}, bf16[448,1280]{1,0:T(8,128)(2,1)}, u32[]{:S(2)}) copy-start(bf16[448,1280]{1,0:T(8,128)(2,1)} %param.25) | copy-start | bytes 3440644
  7.2 9.8 %copy-start.33 = (f32[16]{0:T(128)S(1)}, f32[16]{0:T(128)}, u32[]{:S(2)}) copy-start(f32[16]{0:T(128)} %constant.119) | copy-start | bytes 196
  7.2 6.7 %copy-start.2 = (bf16[640,1280]{1,0:T(8,128)(2,1)S(1)}, bf16[640,1280]{1,0:T(8,128)(2,1)}, u32[]{:S(2)}) copy-start(bf16[640,1280]{1,0:T(8,128)(2,1)} %own_ref.3) | copy-start | bytes 4915204
  7.2 7.7 %copy-start.29 = (bf16[640]{0:T(1024)(128)(2,1)S(1)}, bf16[640]{0:T(1024)(128)(2,1)}, u32[]{:S(2)}) copy-start(bf16[640]{0:T(1024)(128)(2,1)} %param.17) | copy-start | bytes 3844
  7.2 7.6 %copy-start.32 = (bf16[640]{0:T(1024)(128)(2,1)S(1)}, bf16[640]{0:T(1024)(128)(2,1)}, u32[]{:S(2)}) copy-start(bf16[640]{0:T(1024)(128)(2,1)} %param.22) | copy-start | bytes 3844
  7.2 7.7 %copy-start.28 = (bf16[640,16]{0,1:T(8,128)(2,1)S(1)}, bf16[640,16]{0,1:T(8,128)(2,1)}, u32[]{:S(2)}) copy-start(bf16[640,16]{0,1:T(8,128)(2,1)} %param.23) | copy-start | bytes 61444
  7.3 10.2 %copy-start.30 = (s32[1,128,7]{1,0,2:T(1,128)S(1)}, s32[1,128,7]{1,0,2:T(1,128)}, u32[]{:S(2)}) copy-start(s32[1,128,7]{1,0,2:T(1,128)} %param.28) | copy-start | bytes 10756
  7.3 10.2 %copy-start.31 = (s32[1,1,896]{2,1,0:T(1,128)S(1)}, s32[1,1,896]{2,1,0:T(1,128)}, u32[]{:S(2)}) copy-start(s32[1,1,896]{2,1,0:T(1,128)} %param.29) | copy-start | bytes 10756
  7.3 44.3 %all-gather.16.cloned.1.call-start = ((), (), s32[]{:S(2)}) async-start(), calls=%async_computation.10 | async-start | bytes 5570560 | tf_op jit(solution)/shard_map/all_gather | solution.py:1129
  8.0 98.0 %all-gather.10.cloned.1.call-start = ((), (), s32[]{:S(2)}) async-start(), calls=%async_computation.6 | async-start | bytes 6127616 | tf_op jit(solution)/shard_map/all_gather | solution.py:1129
  10.8 7.9 %copy-start.13 = (bf16[640,384]{1,0:T(8,128)(2,1)}, bf16[640,384]{1,0:T(8,128)(2,1)S(1)}, u32[]{:S(2)}) copy-start(bf16[640,384]{1,0:T(8,128)(2,1)S(1)} %pad_maximum_fusion.5.own_ref) | copy-start | bytes 1474564
  10.8 32.5 %collective-permute-start = (bf16[640,384]{1,0:T(8,128)(2,1)S(1)}, bf16[640,384]{1,0:T(8,128)(2,1)}, u32[]{:S(2)}, u32[]{:S(2)}) collective-permute-start(bf16[640,384]{1,0:T(8,128)(2,1)S(1)} %pad_maximum_fusion.5.own_ref), channel_id=1, source_target_pairs={{0,1},{1,0},{2,3},{3,2},{4,5},{5,4},{6,7},{7,6},{8,9},{9,8},{10,11... | collective-permute-start | bytes 1474568 | tf_op jit(solution)/shard_map/ppermute | solution.py:1119
  14.8 36.7 %collective-permute-start.2 = (bf16[640,640]{1,0:T(8,128)(2,1)}, bf16[640,640]{1,0:T(8,128)(2,1)S(1)}, u32[]{:S(2)}, u32[]{:S(2)}) collective-permute-start(bf16[640,640]{1,0:T(8,128)(2,1)} %constant_dynamic-slice_fusion.6), channel_id=1, source_target_pairs={{0,1},{1,0},{2,3},{3,2},{4,5},{5,4},{6,7},{7,6},{8,9},{9,8},{10,11... | collective-permute-start | bytes 2457608 | tf_op jit(solution)/shard_map/ppermute | solution.py:1119
  14.9 28.4 %collective-permute-start.1 = (bf16[18,640]{1,0:T(8,128)(2,1)S(1)}, bf16[18,640]{1,0:T(8,128)(2,1)S(1)}, u32[]{:S(2)}, u32[]{:S(2)}) collective-permute-start(bf16[18,640]{1,0:T(8,128)(2,1)S(1)} %pad_maximum_fusion.11), channel_id=1, source_target_pairs={{0,1},{1,0},{2,3},{3,2},{4,5},{5,4},{6,7},{7,6},{8,9},{9,8},{10,11... | collective-permute-start | bytes 69128 | tf_op jit(solution)/shard_map/ppermute | solution.py:1119
  43.3 8.3 %copy-start.25 = (bf16[18,1280]{1,0:T(8,128)(2,1)}, bf16[18,1280]{1,0:T(8,128)(2,1)S(1)}, u32[]{:S(2)}) copy-start(bf16[18,1280]{1,0:T(8,128)(2,1)S(1)} %maximum_select_fusion) | copy-start | bytes 138244
  43.4 8.2 %collective-permute-start.3 = (bf16[80,1792]{1,0:T(8,128)(2,1)S(1)}, bf16[80,1792]{1,0:T(8,128)(2,1)S(1)}, u32[]{:S(2)}, u32[]{:S(2)}) collective-permute-start(bf16[80,1792]{1,0:T(8,128)(2,1)S(1)} %slice_bitcast_fusion.1), channel_id=1, source_target_pairs={{0,1},{1,0},{2,3},{3,2},{4,5},{5,4},{6,7},{7,6},{8,9},{9,8},{10,11... | collective-permute-start | bytes 860168 | tf_op jit(solution)/shard_map/ppermute | solution.py:1119
  51.6 12.0 %copy-start.5 = (bf16[640,640]{1,0:T(8,128)(2,1)}, bf16[640,640]{1,0:T(8,128)(2,1)S(1)}, u32[]{:S(2)}) copy-start(bf16[640,640]{1,0:T(8,128)(2,1)S(1)} %collective-permute-done.2.near_ref) | copy-start | bytes 2457604
  52.3 44.4 %collective-permute-start.5 = (bf16[560,1792]{1,0:T(8,128)(2,1)}, bf16[560,1792]{1,0:T(8,128)(2,1)}, u32[]{:S(2)}, u32[]{:S(2)}) collective-permute-start(bf16[560,1792]{1,0:T(8,128)(2,1)} %slice_bitcast_fusion), channel_id=1, source_target_pairs={{0,1},{1,0},{2,3},{3,2},{4,5},{5,4},{6,7},{7,6},{8,9},{9,8},{10,11... | collective-permute-start | bytes 6021128 | tf_op jit(solution)/shard_map/ppermute | solution.py:1119
  53.7 19.3 %collective-permute-start.4 = (bf16[640,640]{1,0:T(8,128)(2,1)S(1)}, bf16[640,640]{1,0:T(8,128)(2,1)S(1)}, u32[]{:S(2)}, u32[]{:S(2)}) collective-permute-start(bf16[640,640]{1,0:T(8,128)(2,1)S(1)} %collective-permute-done.2.near_ref), channel_id=1, source_target_pairs={{0,2},{2,0},{4,6},{6,4},{8,10},{10,8},{12,14},{14,12},{16,18},{18,... | collective-permute-start | bytes 2457608 | tf_op jit(solution)/shard_map/ppermute | solution.py:1187
  63.5 16.9 %slice-start.2 = ((bf16[18,1280]{1,0:T(8,128)(2,1)}), bf16[16,1280]{1,0:T(8,128)(2,1)S(1)}, s32[]{:S(2)}) async-start(bf16[18,1280]{1,0:T(8,128)(2,1)} %copy-done.25), calls=%async_computation.15 | async-start | bytes 81920 | tf_op jit(solution)/shard_map/slice | solution.py:1177
  73.0 26.7 %copy-start.6 = (bf16[640,640]{1,0:T(8,128)(2,1)}, bf16[640,640]{1,0:T(8,128)(2,1)S(1)}, u32[]{:S(2)}) copy-start(bf16[640,640]{1,0:T(8,128)(2,1)S(1)} %collective-permute-done.4.far_ref) | copy-start | bytes 2457604
  73.1 26.7 %all-to-all-start = ((bf16[16,128,128]{2,1,0:T(8,128)(2,1)}), bf16[16,128,128]{2,1,0:T(8,128)(2,1)S(1)}, u32[]{:S(2)}, u32[]{:S(2)}) async-start(bf16[16,128,128]{2,1,0:T(8,128)(2,1)} %bitcast.61), calls=%async_computation | async-start | bytes 1048576 | tf_op jit(solution)/shard_map/all_to_all | solution.py:1148
  79.1 63.5 %all-gather.12.cloned.1.call-start = ((), (), s32[]{:S(2)}) async-start(), calls=%async_computation.7 | async-start | bytes 6127616 | tf_op jit(solution)/shard_map/all_gather | solution.py:1129
  106.0 79.1 %all-gather.14.cloned.1.call-start = ((), (), s32[]{:S(2)}) async-start(), calls=%async_computation.8 | async-start | bytes 5570560 | tf_op jit(solution)/shard_map/all_gather | solution.py:1129
  106.1 28.5 %collective-permute-start.6 = (bf16[448,1280]{1,0:T(8,128)(2,1)}, bf16[448,1280]{1,0:T(8,128)(2,1)}, u32[]{:S(2)}, u32[]{:S(2)}) collective-permute-start(bf16[448,1280]{1,0:T(8,128)(2,1)} %bitcast.71), channel_id=1, source_target_pairs={{0,1},{1,0},{2,3},{3,2},{4,5},{5,4},{6,7},{7,6},{8,9},{9,8},{10,11... | collective-permute-start | bytes 3440648 | tf_op jit(solution)/shard_map/ppermute | solution.py:1119
  109.0 5.9 %copy-start.26 = (bf16[640,112]{1,0:T(8,128)(2,1)}, bf16[640,112]{1,0:T(8,128)(2,1)S(1)}, u32[]{:S(2)}) copy-start(bf16[640,112]{1,0:T(8,128)(2,1)S(1)} %pad_maximum_fusion.9.own_shared_in_ref) | copy-start | bytes 430084
  109.1 6.6 %copy-start.27 = (bf16[56,1280]{1,0:T(8,128)(2,1)}, bf16[56,1280]{1,0:T(8,128)(2,1)S(1)}, u32[]{:S(2)}) copy-start(bf16[56,1280]{1,0:T(8,128)(2,1)S(1)} %constant_dynamic-slice_fusion.3.own_shared_out_ref) | copy-start | bytes 430084
  109.1 34.5 %copy-start.4 = (bf16[640,1280]{1,0:T(8,128)(2,1)S(1)}, bf16[640,1280]{1,0:T(8,128)(2,1)}, u32[]{:S(2)}) copy-start(bf16[640,1280]{1,0:T(8,128)(2,1)} %wv_ref.1) | copy-start | bytes 4915204
  114.9 23.1 %collective-permute-start.7 = (bf16[640,112]{1,0:T(8,128)(2,1)S(1)}, bf16[640,112]{1,0:T(8,128)(2,1)S(1)}, u32[]{:S(2)}, u32[]{:S(2)}) collective-permute-start(bf16[640,112]{1,0:T(8,128)(2,1)S(1)} %pad_maximum_fusion.9.own_shared_in_ref), channel_id=1, source_target_pairs={{0,1},{1,0},{2,3},{3,2},{4,5},{5,4},{6,7},{7,6},{8,9},{9,8},{10,11... | collective-permute-start | bytes 430088 | tf_op jit(solution)/shard_map/ppermute | solution.py:1119
  115.6 24.3 %collective-permute-start.8 = (bf16[56,1280]{1,0:T(8,128)(2,1)S(1)}, bf16[56,1280]{1,0:T(8,128)(2,1)S(1)}, u32[]{:S(2)}, u32[]{:S(2)}) collective-permute-start(bf16[56,1280]{1,0:T(8,128)(2,1)S(1)} %constant_dynamic-slice_fusion.3.own_shared_out_ref), channel_id=1, source_target_pairs={{0,1},{1,0},{2,3},{3,2},{4,5},{5,4},{6,7},{7,6},{8,9},{9,8},{10,11... | collective-permute-start | bytes 430088 | tf_op jit(solution)/shard_map/ppermute | solution.py:1119
  138.0 8.1 %copy-start.35 = (bf16[640,112]{1,0:T(8,128)(2,1)}, bf16[640,112]{1,0:T(8,128)(2,1)S(1)}, u32[]{:S(2)}) copy-start(bf16[640,112]{1,0:T(8,128)(2,1)S(1)} %collective-permute-done.7.other_shared_in_ref) | copy-start | bytes 430084
  139.9 6.2 %copy-start.36 = (bf16[56,1280]{1,0:T(8,128)(2,1)}, bf16[56,1280]{1,0:T(8,128)(2,1)S(1)}, u32[]{:S(2)}) copy-start(bf16[56,1280]{1,0:T(8,128)(2,1)S(1)} %collective-permute-done.8.other_shared_out_ref) | copy-start | bytes 430084
  142.6 104.2 %reduce-scatter.2.cloned.1.call-start = ((), (), s32[]{:S(2)}) async-start(), calls=%async_computation.9 | async-start | bytes 11141120 | tf_op jit(solution)/shard_map/reduce_scatter | solution.py:1259
  147.7 37.3 %collective-permute-start.9 = (bf16[960,640]{1,0:T(8,128)(2,1)}, bf16[960,640]{1,0:T(8,128)(2,1)S(1)}, u32[]{:S(2)}, u32[]{:S(2)}) collective-permute-start(bf16[960,640]{1,0:T(8,128)(2,1)} %get-tuple-element.260), channel_id=1, source_target_pairs={{0,1},{1,0},{2,3},{3,2},{4,5},{5,4},{6,7},{7,6},{8,9},{9,8},{10,11... | collective-permute-start | bytes 3686408 | tf_op jit(solution)/shard_map/ppermute | solution.py:1119
  186.1 6.2 %slice-start = ((s8[5767168]{0:T(1024)(128)(4,1)}), s8[1572864]{0:T(1024)(128)(4,1)S(1)}, s32[]{:S(2)}) async-start(s8[5767168]{0:T(1024)(128)(4,1)} %bitcast.46), calls=%async_computation.13 | async-start | bytes 3145728
  187.4 5.0 %slice-start.1 = ((s8[5767168]{0:T(1024)(128)(4,1)}), s8[4194304]{0:T(1024)(128)(4,1)S(1)}, s32[]{:S(2)}) async-start(s8[5767168]{0:T(1024)(128)(4,1)} %bitcast.46), calls=%async_computation.14 | async-start | bytes 8388608
  187.4 5.0 %copy-start.37 = (bf16[2048,128]{1,0:T(8,128)(2,1)S(1)}, bf16[2048,128]{1,0:T(8,128)(2,1)}, u32[]{:S(2)}) copy-start(bf16[2048,128]{1,0:T(8,128)(2,1)} %get-tuple-element.148) | copy-start | bytes 1572868
  191.6 29.4 %collective-permute-start.10 = (bf16[112,640]{1,0:T(8,128)(2,1)S(1)}, bf16[112,640]{1,0:T(8,128)(2,1)S(1)}, u32[]{:S(2)}, u32[]{:S(2)}) collective-permute-start(bf16[112,640]{1,0:T(8,128)(2,1)S(1)} %fusion.9), channel_id=1, source_target_pairs={{0,1},{1,0},{2,3},{3,2},{4,5},{5,4},{6,7},{7,6},{8,9},{9,8},{10,11... | collective-permute-start | bytes 430088 | tf_op jit(solution)/shard_map/ppermute | solution.py:1119
  193.3 27.7 %collective-permute-start.11 = (bf16[56,1280]{1,0:T(8,128)(2,1)S(1)}, bf16[56,1280]{1,0:T(8,128)(2,1)S(1)}, u32[]{:S(2)}, u32[]{:S(2)}) collective-permute-start(bf16[56,1280]{1,0:T(8,128)(2,1)S(1)} %slice.294), channel_id=1, source_target_pairs={{0,1},{1,0},{2,3},{3,2},{4,5},{5,4},{6,7},{7,6},{8,9},{9,8},{10,11... | collective-permute-start | bytes 430088 | tf_op jit(solution)/shard_map/ppermute | solution.py:1119
  194.7 64.4 %collective-permute-start.12 = (bf16[960,640]{1,0:T(8,128)(2,1)}, bf16[960,640]{1,0:T(8,128)(2,1)S(1)}, u32[]{:S(2)}, u32[]{:S(2)}) collective-permute-start(bf16[960,640]{1,0:T(8,128)(2,1)} %get-tuple-element.259), channel_id=1, source_target_pairs={{0,1},{1,0},{2,3},{3,2},{4,5},{5,4},{6,7},{7,6},{8,9},{9,8},{10,11... | collective-permute-start | bytes 3686408 | tf_op jit(solution)/shard_map/ppermute | solution.py:1119
  221.1 38.1 %collective-permute-start.13 = (bf16[448,1280]{1,0:T(8,128)(2,1)}, bf16[448,1280]{1,0:T(8,128)(2,1)S(1)}, u32[]{:S(2)}, u32[]{:S(2)}) collective-permute-start(bf16[448,1280]{1,0:T(8,128)(2,1)} %get-tuple-element.165), channel_id=1, source_target_pairs={{0,1},{1,0},{2,3},{3,2},{4,5},{5,4},{6,7},{7,6},{8,9},{9,8},{10,11... | collective-permute-start | bytes 3440648 | tf_op jit(solution)/shard_map/ppermute | solution.py:1119
  222.6 10.4 %all-to-all-start.1 = ((f32[16,1,128]{2,1,0:T(1,128)}), f32[16,1,128]{2,1,0:T(1,128)S(1)}, u32[]{:S(2)}, u32[]{:S(2)}) async-start(f32[16,1,128]{2,1,0:T(1,128)} %bitcast.15), calls=%async_computation.2 | async-start | bytes 16384 | tf_op jit(solution)/shard_map/all_to_all | solution.py:1148
  254.0 19.6 %all-to-all-start.2 = ((bf16[16,128,128]{2,1,0:T(8,128)(2,1)}), bf16[16,128,128]{2,1,0:T(8,128)(2,1)S(1)}, u32[]{:S(2)}, u32[]{:S(2)}) async-start(bf16[16,128,128]{2,1,0:T(8,128)(2,1)} %get-tuple-element.158), calls=%async_computation.3 | async-start | bytes 1048576 | tf_op jit(solution)/shard_map/all_to_all | solution.py:1148
  259.1 149.0 %all-gather.20.cloned.1.call-start = ((), (), s32[]{:S(2)}) async-start(), calls=%async_computation.12 | async-start | bytes 4874240 | tf_op jit(solution)/shard_map/all_gather | solution.py:1129
  259.2 39.8 %copy-start.20 = (bf16[960,640]{1,0:T(8,128)(2,1)}, bf16[960,640]{1,0:T(8,128)(2,1)S(1)}, u32[]{:S(2)}) copy-start(bf16[960,640]{1,0:T(8,128)(2,1)S(1)} %collective-permute-done.12) | copy-start | bytes 3686404
  259.2 14.4 %copy-start.21 = (bf16[448,1280]{1,0:T(8,128)(2,1)}, bf16[448,1280]{1,0:T(8,128)(2,1)S(1)}, u32[]{:S(2)}) copy-start(bf16[448,1280]{1,0:T(8,128)(2,1)S(1)} %collective-permute-done.13) | copy-start | bytes 3440644
  273.6 27.9 %all-to-all-start.3 = ((bf16[16,144,128]{2,1,0:T(8,128)(2,1)}), bf16[16,144,128]{2,1,0:T(8,128)(2,1)S(1)}, u32[]{:S(2)}, u32[]{:S(2)}) async-start(bf16[16,144,128]{2,1,0:T(8,128)(2,1)} %get-tuple-element.174), calls=%async_computation.4 | async-start | bytes 1179648 | tf_op jit(solution)/shard_map/all_to_all | solution.py:1308
  279.9 21.7 %collective-permute-start.14 = (bf16[240,1792]{1,0:T(8,128)(2,1)}, bf16[240,1792]{1,0:T(8,128)(2,1)S(1)}, u32[]{:S(2)}, u32[]{:S(2)}) collective-permute-start(bf16[240,1792]{1,0:T(8,128)(2,1)} %slice.226), channel_id=1, source_target_pairs={{0,1},{1,0},{2,3},{3,2},{4,5},{5,4},{6,7},{7,6},{8,9},{9,8},{10,11... | collective-permute-start | bytes 2580488 | tf_op jit(solution)/shard_map/ppermute | solution.py:1119
  302.5 41.8 %all-to-all-start.4 = ((bf16[16,128,384]{2,1,0:T(8,128)(2,1)}), bf16[16,128,384]{2,1,0:T(8,128)(2,1)S(1)}, u32[]{:S(2)}, u32[]{:S(2)}) async-start(bf16[16,128,384]{2,1,0:T(8,128)(2,1)} %bitcast.56), calls=%async_computation.5 | async-start | bytes 3145728 | tf_op jit(solution)/shard_map/all_to_all | solution.py:1148
  308.2 107.8 %all-gather.18.cloned.1.call-start = ((), (), s32[]{:S(2)}) async-start(), calls=%async_computation.11 | async-start | bytes 11419648 | tf_op jit(solution)/shard_map/all_gather | solution.py:1129
  318.1 7.7 %collective-permute-start.16 = (bf16[656,128]{1,0:T(8,128)(2,1)S(1)}, bf16[656,128]{1,0:T(8,128)(2,1)S(1)}, u32[]{:S(2)}, u32[]{:S(2)}) collective-permute-start(bf16[656,128]{1,0:T(8,128)(2,1)S(1)} %pad_maximum_fusion.8), channel_id=1, source_target_pairs={{0,1},{1,0},{2,3},{3,2},{4,5},{5,4},{6,7},{7,6},{8,9},{9,8},{10,11... | collective-permute-start | bytes 503816 | tf_op jit(solution)/shard_map/ppermute | solution.py:1119
  319.6 18.8 %copy-start.15 = (bf16[640,128]{1,0:T(8,128)(2,1)S(1)}, bf16[640,128]{1,0:T(8,128)(2,1)}, u32[]{:S(2)}) copy-start(bf16[640,128]{1,0:T(8,128)(2,1)} %copy-done.14) | copy-start | bytes 491524
  319.6 18.8 %copy-start.17 = (bf16[640,128]{1,0:T(8,128)(2,1)S(1)}, bf16[640,128]{1,0:T(8,128)(2,1)}, u32[]{:S(2)}) copy-start(bf16[640,128]{1,0:T(8,128)(2,1)} %copy-done.16) | copy-start | bytes 491524
  325.1 13.7 %copy-start.12 = (f32[1280,128]{1,0:T(8,128)S(1)}, f32[1280,128]{1,0:T(8,128)}, u32[]{:S(2)}) copy-start(f32[1280,128]{1,0:T(8,128)} %turned_product.2) | copy-start | bytes 1966084
  325.1 13.3 %collective-permute-start.15 = (bf16[640,384]{1,0:T(8,128)(2,1)S(1)}, bf16[640,384]{1,0:T(8,128)(2,1)S(1)}, u32[]{:S(2)}, u32[]{:S(2)}) collective-permute-start(bf16[640,384]{1,0:T(8,128)(2,1)S(1)} %dynamic-slice_convert_fusion), channel_id=1, source_target_pairs={{0,1},{1,0},{2,3},{3,2},{4,5},{5,4},{6,7},{7,6},{8,9},{9,8},{10,11... | collective-permute-start | bytes 1474568 | tf_op jit(solution)/shard_map/ppermute | solution.py:1119
  344.3 5.6 %copy-start.3 = (bf16[16,128,384]{2,1,0:T(8,128)(2,1)}, bf16[16,128,384]{2,1,0:T(8,128)(2,1)S(1)}, u32[]{:S(2)}) copy-start(bf16[16,128,384]{2,1,0:T(8,128)(2,1)S(1)} %all-to-all-done.4.got_ref) | copy-start | bytes 4718596
  344.3 6.3 %copy-start.10 = (bf16[640,1792]{1,0:T(8,128)(2,1)S(1)}, bf16[640,1792]{1,0:T(8,128)(2,1)}, u32[]{:S(2)}) copy-start(bf16[640,1792]{1,0:T(8,128)(2,1)} %get-tuple-element.171) | copy-start | bytes 6881284
  347.3 6.0 %copy-start.8 = (f32[448,1280]{1,0:T(8,128)S(1)}, f32[448,1280]{1,0:T(8,128)}, u32[]{:S(2)}) copy-start(f32[448,1280]{1,0:T(8,128)} %get-tuple-element.197) | copy-start | bytes 6881284
  347.3 6.0 %copy-start.22 = (bf16[448,1280]{1,0:T(8,128)(2,1)S(1)}, bf16[448,1280]{1,0:T(8,128)(2,1)}, u32[]{:S(2)}) copy-start(bf16[448,1280]{1,0:T(8,128)(2,1)} %copy-done.21) | copy-start | bytes 3440644
  349.9 43.8 %collective-permute-start.17 = (bf16[1920,640]{1,0:T(8,128)(2,1)}, bf16[1920,640]{1,0:T(8,128)(2,1)}, u32[]{:S(2)}, u32[]{:S(2)}) collective-permute-start(bf16[1920,640]{1,0:T(8,128)(2,1)} %constant_dynamic-update-slice_fusion.near_ref), channel_id=1, source_target_pairs={{0,2},{2,0},{4,6},{6,4},{8,10},{10,8},{12,14},{14,12},{16,18},{18,... | collective-permute-start | bytes 7372808 | tf_op jit(solution)/shard_map/ppermute | solution.py:1353
  351.8 51.3 %collective-permute-start.18 = (bf16[400,1792]{1,0:T(8,128)(2,1)}, bf16[400,1792]{1,0:T(8,128)(2,1)}, u32[]{:S(2)}, u32[]{:S(2)}) collective-permute-start(bf16[400,1792]{1,0:T(8,128)(2,1)} %slice.237), channel_id=1, source_target_pairs={{0,1},{1,0},{2,3},{3,2},{4,5},{5,4},{6,7},{7,6},{8,9},{9,8},{10,11... | collective-permute-start | bytes 4300808 | tf_op jit(solution)/shard_map/ppermute | solution.py:1119
  364.0 28.8 %copy-start.7 = (f32[1280,128]{1,0:T(8,128)S(1)}, f32[1280,128]{1,0:T(8,128)}, u32[]{:S(2)}) copy-start(f32[1280,128]{1,0:T(8,128)} %turned_product.3) | copy-start | bytes 1966084
  364.0 28.8 %collective-permute-start.19 = (f32[640,16]{1,0:T(8,128)S(1)}, f32[640,16]{1,0:T(8,128)S(1)}, u32[]{:S(2)}, u32[]{:S(2)}) collective-permute-start(f32[640,16]{1,0:T(8,128)S(1)} %slice.261), channel_id=1, source_target_pairs={{0,1},{1,0},{2,3},{3,2},{4,5},{5,4},{6,7},{7,6},{8,9},{9,8},{10,11... | collective-permute-start | bytes 122888 | tf_op jit(solution)/shard_map/ppermute | solution.py:1119
  416.0 13.7 %copy-start.1 = (bf16[448,1280]{1,0:T(8,128)(2,1)S(1)}, bf16[448,1280]{1,0:T(8,128)(2,1)}, u32[]{:S(2)}) copy-start(bf16[448,1280]{1,0:T(8,128)(2,1)} %param.25) | copy-start | bytes 3440644
  (10 other events, 13.6 us)
Sparse Core Ops, SparseCore 0:
  9.7 39.8 all-gather.15
  51.8 47.2 all-gather.9
  106.1 36.4 all-gather.11
  144.6 36.1 all-gather.13
  186.3 60.4 reduce-scatter.1
  273.7 57.3 all-gather.19
  344.4 66.0 all-gather.17
where the time goes:
time: 441 us; the launch traced here: 437 us
  Pallas kernels  158 us (36%)
  waiting for transfers between devices  151 us (34%)
  starting transfers between devices  49.1 us (11%)
  local copies, waits for them, and re-layouts  31.1 us (7%)
  other arithmetic  21.9 us (5%)
  between operations  15 us (3%)
  matrix products  10.5 us (2%)
    ppermute x18, waiting for transfers between devices, across(): return lax.ppermute(value, 'fsdp', [(0, 1), (1, 0)])  106 us
    pallas_call x1, Pallas kernels, run_experts(): pl.pallas_call(functools.partial(experts_kernel, capacity, tokens, expert...  36 us
    all_to_all x4, waiting for transfers between devices, swapped(): return lax.all_to_all(value, 'ctx', split_axis=0, concat_axis=0, tiled=True)  27.6 us
    pallas_call x2, Pallas kernels, slot_grads(): pl.pallas_call(slot_grads_kernel, grid=(wide // (2 * HEAD_DIM),), in_spec...  23.6 us
    ppermute x18, starting transfers between devices, across(): return lax.ppermute(value, 'fsdp', [(0, 1), (1, 0)])  23.5 us
    all_to_all x4, starting transfers between devices, swapped(): return lax.all_to_all(value, 'ctx', split_axis=0, concat_axis=0, tiled=True)  20.9 us
    pallas_call x1, Pallas kernels, attend_back(): pl.pallas_call(functools.partial(attend_back_kernel, ring), grid=(length...  17.6 us
    pallas_call x2, Pallas kernels, turned_product(): pl.pallas_call(turned_product_kernel, grid=(length // tile,), in_specs=[p...  15.7 us
  transfers between devices with their start and end apart: 32, of which 15 were waited for; matrix products, arithmetic and copies ran while one was open for 13% of the time, Pallas kernels for 34%

commit v1 on v0

--- a/solution.py
+++ b/solution.py
@@ -43,18 +43,19 @@
 def rotary_tables(starts, count, width):
     half = width // 2
     freqs = jnp.exp(-math.log(10000.0) * jnp.arange(half, dtype=f32) * 2.0 / width)
+    freqs = jnp.concatenate([freqs, freqs])
     first = starts.astype(f32)[:, None] * freqs[None, :]
     second = jnp.arange(count, dtype=f32)[:, None] * freqs[None, :]
     angles = jnp.concatenate([first, second], axis=0)
-    cosine, sine = lax.optimization_barrier((jnp.cos(angles), jnp.sin(angles)))
+    sign = jnp.where(jnp.arange(width) < half, -1.0, 1.0)
+    cosine, sine = lax.optimization_barrier((jnp.cos(angles), jnp.sin(angles) * sign))
     spans = starts.shape[0]
     cos_a, sin_a = cosine[:spans, None], sine[:spans, None]
     cos_b, sin_b = cosine[None, spans:], sine[None, spans:]
-    cosine = (cos_a * cos_b - sin_a * sin_b).reshape(spans * count, half)
-    sine = (sin_a * cos_b + cos_a * sin_b).reshape(spans * count, half)
+    shape = (spans * count, width)
     return (
-        jnp.concatenate([cosine, cosine], axis=1),
-        jnp.concatenate([-sine, sine], axis=1),
+        (cos_a * cos_b - sin_a * sin_b).reshape(shape),
+        (sin_a * cos_b + cos_a * sin_b).reshape(shape),
     )
 
 
@@ -282,7 +283,7 @@
 
 def project(side, x, gain, own, other, cosine, sine):
     length, width = x.shape
-    tile = min(TILE // 2, length)
+    tile = min(TILE, length)
     part = pl.BlockSpec((tile, HEAD_DIM), lambda i: (i, 0))
     wide = pl.BlockSpec((tile, width), lambda i: (i, 0))
     return pl.pallas_call(
@@ -360,7 +361,7 @@
         far_sum_ref[...] += dot(got_ref[theirs], far_ref[at, :])
         return carry
 
-    lax.fori_loop(0, HEADS // 2, visit, 0)
+    lax.fori_loop(0, HEADS // 2, visit, 0, unroll=True)
     second, near, far = second_ref[...], near_sum_ref[...], far_sum_ref[...]
     second += jnp.where(
         spot_ref[1] == 0,
@@ -466,7 +467,7 @@
         send_ref[theirs] = other.astype(bf16)
         return carry
 
-    lax.fori_loop(0, HEADS // 2, visit, 0)
+    lax.fori_loop(0, HEADS // 2, visit, 0, unroll=True)
     for h in ring_of(spans)[HEADS:]:
         send_ref[h] = jnp.zeros((tokens, HEAD_DIM), bf16)
 
@@ -496,8 +497,10 @@
     wq_ref,
     wk_ref,
     wv_ref,
-    near_ref,
-    far_ref,
+    near_q_ref,
+    near_rest_ref,
+    far_q_ref,
+    far_rest_ref,
     x_ref,
     gain_ref,
     grad_second_ref,
@@ -520,7 +523,8 @@
         upper = pl.ds(pl.multiple_of((count + h) * HEAD_DIM, HEAD_DIM), HEAD_DIM)
         for i, weight in enumerate((wq_ref, wk_ref, wv_ref)):
             at = slice(i * HEAD_DIM, (i + 1) * HEAD_DIM)
-            rows = slice(i * half, (i + 1) * half)
+            near_ref, far_ref = (near_rest_ref, far_rest_ref) if i else (near_q_ref, far_q_ref)
+            rows = slice(max(i - 1, 0) * half, max(i, 1) * half)
             grads = jnp.concatenate([got_ref[low, :, at], got_ref[high, :, at]], axis=1)
             weights = jnp.concatenate([weight[:, window], weight[:, upper]], axis=1)
             own_sum_ref[...] += dot_nt(grads, weights)
@@ -543,12 +547,13 @@
     out_ref[...] = grad_second_ref[...] + scale * hat - resid * (scale * scale * scale) * mean
 
 
-def inputs_back(side, core, got, w_query, w_key, w_value, near, far, x, gain, grad_second):
+def inputs_back(side, core, got, *values):
+    x = values[-3]
     smem = pl.BlockSpec(memory_space=pltpu.SMEM)
     memory = pl.BlockSpec(memory_space=pltpu.VMEM)
     return pl.pallas_call(
         inputs_back_kernel,
-        in_specs=[smem] * 2 + [memory] * 9,
+        in_specs=[smem] * 2 + [memory] * (1 + len(values)),
         out_specs=memory,
         out_shape=jax.ShapeDtypeStruct(x.shape, f32),
         scratch_shapes=[pltpu.VMEM((x.shape[0], x.shape[1] // 2), f32)] * 2,
@@ -557,14 +562,7 @@
         side.reshape(1),
         core.reshape(1),
         got,
-        w_query,
-        w_key,
-        w_value,
-        near,
-        far,
-        x,
-        gain,
-        grad_second,
+        *values,
     )
 
 
@@ -768,7 +766,8 @@
     grad_slots_ref,
     own_in_ref,
     first_in_ref,
-    rest_in_ref,
+    middle_in_ref,
+    last_in_ref,
     own_down_ref,
     other_down_ref,
     own_shared_in_ref,
@@ -794,11 +793,11 @@
     def _():
         side = here_ref[1]
         rows = own_in_ref.shape[0]
-        first = first_in_ref.shape[0]
+        in_ref[pl.ds(pl.multiple_of(side * rows, 64), rows), :] = own_in_ref[...]
         at = (1 - side) * rows
-        in_ref[pl.ds(pl.multiple_of(side * rows, 64), rows), :] = own_in_ref[...]
-        in_ref[pl.ds(pl.multiple_of(at, 16), first), :] = first_in_ref[...]
-        in_ref[pl.ds(pl.multiple_of(at + first, 16), rows - first), :] = rest_in_ref[...]
+        for ref in (first_in_ref, middle_in_ref, last_in_ref):
+            in_ref[pl.ds(pl.multiple_of(at, 16), ref.shape[0]), :] = ref[...]
+            at = at + ref.shape[0]
         rows = own_down_ref.shape[0]
         down_ref[pl.ds(pl.multiple_of(side * rows, 64), rows), :] = own_down_ref[...]
         down_ref[pl.ds(pl.multiple_of((1 - side) * rows, 64), rows), :] = other_down_ref[...]
@@ -869,7 +868,7 @@
     grad_dispatched_ref[...] = grad_dispatched
     scaled_ref[...] = scaled
     lanes = shared_out_ref.shape[0]
-    size = min(2 * HEAD_DIM, chunk)
+    size = min(4 * HEAD_DIM, chunk)
 
     def visit(i, carry):
         at = pl.ds(pl.multiple_of(i * size, size), size)
@@ -1023,6 +1022,42 @@
     )(side.reshape(1), left, right)
 
 
+def shared_grads_kernel(grad_ref, normed_ref, hidden_ref, g_ref, in_ref, out_ref):
+    @pl.when(pl.program_id(0) == 0)
+    def _():
+        in_ref[...] = jnp.zeros_like(in_ref)
+        out_ref[...] = jnp.zeros_like(out_ref)
+
+    in_ref[...] += dot_tn(grad_ref[...], normed_ref[...])
+    out_ref[...] += dot_tn(hidden_ref[...], g_ref[...])
+
+
+def shared_products(grad, normed_wide, hidden, g_wide, width):
+    length, lanes = hidden.shape
+    tile = 4 * HEAD_DIM
+
+    def block(columns):
+        return pl.BlockSpec((tile, columns), lambda i: (i, 0))
+
+    def whole(rows):
+        return pl.BlockSpec((rows, width), lambda i: (0, 0))
+
+    return pl.pallas_call(
+        shared_grads_kernel,
+        grid=(length // tile,),
+        in_specs=[block(2 * lanes), block(width), block(lanes), block(width)],
+        out_specs=[whole(2 * lanes), whole(lanes)],
+        out_shape=[
+            jax.ShapeDtypeStruct((2 * lanes, width), f32),
+            jax.ShapeDtypeStruct((lanes, width), f32),
+        ],
+        name="shared_products",
+        cost_estimate=pl.CostEstimate(
+            flops=6 * length * lanes * width, bytes_accessed=6 * length * width, transcendentals=0
+        ),
+    )(grad, normed_wide, hidden, g_wide)
+
+
 def turned_product_kernel(side_ref, left_ref, right_ref, out_ref, sum_ref):
     step = pl.program_id(0)
 
@@ -1049,7 +1084,7 @@
 
 def turned_product(side, left, right, wide):
     length, lanes = right.shape
-    tile = 2 * HEAD_DIM
+    tile = 4 * HEAD_DIM
     return pl.pallas_call(
         turned_product_kernel,
         grid=(length // tile,),
@@ -1177,12 +1212,12 @@
     router_w = small[:experts]
     gain_one = small[experts : experts + 1].astype(f32)
     gain_two = small[experts + 1 :].astype(f32)
-    quarter = half // 8
-    chunks = [expert_in[0, :quarter], expert_in[0, quarter:]]
+    quarter = half // 4
+    chunks = [expert_in[0, :quarter], expert_in[0, quarter:-quarter], expert_in[0, -quarter:]]
     head_other, *chunks = tied(head_other, *chunks)
     chunks = [across(chunk) for chunk in chunks]
-    x_all, cosine, sine, head_other, gain_one, output_near, chunks[0] = tied(
-        x_all, cosine, sine, head_other, gain_one, output_near, chunks[0]
+    x_all, cosine, sine, head_other, gain_one, output_near = tied(
+        x_all, cosine, sine, head_other, gain_one, output_near
     )
     output_far = lax.ppermute(output_near, "ctx", swap_core)
     g_wide_all = everyone(after(g_wide, x_all))
@@ -1193,7 +1228,7 @@
         side, x_all, gain_one, head_own, head_other, cosine, sine
     )
     context, lse, attended = attend(query, key, value, is_ring)
-    attended, output_far = tied(attended, output_far)
+    attended, output_far, chunks[0] = tied(attended, output_far, chunks[0])
     down_other = across(after(expert_out[0], attended))
     got = swapped(attended.reshape(spans, tokens, HEAD_DIM))
     got, chunks[1] = tied(got, chunks[1])
@@ -1211,7 +1246,7 @@
         own_table,
         experts,
     )
-    normed2_wide, g_wide_all = tied(normed2_wide, g_wide_all)
+    normed2_wide, g_wide_all, chunks[2] = tied(normed2_wide, g_wide_all, chunks[2])
     normed2_wide = everyone(normed2_wide)
     grad_slots = pick_slots(here, g_wide_all, width, capacity, tokens)
     shared_in_other = across(after(shared_in_own, grad_slots))
@@ -1224,8 +1259,7 @@
     dense = [
         columns(after(w, grad_slots), core * half, half) for w in (w_query, w_key, w_value)
     ]
-    dense = jnp.concatenate(dense, axis=0)
-    near = [across(dense[: dense.shape[0] // 2]), across(dense[dense.shape[0] // 2 :])]
+    near = [across(dense[0]), across(jnp.concatenate(dense[1:], axis=0))]
     spots = [ring_position(i, spans) for i in range(spans)]
     (
         dispatched,
@@ -1243,8 +1277,7 @@
         grad_slots,
         (
             expert_in[0],
-            chunks[0],
-            chunks[1],
+            *chunks,
             expert_out[0],
             down_other,
             shared_in_own,
@@ -1260,12 +1293,14 @@
         parts, "ctx", scatter_dimension=0, tiled=True, axis_index_groups=groups
     )
     gate_dot = gate_dot[0].reshape(spans, tokens)
-    grad_shared_in = dot_tn(grad_sproj, normed2_all)
+    grad_shared_in, grad_shared_out = shared_products(
+        grad_sproj, normed2_wide, shared_hidden, g_wide_all, width
+    )
     grad_shared_in = jnp.concatenate(
         [grad_shared_in[:units], grad_shared_in[lanes : lanes + units]], axis=0
     )
     grad_shared_in = reduced(grad_shared_in, 1).astype(bf16)
-    grad_shared_out = dot_tn(shared_hidden, g_all)[:units].astype(bf16)
+    grad_shared_out = grad_shared_out[:units].astype(bf16)
     grad_shared_out = grad_shared_out.astype(f32) + across(grad_shared_out).astype(f32)
     grad_shared_out = grad_shared_out.astype(bf16)
     shared_grads = jnp.concatenate(
@@ -1277,14 +1312,16 @@
     own_down, down_theirs = slot_grads(side, expert_hidden, grad_result)
     own_in, in_theirs = slot_grads(side, dispatched, grad_proj)
     down_theirs = across(after(down_theirs, parts))
+    cuts_at = [0, half // 4, half * 9 // 16, half]
     sums, in_theirs, shared_grads, gate_grads = tied(
         sums,
         in_theirs,
         row_major(shared_grads),
         gate_grads,
     )
-    split = half * 3 // 8
-    in_upper = across(in_theirs[:split])
+    split = half * 5 // 16
+    in_parts = [in_theirs[a:b] for a, b in zip(cuts_at, cuts_at[1:])]
+    in_parts[0], in_parts[1] = across(in_parts[0]), across(in_parts[1])
 
     sent, cuts, grad_second, layer_out = mix_back(
         spot,
@@ -1302,8 +1339,8 @@
         spans,
     )
     arrived = swapped(sent).reshape(length, HEAD_DIM)
-    arrived, shared_grads, cuts, near[1], down_theirs = tied(
-        arrived, shared_grads, cuts, near[1], down_theirs
+    arrived, shared_grads, cuts, near[1], down_theirs, in_parts[0] = tied(
+        arrived, shared_grads, cuts, near[1], down_theirs, in_parts[0]
     )
     cuts = lax.all_to_all(
         cuts, "ctx", split_axis=0, concat_axis=0, tiled=True, axis_index_groups=groups
@@ -1313,7 +1350,7 @@
     grad_heads, grad_heads_ring = attend_back(
         query, key, value, arrived, context, lse, cosine, sine, is_ring
     )
-    grad_heads, grad_heads_ring, in_upper = tied(grad_heads, grad_heads_ring, in_upper)
+    grad_heads, grad_heads_ring, in_parts[1] = tied(grad_heads, grad_heads_ring, in_parts[1])
     cut = width // spans
     gain_rows = cuts[:, tokens : tokens + 2, :cut].astype(f32)
     gain_rows = jnp.sum(gain_rows, axis=(0, 1))
@@ -1326,6 +1363,8 @@
     gain_low = jnp.roll((gain_rows - gain_high.astype(f32)).astype(bf16), 1, axis=0)
     theirs = jnp.concatenate([theirs.astype(bf16), gain_high + gain_low], axis=0)
     grad_heads_ring, theirs = tied(grad_heads_ring, theirs)
+    head_mine, head_theirs = halves(dot_tn(normed1_all, grad_heads_ring))
+    head_theirs = head_theirs.astype(bf16)
     theirs = across(theirs).astype(f32)
     grad_output = mine + theirs[:half]
     gain_rows = gain_rows[:1] + theirs[half : half + 1] + theirs[half + 1 : half + 2]
@@ -1334,8 +1373,6 @@
     gain_rows = jnp.pad(
         jnp.concatenate([gain_high, gain_low], axis=0), ((0, 14), (3 * HEAD_DIM, 0))
     )
-    head_mine, head_theirs = halves(dot_tn(normed1_all, grad_heads_ring))
-    head_theirs = head_theirs.astype(bf16)
     got = swapped(grad_heads.reshape(spans, tokens, 3 * HEAD_DIM))
     grad_head_w = (head_mine + across(head_theirs).astype(f32)).astype(bf16)
     part = jnp.sum(grad_head_w.astype(f32) * head_own.astype(f32), axis=1, keepdims=True)
@@ -1346,23 +1383,22 @@
     grad_output = jnp.where(lane == cut + 1, part - part_high, grad_output)
     head_grads = jnp.concatenate([grad_head_w, grad_output.astype(bf16)], axis=1)
     head_grads = jnp.concatenate([head_grads, gain_rows], axis=0)
-    in_lower = across(after(in_theirs[split:], head_grads))
+    head_pack = head_grads
     head_grads, got = tied(row_major(head_grads), got)
     head_grads = everyone(head_grads[None])
-    near = jnp.concatenate(near, axis=0)
-    far = lax.ppermute(near, "ctx", swap_core)
+    in_parts[2] = across(after(in_parts[2], head_pack))
+    far = [lax.ppermute(part, "ctx", swap_core) for part in near]
 
     grad_inputs = inputs_back(
-        side, core, got, w_query, w_key, w_value, near, far, x, gain_one, grad_second
-    )
-    grad_inputs, in_lower = tied(grad_inputs, in_lower)
+        side, core, got, w_query, w_key, w_value, *near, *far, x, gain_one, grad_second
+    )
     grad_query, grad_key, grad_value, grad_output, grad_norm1, grad_norm2 = place_heads(
         side, head_grads, norm1_gain.astype(f32), width
     )
     grad_expert_in = jnp.concatenate(
         [
-            own_in[:split] + in_upper.astype(f32),
-            own_in[split:] + in_lower.astype(f32),
+            own_in[a:b] + part.astype(f32)
+            for a, b, part in zip(cuts_at, cuts_at[1:], in_parts)
         ],
         axis=0,
     )

time: 441 us -> 428 us (0.971)
  local copies, waits for them, and re-layouts: 31.1 us -> 22.9 us
  matrix products: 10.5 us -> 5.37 us
    all_gather x6, waiting for transfers between devices: 2.74 us -> 17.7 us  [everyone(): lax.all_gather(value, 'ctx', axis=0, tiled=True, axis_index_groups=groups)]
    pallas_call x1 -> x2, Pallas kernels: 9.45 us -> 17 us  [the longest x1 9.52 us: inputs_back(): pl.pallas_call(inputs_back_kernel, in_specs=[smem] * 2 + [memory] * (1 +...]
    all_to_all x4, waiting for transfers between devices: 27.6 us -> 21.3 us  [swapped(): return lax.all_to_all(value, 'ctx', split_axis=0, concat_axis=0, tiled=True)]
    unnamed x85 -> x70, local copies, waits for them, and re-layouts: 9.14 us -> 3.06 us
    dot_general x3 -> x1, matrix products: 10.5 us -> 5.37 us  [dot_tn(): lax.dot_general(a, b, (((0,), (0,)), ((), ())), preferred_element_type=f32)]
    ppermute x18 -> x20, waiting for transfers between devices: 106 us -> 103 us  [across(): return lax.ppermute(value, 'fsdp', [(0, 1), (1, 0)])]
    ppermute x18 -> x20, starting transfers between devices: 23.5 us -> 25.4 us  [across(): return lax.ppermute(value, 'fsdp', [(0, 1), (1, 0)])]
  transfers between devices with their start and end apart: 32 -> 35, of which waited for: 15 -> 18; matrix products, arithmetic and copies ran while one was open for 13% -> 11% of each run, Pallas kernels for 34% -> 34%
where the time goes in v1:
time: 428 us; the launch traced here: 427 us
  Pallas kernels  155 us (36%)
  waiting for transfers between devices  153 us (36%)
  starting transfers between devices  51.1 us (12%)
  other arithmetic  24 us (6%)
  local copies, waits for them, and re-layouts  22.9 us (5%)
  between operations  14.9 us (3%)
  matrix products  5.37 us (1%)
    ppermute x20, waiting for transfers between devices, across(): return lax.ppermute(value, 'fsdp', [(0, 1), (1, 0)])  103 us
    pallas_call x1, Pallas kernels, run_experts(): pl.pallas_call(functools.partial(experts_kernel, capacity, tokens, expert...  32.5 us
    ppermute x20, starting transfers between devices, across(): return lax.ppermute(value, 'fsdp', [(0, 1), (1, 0)])  25.4 us
    pallas_call x2, Pallas kernels, slot_grads(): pl.pallas_call(slot_grads_kernel, grid=(wide // (2 * HEAD_DIM),), in_spec...  23.6 us
    all_to_all x4, waiting for transfers between devices, swapped(): return lax.all_to_all(value, 'ctx', split_axis=0, concat_axis=0, tiled=True)  21.3 us
    all_to_all x4, starting transfers between devices, swapped(): return lax.all_to_all(value, 'ctx', split_axis=0, concat_axis=0, tiled=True)  18.4 us
    all_gather x6, waiting for transfers between devices, everyone(): lax.all_gather(value, 'ctx', axis=0, tiled=True, axis_index_groups=groups)  17.7 us
    pallas_call x1, Pallas kernels, attend_back(): pl.pallas_call(functools.partial(attend_back_kernel, ring), grid=(length...  17.6 us
  transfers between devices with their start and end apart: 35, of which 18 were waited for; matrix products, arithmetic and copies ran while one was open for 11% of the time, Pallas kernels for 34%

profile of v1, /device:TPU:0, one launch (start us, length us, event | category | flops | bytes accessed | tf_op | source)
XLA Modules:
  0.0 426.7 jit_solution(9891132984340700303)
XLA Ops:
  10.9 3.0 collective-permute-start
  15.0 2.0 collective-permute-start.1
  18.6 1.6 multiply_add_fusion
  23.9 19.4 %collective-permute-done.1 = bf16[18,640]{1,0:T(8,128)(2,1)S(1)} collective-permute-done((bf16[18,640]{1,0:T(8,128)(2,1)S(1)}, bf16[18,640]{1,0:T(8,128)(2,1)S(1)}, u32[]{:S(2)}, u32[]{:S(2)}) %collective-permute-start.1) | collective-permute-done | bytes 23072 | tf_op jit(solution)/shard_map/ppermute | solution.py:1154
  43.9 5.5 %all-gather.16.cloned.1.call-done = bf16[1,2048,1280]{2,1,0:T(8,128)(2,1)} async-done(((bf16[1,128,1280]{2,1,0:T(8,128)(2,1)}), bf16[1,2048,1280]{2,1,0:T(8,128)(2,1)}) %all-gather.16.cloned.1.call-update) | async-done | bytes 5242896 | tf_op jit(solution)/shard_map/all_gather | solution.py:1164
  49.7 1.6 collective-permute-start.4
  51.7 8.0 %project.1 = (bf16[2048,1280]{1,0:T(8,128)(2,1)}, bf16[2048,128]{1,0:T(8,128)(2,1)}, bf16[2048,128]{1,0:T(8,128)(2,1)}, bf16[2048,128]{1,0:T(8,128)(2,1)}) custom-call(s32[1]{0:T(128)} %bitcast.side_ref, bf16[2048,1280]{1,0:T(8,128)(2,1)} %bitcast.44, f32[1,1280]{1,0:T(1,128)} %get-tuple-element.113.gain_ref, bf16[640,384]{1,0:T(8,128)(2,1)} %copy-done.14, ...), custom_call_target="tpu_custom_call" | custom-call | flops 2013265920 | bytes 10485760 | tf_op jit(solution)/shard_map/project/pallas_call | solution.py:289
  59.7 9.5 %attend.1 = (f32[2048,128]{1,0:T(8,128)}, f32[1,2048]{1,0:T(1,128)}, bf16[2048,128]{1,0:T(8,128)(2,1)}) custom-call(bf16[2048,128]{1,0:T(8,128)(2,1)} %get-tuple-element.117.q_ref, bf16[2048,128]{1,0:T(8,128)(2,1)} %get-tuple-element.118.k_ref, bf16[2048,128]{1,0:T(8,128)(2,1)} %get-tuple-element.119.v_ref), custom_call_target="tpu_custom_call" | custom-call | flops 1073741824 | bytes 3145728 | tf_op jit(solution)/shard_map/attend/pallas_call | solution.py:134
  69.3 3.6 all-to-all-start
  72.9 1.5 collective-permute-start.6
  76.5 14.0 %collective-permute-done.5.middle_in_ref = bf16[320,1792]{1,0:T(8,128)(2,1)} collective-permute-done((bf16[320,1792]{1,0:T(8,128)(2,1)}, bf16[320,1792]{1,0:T(8,128)(2,1)}, u32[]{:S(2)}, u32[]{:S(2)}) %collective-permute-start.5) | collective-permute-done | bytes 1146912 | tf_op jit(solution)/shard_map/ppermute | solution.py:1154
  90.4 5.1 %all-to-all-done.got_ref = bf16[16,128,128]{2,1,0:T(8,128)(2,1)S(1)} async-done(((bf16[16,128,128]{2,1,0:T(8,128)(2,1)}), bf16[16,128,128]{2,1,0:T(8,128)(2,1)S(1)}, u32[]{:S(2)}, u32[]{:S(2)}) %all-to-all-start) | async-done | bytes 524320 | tf_op jit(solution)/shard_map/all_to_all | solution.py:1183
  96.3 4.8 %mix.1 = (f32[128,1280]{1,0:T(8,128)}, bf16[128,1408]{1,0:T(8,128)(2,1)}, f32[128,1]{1,0:T(8,128)}, f32[128,128]{1,0:T(8,128)}, bf16[128,1280]{1,0:T(8,128)(2,1)}) custom-call(s32[2]{0:T(128)} %pad_add_fusion.spot_ref, bf16[16,128,128]{2,1,0:T(8,128)(2,1)} %copy-done.12, bf16[640,1280]{1,0:T(8,128)(2,1)} %own_ref.3, bf16[640,640]{1,0:T(8,128)(2,1)} %copy-done.7, ...), custom_call_target="tpu_custom_call" | custom-call | tf_op jit(solution)/shard_map/mix/pallas_call | solution.py:392
  102.1 1.7 collective-permute-start.7
  103.8 1.2 constant_dynamic-slice_fusion.5
  105.2 5.8 %pick_slots.1.grad_slots_ref = bf16[896,1280]{1,0:T(8,128)(2,1)} custom-call(s32[1]{0:T(128)} %bitcast.2.here_ref, bf16[2048,1408]{1,0:T(8,128)(2,1)} %all-gather.10.cloned.1.call-done.g_ref), custom_call_target="tpu_custom_call" | custom-call | flops 1174405120 | bytes 8650752 | tf_op jit(solution)/shard_map/pick_slots/pallas_call | solution.py:737
  111.7 1.4 collective-permute-start.9
  113.1 17.6 %collective-permute-done.7.other_down_ref = bf16[448,1280]{1,0:T(8,128)(2,1)} collective-permute-done((bf16[448,1280]{1,0:T(8,128)(2,1)}, bf16[448,1280]{1,0:T(8,128)(2,1)}, u32[]{:S(2)}, u32[]{:S(2)}) %collective-permute-start.7) | collective-permute-done | bytes 1146912 | tf_op jit(solution)/shard_map/ppermute | solution.py:1154
  130.7 3.4 collective-permute-done.8.other_shared_in_ref
  134.1 1.5 collective-permute-done.9.other_shared_out_ref
  135.6 3.8 all-gather.12.cloned.1.call-done.normed_ref.left_ref
  140.4 1.6 collective-permute-start.10
  142.0 32.5 %experts.1 = (bf16[896,1280]{1,0:T(8,128)(2,1)}, bf16[896,896]{1,0:T(8,128)(2,1)}, bf16[896,1280]{1,0:T(8,128)(2,1)}, bf16[896,1792]{1,0:T(8,128)(2,1)}, bf16[20...) custom-call(s32[3]{0:T(128)} %pad_add_fusion.1.here_ref, ...), custom_call_target="tpu_custom_call" | custom-call | flops 20000000000 | bytes 40000000 | tf_op jit(solution)/shard_map/experts/pallas_call | solution.py:925
  174.6 3.2 all-gather.14.cloned.1.call-done.left_ref
  177.8 7.5 %shared_products.1 = (f32[256,1280]{1,0:T(8,128)}, f32[128,1280]{1,0:T(8,128)}) custom-call(bf16[2048,256]{1,0:T(8,128)(2,1)} %get-tuple-element.151.grad_ref, bf16[2048,1408]{1,0:T(8,128)(2,1)} %all-gather.12.cloned.1.call-done.normed_ref.left_ref, bf16[2048,128]{1,0:T(8,128)(2,1)} %get-tuple-element.152.hidden_ref, ...), custom_call_target="tpu_custom_call" | custom-call | flops 2013265920 | bytes 15728640 | tf_op jit(solution)/shard_map/shared_products/pallas_call | solution.py:1045
  185.3 1.2 fusion.24
  186.6 1.5 collective-permute-start.11
  189.9 1.3 pad_maximum_fusion
  191.2 1.4 collective-permute-start.13
  193.4 1.2 concatenate.65
  194.6 14.4 %slot_grads.2 = (f32[640,1792]{1,0:T(8,128)}, bf16[640,1792]{1,0:T(8,128)(2,1)}) custom-call(s32[1]{0:T(128)} %bitcast.side_ref, bf16[896,1280]{1,0:T(8,128)(2,1)} %get-tuple-element.148.left_ref, bf16[896,1792]{1,0:T(8,128)(2,1)} %get-tuple-element.149.right_ref), custom_call_target="tpu_custom_call" | custom-call | flops 4110417920 | bytes 12386304 | tf_op jit(solution)/shard_map/slot_grads/pallas_call | solution.py:1002
  209.0 9.2 %slot_grads.3 = (f32[448,1280]{1,0:T(8,128)}, bf16[448,1280]{1,0:T(8,128)(2,1)}) custom-call(s32[1]{0:T(128)} %bitcast.side_ref, bf16[896,896]{1,0:T(8,128)(2,1)} %get-tuple-element.169.left_ref, bf16[896,1280]{1,0:T(8,128)(2,1)} %get-tuple-element.170.right_ref), custom_call_target="tpu_custom_call" | custom-call | flops 2055208960 | bytes 7340032 | tf_op jit(solution)/shard_map/slot_grads/pallas_call | solution.py:1002
  220.0 3.7 all-to-all-start.1
  224.4 5.8 %all-to-all-done.1 = f32[16,1,128]{2,1,0:T(1,128)S(1)} async-done(((f32[16,1,128]{2,1,0:T(1,128)}), f32[16,1,128]{2,1,0:T(1,128)S(1)}, u32[]{:S(2)}, u32[]{:S(2)}) %all-to-all-start.1) | async-done | bytes 8224 | tf_op jit(solution)/shard_map/all_to_all | solution.py:1183
  230.3 10.8 %reduce-scatter.2.cloned.1.call-done.sums_ref = bf16[128,2560]{1,0:T(8,128)(2,1)} async-done(((bf16[2048,2560]{1,0:T(8,128)(2,1)}), bf16[128,2560]{1,0:T(8,128)(2,1)}) %reduce-scatter.2.cloned.1.call-update) | async-done | bytes 655376 | tf_op jit(solution)/shard_map/reduce_scatter | solution.py:1292
  241.7 5.2 %mix_back.1 = (bf16[16,128,128]{2,1,0:T(8,128)(2,1)}, bf16[16,144,128]{2,1,0:T(8,128)(2,1)}, f32[128,1280]{1,0:T(8,128)}, bf16[128,1280]{1,0:T(8,128)(2,1)}) custom-call(s32[2]{0:T(128)} %pad_add_fusion.spot_ref, bf16[128,2560]{1,0:T(8,128)(2,1)} %reduce-scatter.2.cloned.1.call-done.sums_ref, f32[128,128]{1,0:T(8,128)} %get-tuple-element.158.gates_ref, ...), custom_call_target="tpu_custom_call" | custom-call | tf_op jit(solution)/shard_map/mix_back/pallas_call | solution.py:479
  246.9 5.1 %all-to-all-start.2 = ((bf16[16,128,128]{2,1,0:T(8,128)(2,1)}), bf16[16,128,128]{2,1,0:T(8,128)(2,1)}, u32[]{:S(2)}, u32[]{:S(2)}) async-start(bf16[16,128,128]{2,1,0:T(8,128)(2,1)} %get-tuple-element.164), calls=%async_computation.3 | async-start | bytes 1048576 | tf_op jit(solution)/shard_map/all_to_all | solution.py:1183
  252.3 1.6 collective-permute-start.15
  254.0 1.4 collective-permute-done.14
  255.3 12.4 %collective-permute-done.15 = bf16[160,1792]{1,0:T(8,128)(2,1)} collective-permute-done((bf16[160,1792]{1,0:T(8,128)(2,1)S(1)}, bf16[160,1792]{1,0:T(8,128)(2,1)}, u32[]{:S(2)}, u32[]{:S(2)}) %collective-permute-start.15) | collective-permute-done | bytes 573472 | tf_op jit(solution)/shard_map/ppermute | solution.py:1154
  267.8 5.8 %all-to-all-start.3 = ((bf16[16,144,128]{2,1,0:T(8,128)(2,1)}), bf16[16,144,128]{2,1,0:T(8,128)(2,1)S(1)}, u32[]{:S(2)}, u32[]{:S(2)}) async-start(bf16[16,144,128]{2,1,0:T(8,128)(2,1)} %get-tuple-element.181), calls=%async_computation.4 | async-start | bytes 1179648 | tf_op jit(solution)/shard_map/all_to_all | solution.py:1345
  274.4 1.6 collective-permute-start.16
  276.0 17.6 %attend_back.1 = (bf16[2048,384]{1,0:T(8,128)(2,1)}, bf16[2048,384]{1,0:T(8,128)(2,1)}) custom-call(bf16[2048,128]{1,0:T(8,128)(2,1)} %get-tuple-element.117.q_ref, bf16[2048,128]{1,0:T(8,128)(2,1)} %get-tuple-element.118.k_ref, bf16[2048,128]{1,0:T(8,128)(2,1)} %get-tuple-element.119.v_ref, bf16[2048,128]{1,0:T(8,128)(2,1)} %bitcast.20.grad_ref, ...), custom_call_target="tpu_custom_call" | custom-call | flops 2684354560 | bytes 5242880 | tf_op jit(solution)/shard_map/attend_back/pallas_call | solution.py:243
  293.6 6.0 %all-to-all-start.4 = ((bf16[16,128,384]{2,1,0:T(8,128)(2,1)}), bf16[16,128,384]{2,1,0:T(8,128)(2,1)S(1)}, u32[]{:S(2)}, u32[]{:S(2)}) async-start(bf16[16,128,384]{2,1,0:T(8,128)(2,1)} %bitcast.55), calls=%async_computation.5 | async-start | bytes 3145728 | tf_op jit(solution)/shard_map/all_to_all | solution.py:1183
  300.5 5.9 %turned_product.2 = f32[1280,128]{1,0:T(8,128)} custom-call(s32[1]{0:T(128)} %bitcast.side_ref, bf16[2048,1280]{1,0:T(8,128)(2,1)} %all-gather.14.cloned.1.call-done.left_ref, bf16[2048,128]{1,0:T(8,128)(2,1)} %bitcast.45), custom_call_target="tpu_custom_call" | custom-call | flops 671088640 | bytes 5242880 | tf_op jit(solution)/shard_map/turned_product/pallas_call | solution.py:1088
  307.5 1.6 collective-permute-start.18
  309.1 5.4 %fusion.27 = f32[1280,384]{1,0:T(8,128)S(1)} fusion(bf16[2048,1280]{1,0:T(8,128)(2,1)} %get-tuple-element.163, bf16[2048,384]{1,0:T(8,128)(2,1)} %get-tuple-element.182), kind=kOutput, calls=%fused_computation.97 | convolution fusion | flops 2013265920 | bytes 8781824 | tf_op jit(solution)/shard_map/dot_general | solution.py:36
  315.2 12.7 %collective-permute-done.17 = bf16[640,384]{1,0:T(8,128)(2,1)S(1)} collective-permute-done((bf16[640,384]{1,0:T(8,128)(2,1)S(1)}, bf16[640,384]{1,0:T(8,128)(2,1)S(1)}, u32[]{:S(2)}, u32[]{:S(2)}) %collective-permute-start.17) | collective-permute-done | bytes 491552 | tf_op jit(solution)/shard_map/ppermute | solution.py:1154
  329.4 10.4 %all-to-all-done.4.got_ref = bf16[16,128,384]{2,1,0:T(8,128)(2,1)S(1)} async-done(((bf16[16,128,384]{2,1,0:T(8,128)(2,1)}), bf16[16,128,384]{2,1,0:T(8,128)(2,1)S(1)}, u32[]{:S(2)}, u32[]{:S(2)}) %all-to-all-start.4) | async-done | bytes 1572896 | tf_op jit(solution)/shard_map/all_to_all | solution.py:1183
  340.7 2.2 slice.235
  343.2 3.2 add_bitcast_fusion
  346.4 1.6 collective-permute-start.22
  348.0 1.5 convert_add_fusion.1
  349.5 6.1 %turned_product.3 = f32[1280,128]{1,0:T(8,128)} custom-call(s32[1]{0:T(128)} %bitcast.side_ref, bf16[2048,1408]{1,0:T(8,128)(2,1)} %all-gather.12.cloned.1.call-done.normed_ref.left_ref, bf16[2048,128]{1,0:T(8,128)(2,1)} %bitcast.46), custom_call_target="tpu_custom_call" | custom-call | flops 671088640 | bytes 5242880 | tf_op jit(solution)/shard_map/turned_product/pallas_call | solution.py:1088
  357.0 1.5 convert_add_fusion.2
  358.6 19.4 %collective-permute-done.21 = f32[640,16]{1,0:T(8,128)S(1)} collective-permute-done((f32[640,16]{1,0:T(8,128)S(1)}, f32[640,16]{1,0:T(8,128)S(1)}, u32[]{:S(2)}, u32[]{:S(2)}) %collective-permute-start.21) | collective-permute-done | bytes 40992 | tf_op jit(solution)/shard_map/ppermute | solution.py:1154
  378.9 2.0 convert_add_fusion
  381.0 2.4 maximum_bitcast_fusion
  383.4 9.5 %inputs_back.1 = f32[128,1280]{1,0:T(8,128)} custom-call(s32[1]{0:T(128)} %bitcast.side_ref, s32[1]{0:T(128)} %bitcast.1.core_ref, bf16[16,128,384]{2,1,0:T(8,128)(2,1)} %copy-done.3, bf16[640,1280]{1,0:T(8,128)(2,1)} %wq_ref.1, bf16[640,1280]{1,0:T(8,128)(2,1)} %wk_ref.1, bf16[640,1280]{1,0:T(8,128)(2,1)} %wv_ref.1, ...), custom_call_target="tpu_custom_call" | custom-call | tf_op jit(solution)/shard_map/inputs_back/pallas_call | solution.py:554
  392.9 8.0 %place_shared.1 = (f32[640,1792]{1,0:T(8,128)}, f32[448,1280]{1,0:T(8,128)}) custom-call(s32[1]{0:T(128)} %bitcast.side_ref, bf16[16,224,640]{2,1,0:T(8,128)(2,1)} %bitcast.47), custom_call_target="tpu_custom_call" | custom-call | tf_op jit(solution)/shard_map/place_shared/pallas_call | solution.py:679
  400.9 5.2 %all-gather.18.cloned.1.call-done = bf16[10496,512]{1,0:T(8,128)(2,1)} async-done(((bf16[656,512]{1,0:T(8,128)(2,1)}), bf16[10496,512]{1,0:T(8,128)(2,1)}) %all-gather.18.cloned.1.call-update) | async-done | bytes 10747920 | tf_op jit(solution)/shard_map/all_gather | solution.py:1164
  406.1 11.2 %place_heads.1 = (f32[640,1280]{1,0:T(8,128)}, f32[640,1280]{1,0:T(8,128)}, f32[640,1280]{1,0:T(8,128)}, f32[640,1280]{1,0:T(8,128)}, f32[1,640]{1,0:T(1,128)}, /*index=5*/f32[1,640]{1,0:T(1,128)}) custom-call(s32[1]{0:T(128)} %bitcast.side_ref, bf16[16,656,512]{2,1,0:T(8,128)(2,1)} %bitcast.41, bf16[16,656,512]{2,1,0:T(8,128)(2,1)} %bitcast.42, ...), custom_call_target="tpu_custom_call" | custom-call | tf_op jit(solution)/shard_map/place_heads/pallas_call | solution.py:631
  417.3 1.3 reduce.1
  418.6 1.3 reduce.2
  (189 shorter events, 31.5 us)
Async XLA Ops:
  7.2 98.0 %copy-start = (bf16[448,1280]{1,0:T(8,128)(2,1)S(1)}, bf16[448,1280]{1,0:T(8,128)(2,1)}, u32[]{:S(2)}) copy-start(bf16[448,1280]{1,0:T(8,128)(2,1)} %param.25) | copy-start | bytes 3440644
  7.2 6.7 %copy-start.2 = (bf16[640,1280]{1,0:T(8,128)(2,1)S(1)}, bf16[640,1280]{1,0:T(8,128)(2,1)}, u32[]{:S(2)}) copy-start(bf16[640,1280]{1,0:T(8,128)(2,1)} %own_ref.3) | copy-start | bytes 4915204
  7.2 7.7 %copy-start.27 = (bf16[640]{0:T(1024)(128)(2,1)S(1)}, bf16[640]{0:T(1024)(128)(2,1)}, u32[]{:S(2)}) copy-start(bf16[640]{0:T(1024)(128)(2,1)} %param.17) | copy-start | bytes 3844
  7.2 7.7 %copy-start.30 = (bf16[640]{0:T(1024)(128)(2,1)S(1)}, bf16[640]{0:T(1024)(128)(2,1)}, u32[]{:S(2)}) copy-start(bf16[640]{0:T(1024)(128)(2,1)} %param.22) | copy-start | bytes 3844
  7.2 7.7 %copy-start.26 = (bf16[640,16]{0,1:T(8,128)(2,1)S(1)}, bf16[640,16]{0,1:T(8,128)(2,1)}, u32[]{:S(2)}) copy-start(bf16[640,16]{0,1:T(8,128)(2,1)} %param.23) | copy-start | bytes 61444
  7.2 42.2 %all-gather.16.cloned.1.call-start = ((), (), s32[]{:S(2)}) async-start(), calls=%async_computation.10 | async-start | bytes 5570560 | tf_op jit(solution)/shard_map/all_gather | solution.py:1164
  8.0 9.1 %copy-start.31 = (f32[16]{0:T(128)S(1)}, f32[16]{0:T(128)}, u32[]{:S(2)}) copy-start(f32[16]{0:T(128)} %constant.125) | copy-start | bytes 196
  8.0 94.1 %all-gather.10.cloned.1.call-start = ((), (), s32[]{:S(2)}) async-start(), calls=%async_computation.6 | async-start | bytes 6127616 | tf_op jit(solution)/shard_map/all_gather | solution.py:1164
  9.0 8.5 %copy-start.28 = (s32[1,128,7]{1,0,2:T(1,128)S(1)}, s32[1,128,7]{1,0,2:T(1,128)}, u32[]{:S(2)}) copy-start(s32[1,128,7]{1,0,2:T(1,128)} %param.28) | copy-start | bytes 10756
  9.0 8.5 %copy-start.29 = (s32[1,1,896]{2,1,0:T(1,128)S(1)}, s32[1,1,896]{2,1,0:T(1,128)}, u32[]{:S(2)}) copy-start(s32[1,1,896]{2,1,0:T(1,128)} %param.29) | copy-start | bytes 10756
  10.9 9.3 %copy-start.14 = (bf16[640,384]{1,0:T(8,128)(2,1)}, bf16[640,384]{1,0:T(8,128)(2,1)S(1)}, u32[]{:S(2)}) copy-start(bf16[640,384]{1,0:T(8,128)(2,1)S(1)} %pad_maximum_fusion.2.own_ref) | copy-start | bytes 1474564
  10.9 33.0 %collective-permute-start = (bf16[640,384]{1,0:T(8,128)(2,1)S(1)}, bf16[640,384]{1,0:T(8,128)(2,1)}, u32[]{:S(2)}, u32[]{:S(2)}) collective-permute-start(bf16[640,384]{1,0:T(8,128)(2,1)S(1)} %pad_maximum_fusion.2.own_ref), channel_id=1, source_target_pairs={{0,1},{1,0},{2,3},{3,2},{4,5},{5,4},{6,7},{7,6},{8,9},{9,8},{10,11... | collective-permute-start | bytes 1474568 | tf_op jit(solution)/shard_map/ppermute | solution.py:1154
  14.8 29.1 %collective-permute-start.2 = (bf16[640,640]{1,0:T(8,128)(2,1)}, bf16[640,640]{1,0:T(8,128)(2,1)S(1)}, u32[]{:S(2)}, u32[]{:S(2)}) collective-permute-start(bf16[640,640]{1,0:T(8,128)(2,1)} %constant_dynamic-slice_fusion.6), channel_id=1, source_target_pairs={{0,1},{1,0},{2,3},{3,2},{4,5},{5,4},{6,7},{7,6},{8,9},{9,8},{10,11... | collective-permute-start | bytes 2457608 | tf_op jit(solution)/shard_map/ppermute | solution.py:1154
  15.0 28.3 %collective-permute-start.1 = (bf16[18,640]{1,0:T(8,128)(2,1)S(1)}, bf16[18,640]{1,0:T(8,128)(2,1)S(1)}, u32[]{:S(2)}, u32[]{:S(2)}) collective-permute-start(bf16[18,640]{1,0:T(8,128)(2,1)S(1)} %pad_maximum_fusion.8), channel_id=1, source_target_pairs={{0,1},{1,0},{2,3},{3,2},{4,5},{5,4},{6,7},{7,6},{8,9},{9,8},{10,11... | collective-permute-start | bytes 69128 | tf_op jit(solution)/shard_map/ppermute | solution.py:1154
  18.5 2.4 copy-start.10
  43.9 15.8 %copy-start.7 = (bf16[640,640]{1,0:T(8,128)(2,1)}, bf16[640,640]{1,0:T(8,128)(2,1)S(1)}, u32[]{:S(2)}) copy-start(bf16[640,640]{1,0:T(8,128)(2,1)S(1)} %collective-permute-done.2.near_ref) | copy-start | bytes 2457604
  49.4 19.9 %collective-permute-start.3 = (bf16[640,640]{1,0:T(8,128)(2,1)S(1)}, bf16[640,640]{1,0:T(8,128)(2,1)S(1)}, u32[]{:S(2)}, u32[]{:S(2)}) collective-permute-start(bf16[640,640]{1,0:T(8,128)(2,1)S(1)} %collective-permute-done.2.near_ref), channel_id=1, source_target_pairs={{0,2},{2,0},{4,6},{6,4},{8,10},{10,8},{12,14},{14,12},{16,18},{18,... | collective-permute-start | bytes 2457608 | tf_op jit(solution)/shard_map/ppermute | solution.py:1222
  49.7 19.6 %collective-permute-start.4 = (bf16[160,1792]{1,0:T(8,128)(2,1)}, bf16[160,1792]{1,0:T(8,128)(2,1)}, u32[]{:S(2)}, u32[]{:S(2)}) collective-permute-start(bf16[160,1792]{1,0:T(8,128)(2,1)} %get-tuple-element.122), channel_id=1, source_target_pairs={{0,1},{1,0},{2,3},{3,2},{4,5},{5,4},{6,7},{7,6},{8,9},{9,8},{10,11... | collective-permute-start | bytes 1720328 | tf_op jit(solution)/shard_map/ppermute | solution.py:1154
  51.3 39.1 %collective-permute-start.5 = (bf16[320,1792]{1,0:T(8,128)(2,1)}, bf16[320,1792]{1,0:T(8,128)(2,1)}, u32[]{:S(2)}, u32[]{:S(2)}) collective-permute-start(bf16[320,1792]{1,0:T(8,128)(2,1)} %slice_bitcast_fusion), channel_id=1, source_target_pairs={{0,1},{1,0},{2,3},{3,2},{4,5},{5,4},{6,7},{7,6},{8,9},{9,8},{10,11... | collective-permute-start | bytes 3440648 | tf_op jit(solution)/shard_map/ppermute | solution.py:1154
  69.3 26.3 %copy-start.8 = (bf16[640,640]{1,0:T(8,128)(2,1)}, bf16[640,640]{1,0:T(8,128)(2,1)S(1)}, u32[]{:S(2)}) copy-start(bf16[640,640]{1,0:T(8,128)(2,1)S(1)} %collective-permute-done.3.far_ref) | copy-start | bytes 2457604
  69.3 26.3 %all-to-all-start = ((bf16[16,128,128]{2,1,0:T(8,128)(2,1)}), bf16[16,128,128]{2,1,0:T(8,128)(2,1)S(1)}, u32[]{:S(2)}, u32[]{:S(2)}) async-start(bf16[16,128,128]{2,1,0:T(8,128)(2,1)} %bitcast.59), calls=%async_computation | async-start | bytes 1048576 | tf_op jit(solution)/shard_map/all_to_all | solution.py:1183
  72.9 66.6 %all-gather.12.cloned.1.call-start = ((), (), s32[]{:S(2)}) async-start(), calls=%async_computation.7 | async-start | bytes 6127616 | tf_op jit(solution)/shard_map/all_gather | solution.py:1164
  72.9 29.1 %collective-permute-start.6 = (bf16[160,1792]{1,0:T(8,128)(2,1)}, bf16[160,1792]{1,0:T(8,128)(2,1)}, u32[]{:S(2)}, u32[]{:S(2)}) collective-permute-start(bf16[160,1792]{1,0:T(8,128)(2,1)} %get-tuple-element.129), channel_id=1, source_target_pairs={{0,1},{1,0},{2,3},{3,2},{4,5},{5,4},{6,7},{7,6},{8,9},{9,8},{10,11... | collective-permute-start | bytes 1720328 | tf_op jit(solution)/shard_map/ppermute | solution.py:1154
  102.1 75.7 %all-gather.14.cloned.1.call-start = ((), (), s32[]{:S(2)}) async-start(), calls=%async_computation.8 | async-start | bytes 5570560 | tf_op jit(solution)/shard_map/all_gather | solution.py:1164
  102.1 28.6 %collective-permute-start.7 = (bf16[448,1280]{1,0:T(8,128)(2,1)}, bf16[448,1280]{1,0:T(8,128)(2,1)}, u32[]{:S(2)}, u32[]{:S(2)}) collective-permute-start(bf16[448,1280]{1,0:T(8,128)(2,1)} %bitcast.69), channel_id=1, source_target_pairs={{0,1},{1,0},{2,3},{3,2},{4,5},{5,4},{6,7},{7,6},{8,9},{9,8},{10,11... | collective-permute-start | bytes 3440648 | tf_op jit(solution)/shard_map/ppermute | solution.py:1154
  105.1 5.9 %copy-start.24 = (bf16[640,112]{1,0:T(8,128)(2,1)}, bf16[640,112]{1,0:T(8,128)(2,1)S(1)}, u32[]{:S(2)}) copy-start(bf16[640,112]{1,0:T(8,128)(2,1)S(1)} %pad_maximum_fusion.6.own_shared_in_ref) | copy-start | bytes 430084
  105.2 6.5 %copy-start.25 = (bf16[56,1280]{1,0:T(8,128)(2,1)}, bf16[56,1280]{1,0:T(8,128)(2,1)S(1)}, u32[]{:S(2)}) copy-start(bf16[56,1280]{1,0:T(8,128)(2,1)S(1)} %constant_dynamic-slice_fusion.3.own_shared_out_ref) | copy-start | bytes 430084
  105.2 35.1 %copy-start.6 = (bf16[640,1280]{1,0:T(8,128)(2,1)S(1)}, bf16[640,1280]{1,0:T(8,128)(2,1)}, u32[]{:S(2)}) copy-start(bf16[640,1280]{1,0:T(8,128)(2,1)} %wq_ref.1) | copy-start | bytes 4915204
  111.1 23.0 %collective-permute-start.8 = (bf16[640,112]{1,0:T(8,128)(2,1)S(1)}, bf16[640,112]{1,0:T(8,128)(2,1)S(1)}, u32[]{:S(2)}, u32[]{:S(2)}) collective-permute-start(bf16[640,112]{1,0:T(8,128)(2,1)S(1)} %pad_maximum_fusion.6.own_shared_in_ref), channel_id=1, source_target_pairs={{0,1},{1,0},{2,3},{3,2},{4,5},{5,4},{6,7},{7,6},{8,9},{9,8},{10,11... | collective-permute-start | bytes 430088 | tf_op jit(solution)/shard_map/ppermute | solution.py:1154
  111.7 23.9 %collective-permute-start.9 = (bf16[56,1280]{1,0:T(8,128)(2,1)S(1)}, bf16[56,1280]{1,0:T(8,128)(2,1)S(1)}, u32[]{:S(2)}, u32[]{:S(2)}) collective-permute-start(bf16[56,1280]{1,0:T(8,128)(2,1)S(1)} %constant_dynamic-slice_fusion.3.own_shared_out_ref), channel_id=1, source_target_pairs={{0,1},{1,0},{2,3},{3,2},{4,5},{5,4},{6,7},{7,6},{8,9},{9,8},{10,11... | collective-permute-start | bytes 430088 | tf_op jit(solution)/shard_map/ppermute | solution.py:1154
  134.1 7.9 %copy-start.32 = (bf16[640,112]{1,0:T(8,128)(2,1)}, bf16[640,112]{1,0:T(8,128)(2,1)S(1)}, u32[]{:S(2)}) copy-start(bf16[640,112]{1,0:T(8,128)(2,1)S(1)} %collective-permute-done.8.other_shared_in_ref) | copy-start | bytes 430084
  135.6 6.4 %copy-start.33 = (bf16[56,1280]{1,0:T(8,128)(2,1)}, bf16[56,1280]{1,0:T(8,128)(2,1)S(1)}, u32[]{:S(2)}) copy-start(bf16[56,1280]{1,0:T(8,128)(2,1)S(1)} %collective-permute-done.9.other_shared_out_ref) | copy-start | bytes 430084
  139.5 101.6 %reduce-scatter.2.cloned.1.call-start = ((), (), s32[]{:S(2)}) async-start(), calls=%async_computation.9 | async-start | bytes 11141120 | tf_op jit(solution)/shard_map/reduce_scatter | solution.py:1292
  140.4 34.2 %collective-permute-start.10 = (bf16[640,640]{1,0:T(8,128)(2,1)S(1)}, bf16[640,640]{1,0:T(8,128)(2,1)}, u32[]{:S(2)}, u32[]{:S(2)}) collective-permute-start(bf16[640,640]{1,0:T(8,128)(2,1)S(1)} %constant_dynamic-slice_fusion.2), channel_id=1, source_target_pairs={{0,1},{1,0},{2,3},{3,2},{4,5},{5,4},{6,7},{7,6},{8,9},{9,8},{10,11... | collective-permute-start | bytes 2457608 | tf_op jit(solution)/shard_map/ppermute | solution.py:1154
  185.3 4.4 %copy-start.4 = (bf16[640,1280]{1,0:T(8,128)(2,1)S(1)}, bf16[640,1280]{1,0:T(8,128)(2,1)}, u32[]{:S(2)}) copy-start(bf16[640,1280]{1,0:T(8,128)(2,1)} %wv_ref.1) | copy-start | bytes 4915204
  185.3 4.5 %copy-start.5 = (bf16[640,1280]{1,0:T(8,128)(2,1)S(1)}, bf16[640,1280]{1,0:T(8,128)(2,1)}, u32[]{:S(2)}) copy-start(bf16[640,1280]{1,0:T(8,128)(2,1)} %wk_ref.1) | copy-start | bytes 4915204
  186.6 32.7 %collective-permute-start.11 = (bf16[112,640]{1,0:T(8,128)(2,1)S(1)}, bf16[112,640]{1,0:T(8,128)(2,1)S(1)}, u32[]{:S(2)}, u32[]{:S(2)}) collective-permute-start(bf16[112,640]{1,0:T(8,128)(2,1)S(1)} %fusion.5), channel_id=1, source_target_pairs={{0,1},{1,0},{2,3},{3,2},{4,5},{5,4},{6,7},{7,6},{8,9},{9,8},{10,11... | collective-permute-start | bytes 430088 | tf_op jit(solution)/shard_map/ppermute | solution.py:1154
  189.0 29.2 %collective-permute-start.12 = (bf16[56,1280]{1,0:T(8,128)(2,1)S(1)}, bf16[56,1280]{1,0:T(8,128)(2,1)S(1)}, u32[]{:S(2)}, u32[]{:S(2)}) collective-permute-start(bf16[56,1280]{1,0:T(8,128)(2,1)S(1)} %slice.283), channel_id=1, source_target_pairs={{0,1},{1,0},{2,3},{3,2},{4,5},{5,4},{6,7},{7,6},{8,9},{9,8},{10,11... | collective-permute-start | bytes 430088 | tf_op jit(solution)/shard_map/ppermute | solution.py:1154
  191.2 62.8 %collective-permute-start.13 = (bf16[1280,640]{1,0:T(8,128)(2,1)}, bf16[1280,640]{1,0:T(8,128)(2,1)}, u32[]{:S(2)}, u32[]{:S(2)}) collective-permute-start(bf16[1280,640]{1,0:T(8,128)(2,1)} %pad_maximum_fusion), channel_id=1, source_target_pairs={{0,1},{1,0},{2,3},{3,2},{4,5},{5,4},{6,7},{7,6},{8,9},{9,8},{10,11... | collective-permute-start | bytes 4915208 | tf_op jit(solution)/shard_map/ppermute | solution.py:1154
  219.3 36.0 %collective-permute-start.14 = (bf16[448,1280]{1,0:T(8,128)(2,1)}, bf16[448,1280]{1,0:T(8,128)(2,1)S(1)}, u32[]{:S(2)}, u32[]{:S(2)}) collective-permute-start(bf16[448,1280]{1,0:T(8,128)(2,1)} %get-tuple-element.172), channel_id=1, source_target_pairs={{0,1},{1,0},{2,3},{3,2},{4,5},{5,4},{6,7},{7,6},{8,9},{9,8},{10,11... | collective-permute-start | bytes 3440648 | tf_op jit(solution)/shard_map/ppermute | solution.py:1154
  220.0 10.2 %all-to-all-start.1 = ((f32[16,1,128]{2,1,0:T(1,128)}), f32[16,1,128]{2,1,0:T(1,128)S(1)}, u32[]{:S(2)}, u32[]{:S(2)}) async-start(f32[16,1,128]{2,1,0:T(1,128)} %bitcast.16), calls=%async_computation.2 | async-start | bytes 16384 | tf_op jit(solution)/shard_map/all_to_all | solution.py:1183
  241.7 10.6 %copy-start.11 = (bf16[640,1792]{1,0:T(8,128)(2,1)S(1)}, bf16[640,1792]{1,0:T(8,128)(2,1)}, u32[]{:S(2)}) copy-start(bf16[640,1792]{1,0:T(8,128)(2,1)} %get-tuple-element.173) | copy-start | bytes 6881284
  246.9 20.9 %all-to-all-start.2 = ((bf16[16,128,128]{2,1,0:T(8,128)(2,1)}), bf16[16,128,128]{2,1,0:T(8,128)(2,1)}, u32[]{:S(2)}, u32[]{:S(2)}) async-start(bf16[16,128,128]{2,1,0:T(8,128)(2,1)} %get-tuple-element.164), calls=%async_computation.3 | async-start | bytes 1048576 | tf_op jit(solution)/shard_map/all_to_all | solution.py:1183
  252.0 141.0 %all-gather.20.cloned.1.call-start = ((), (), s32[]{:S(2)}) async-start(), calls=%async_computation.12 | async-start | bytes 4874240 | tf_op jit(solution)/shard_map/all_gather | solution.py:1164
  252.3 15.4 %collective-permute-start.15 = (bf16[160,1792]{1,0:T(8,128)(2,1)S(1)}, bf16[160,1792]{1,0:T(8,128)(2,1)}, u32[]{:S(2)}, u32[]{:S(2)}) collective-permute-start(bf16[160,1792]{1,0:T(8,128)(2,1)S(1)} %slice.218), channel_id=1, source_target_pairs={{0,1},{1,0},{2,3},{3,2},{4,5},{5,4},{6,7},{7,6},{8,9},{9,8},{10,11... | collective-permute-start | bytes 1720328 | tf_op jit(solution)/shard_map/ppermute | solution.py:1154
  255.3 12.4 %copy-start.22 = (bf16[448,1280]{1,0:T(8,128)(2,1)}, bf16[448,1280]{1,0:T(8,128)(2,1)S(1)}, u32[]{:S(2)}) copy-start(bf16[448,1280]{1,0:T(8,128)(2,1)S(1)} %collective-permute-done.14) | copy-start | bytes 3440644
  267.8 25.8 %all-to-all-start.3 = ((bf16[16,144,128]{2,1,0:T(8,128)(2,1)}), bf16[16,144,128]{2,1,0:T(8,128)(2,1)S(1)}, u32[]{:S(2)}, u32[]{:S(2)}) async-start(bf16[16,144,128]{2,1,0:T(8,128)(2,1)} %get-tuple-element.181), calls=%async_computation.4 | async-start | bytes 1179648 | tf_op jit(solution)/shard_map/all_to_all | solution.py:1345
  274.4 19.1 %collective-permute-start.16 = (bf16[200,1792]{1,0:T(8,128)(2,1)}, bf16[200,1792]{1,0:T(8,128)(2,1)S(1)}, u32[]{:S(2)}, u32[]{:S(2)}) collective-permute-start(bf16[200,1792]{1,0:T(8,128)(2,1)} %slice.219), channel_id=1, source_target_pairs={{0,1},{1,0},{2,3},{3,2},{4,5},{5,4},{6,7},{7,6},{8,9},{9,8},{10,11... | collective-permute-start | bytes 2150408 | tf_op jit(solution)/shard_map/ppermute | solution.py:1154
  293.6 46.2 %all-to-all-start.4 = ((bf16[16,128,384]{2,1,0:T(8,128)(2,1)}), bf16[16,128,384]{2,1,0:T(8,128)(2,1)S(1)}, u32[]{:S(2)}, u32[]{:S(2)}) async-start(bf16[16,128,384]{2,1,0:T(8,128)(2,1)} %bitcast.55), calls=%async_computation.5 | async-start | bytes 3145728 | tf_op jit(solution)/shard_map/all_to_all | solution.py:1183
  299.6 106.5 %all-gather.18.cloned.1.call-start = ((), (), s32[]{:S(2)}) async-start(), calls=%async_computation.11 | async-start | bytes 11419648 | tf_op jit(solution)/shard_map/all_gather | solution.py:1164
  307.5 7.7 %collective-permute-start.18 = (bf16[656,128]{1,0:T(8,128)(2,1)S(1)}, bf16[656,128]{1,0:T(8,128)(2,1)S(1)}, u32[]{:S(2)}, u32[]{:S(2)}) collective-permute-start(bf16[656,128]{1,0:T(8,128)(2,1)S(1)} %pad_maximum_fusion.5), channel_id=1, source_target_pairs={{0,1},{1,0},{2,3},{3,2},{4,5},{5,4},{6,7},{7,6},{8,9},{9,8},{10,11... | collective-permute-start | bytes 503816 | tf_op jit(solution)/shard_map/ppermute | solution.py:1154
  309.1 18.8 %copy-start.16 = (bf16[640,128]{1,0:T(8,128)(2,1)S(1)}, bf16[640,128]{1,0:T(8,128)(2,1)}, u32[]{:S(2)}) copy-start(bf16[640,128]{1,0:T(8,128)(2,1)} %copy-done.15) | copy-start | bytes 491524
  309.1 18.8 %copy-start.18 = (bf16[640,128]{1,0:T(8,128)(2,1)S(1)}, bf16[640,128]{1,0:T(8,128)(2,1)}, u32[]{:S(2)}) copy-start(bf16[640,128]{1,0:T(8,128)(2,1)} %copy-done.17) | copy-start | bytes 491524
  309.1 18.8 %copy-start.20 = (bf16[640,128]{1,0:T(8,128)(2,1)S(1)}, bf16[640,128]{1,0:T(8,128)(2,1)}, u32[]{:S(2)}) copy-start(bf16[640,128]{1,0:T(8,128)(2,1)} %copy-done.19) | copy-start | bytes 491524
  314.5 13.7 %copy-start.13 = (f32[1280,128]{1,0:T(8,128)S(1)}, f32[1280,128]{1,0:T(8,128)}, u32[]{:S(2)}) copy-start(f32[1280,128]{1,0:T(8,128)} %turned_product.2) | copy-start | bytes 1966084
  314.6 13.3 %collective-permute-start.17 = (bf16[640,384]{1,0:T(8,128)(2,1)S(1)}, bf16[640,384]{1,0:T(8,128)(2,1)S(1)}, u32[]{:S(2)}, u32[]{:S(2)}) collective-permute-start(bf16[640,384]{1,0:T(8,128)(2,1)S(1)} %dynamic-slice_convert_fusion), channel_id=1, source_target_pairs={{0,1},{1,0},{2,3},{3,2},{4,5},{5,4},{6,7},{7,6},{8,9},{9,8},{10,11... | collective-permute-start | bytes 1474568 | tf_op jit(solution)/shard_map/ppermute | solution.py:1154
  329.4 13.8 %copy-start.23 = (bf16[448,1280]{1,0:T(8,128)(2,1)S(1)}, bf16[448,1280]{1,0:T(8,128)(2,1)}, u32[]{:S(2)}) copy-start(bf16[448,1280]{1,0:T(8,128)(2,1)} %copy-done.22) | copy-start | bytes 3440644
  339.8 6.6 %copy-start.3 = (bf16[16,128,384]{2,1,0:T(8,128)(2,1)}, bf16[16,128,384]{2,1,0:T(8,128)(2,1)S(1)}, u32[]{:S(2)}) copy-start(bf16[16,128,384]{2,1,0:T(8,128)(2,1)S(1)} %all-to-all-done.4.got_ref) | copy-start | bytes 4718596
  340.5 42.9 %collective-permute-start.19 = (bf16[640,640]{1,0:T(8,128)(2,1)}, bf16[640,640]{1,0:T(8,128)(2,1)}, u32[]{:S(2)}, u32[]{:S(2)}) collective-permute-start(bf16[640,640]{1,0:T(8,128)(2,1)} %collective-permute-done.10.near_q_ref), channel_id=1, source_target_pairs={{0,2},{2,0},{4,6},{6,4},{8,10},{10,8},{12,14},{14,12},{16,18},{18,... | collective-permute-start | bytes 2457608 | tf_op jit(solution)/shard_map/ppermute | solution.py:1390
  342.9 40.5 %collective-permute-start.20 = (bf16[1280,640]{1,0:T(8,128)(2,1)}, bf16[1280,640]{1,0:T(8,128)(2,1)}, u32[]{:S(2)}, u32[]{:S(2)}) collective-permute-start(bf16[1280,640]{1,0:T(8,128)(2,1)} %collective-permute-done.13.near_rest_ref), channel_id=1, source_target_pairs={{0,2},{2,0},{4,6},{6,4},{8,10},{10,8},{12,14},{14,12},{16,18},{18,... | collective-permute-start | bytes 4915208 | tf_op jit(solution)/shard_map/ppermute | solution.py:1390
  346.4 32.5 %collective-permute-start.22 = (bf16[280,1792]{1,0:T(8,128)(2,1)}, bf16[280,1792]{1,0:T(8,128)(2,1)}, u32[]{:S(2)}, u32[]{:S(2)}) collective-permute-start(bf16[280,1792]{1,0:T(8,128)(2,1)} %slice.235), channel_id=1, source_target_pairs={{0,1},{1,0},{2,3},{3,2},{4,5},{5,4},{6,7},{7,6},{8,9},{9,8},{10,11... | collective-permute-start | bytes 3010568 | tf_op jit(solution)/shard_map/ppermute | solution.py:1154
  355.5 22.5 %copy-start.9 = (f32[1280,128]{1,0:T(8,128)S(1)}, f32[1280,128]{1,0:T(8,128)}, u32[]{:S(2)}) copy-start(f32[1280,128]{1,0:T(8,128)} %turned_product.3) | copy-start | bytes 1966084
  356.7 21.3 %collective-permute-start.21 = (f32[640,16]{1,0:T(8,128)S(1)}, f32[640,16]{1,0:T(8,128)S(1)}, u32[]{:S(2)}, u32[]{:S(2)}) collective-permute-start(f32[640,16]{1,0:T(8,128)S(1)} %slice.252), channel_id=1, source_target_pairs={{0,1},{1,0},{2,3},{3,2},{4,5},{5,4},{6,7},{7,6},{8,9},{9,8},{10,11... | collective-permute-start | bytes 122888 | tf_op jit(solution)/shard_map/ppermute | solution.py:1154
  406.1 13.7 %copy-start.1 = (bf16[448,1280]{1,0:T(8,128)(2,1)S(1)}, bf16[448,1280]{1,0:T(8,128)(2,1)}, u32[]{:S(2)}) copy-start(bf16[448,1280]{1,0:T(8,128)(2,1)} %param.25) | copy-start | bytes 3440644
  (5 other events, 5.5 us)
Sparse Core Ops, SparseCore 0:
  9.7 39.6 all-gather.15
  51.6 48.4 all-gather.9
  102.2 37.1 all-gather.11
  141.5 36.2 all-gather.13
  179.9 61.0 reduce-scatter.1
  267.9 66.2 all-gather.19
  339.9 66.1 all-gather.17

commit v2 on v1

--- a/solution.py
+++ b/solution.py
@@ -579,6 +579,8 @@
     output_ref,
     norm_ref,
     norm2_ref,
+    line_ref,
+    line2_ref,
 ):
     for h in range(HEADS):
         at = slice(h * HEAD_DIM, (h + 1) * HEAD_DIM)
@@ -593,11 +595,11 @@
         pair, sums, (((1,), (1,)), ((), ())), precision=exact, preferred_element_type=f32
     )
     block = rest_ref.shape[1]
-    for i in range(norm_ref.shape[1] // block):
+    for i in range(line_ref.shape[1] // block):
 
         @pl.when(pl.program_id(0) == i)
         def _(at=slice(i * block, (i + 1) * block)):
-            norm_ref[:, at] = row[0:1] / gain_ref[:, at]
+            line_ref[:, at] = row[0:1] / gain_ref[:, at]
 
     spans = rest_ref.shape[0]
 
@@ -606,11 +608,18 @@
         for i in range(spans // 2):
             low, high = ring_position(i, spans), ring_position(spans // 2 + i, spans)
             rows = gain_rows_ref[jnp.where(side_ref[0] == 0, low, high)].astype(f32)
-            norm2_ref[:, i * cut : (i + 1) * cut] = (rows[0:1] + rows[1:2])[:, :cut]
+            line2_ref[:, i * cut : (i + 1) * cut] = (rows[0:1] + rows[1:2])[:, :cut]
 
     for c in range(spans):
         piece = rest_ref[ring_position(c, spans), :, :cut].astype(f32)
         output_ref[:, c * cut : (c + 1) * cut] = piece
+
+    @pl.when(pl.program_id(0) == pl.num_programs(0) - 1)
+    def _():
+        for i in range(norm_ref.shape[0]):
+            at = slice(i * HEAD_DIM, (i + 1) * HEAD_DIM)
+            norm_ref[i : i + 1, :] = line_ref[:, at]
+            norm2_ref[i : i + 1, :] = line2_ref[:, at]
 
 
 def ring_position(index, spans):
@@ -638,9 +647,10 @@
             pl.BlockSpec((spans, 16, HEAD_DIM), lambda r: (0, half // 16, 3)),
             line,
         ],
-        out_specs=[part] * 4 + [line] * 2,
+        out_specs=[part] * 4 + [pl.BlockSpec((half // HEAD_DIM, HEAD_DIM), lambda r: (0, 0))] * 2,
         out_shape=[jax.ShapeDtypeStruct((half, width), f32)] * 4
-        + [jax.ShapeDtypeStruct((1, half), f32)] * 2,
+        + [jax.ShapeDtypeStruct((half // HEAD_DIM, HEAD_DIM), f32)] * 2,
+        scratch_shapes=[pltpu.VMEM((1, half), f32)] * 2,
         name="place_heads",
     )(side.reshape(1), got, got, got, gain.reshape(1, half))
 

time: 428 us -> 426 us (level)
  no operation moved by 1% of the time
where the time goes in v2:
time: 426 us; the launch traced here: 424 us
  Pallas kernels  155 us (36%)
  waiting for transfers between devices  153 us (36%)
  starting transfers between devices  50.9 us (12%)
  local copies, waits for them, and re-layouts  22.9 us (5%)
  other arithmetic  21.7 us (5%)
  between operations  14.9 us (3%)
  matrix products  5.37 us (1%)
    ppermute x20, waiting for transfers between devices, across(): return lax.ppermute(value, 'fsdp', [(0, 1), (1, 0)])  102 us
    pallas_call x1, Pallas kernels, run_experts(): pl.pallas_call(functools.partial(experts_kernel, capacity, tokens, expert...  32.6 us
    ppermute x20, starting transfers between devices, across(): return lax.ppermute(value, 'fsdp', [(0, 1), (1, 0)])  25.2 us
    pallas_call x2, Pallas kernels, slot_grads(): pl.pallas_call(slot_grads_kernel, grid=(wide // (2 * HEAD_DIM),), in_spec...  23.6 us
    all_to_all x4, waiting for transfers between devices, swapped(): return lax.all_to_all(value, 'ctx', split_axis=0, concat_axis=0, tiled=True)  21.7 us
    all_to_all x4, starting transfers between devices, swapped(): return lax.all_to_all(value, 'ctx', split_axis=0, concat_axis=0, tiled=True)  18.4 us
    pallas_call x1, Pallas kernels, attend_back(): pl.pallas_call(functools.partial(attend_back_kernel, ring), grid=(length...  17.6 us
    all_gather x6, waiting for transfers between devices, everyone(): lax.all_gather(value, 'ctx', axis=0, tiled=True, axis_index_groups=groups)  17.5 us
  transfers between devices with their start and end apart: 35, of which 18 were waited for; matrix products, arithmetic and copies ran while one was open for 11% of the time, Pallas kernels for 34%

profile of v2, /device:TPU:0, one launch (start us, length us, event | category | flops | bytes accessed | tf_op | source)
XLA Modules:
  0.0 424.3 jit_solution(14654496186048069447)
XLA Ops:
  9.1 1.1 constant_dynamic-slice_fusion.7
  10.9 3.0 collective-permute-start
  15.0 2.0 collective-permute-start.1
  18.6 1.6 multiply_add_fusion
  23.9 19.4 %collective-permute-done.1 = bf16[18,640]{1,0:T(8,128)(2,1)S(1)} collective-permute-done((bf16[18,640]{1,0:T(8,128)(2,1)S(1)}, bf16[18,640]{1,0:T(8,128)(2,1)S(1)}, u32[]{:S(2)}, u32[]{:S(2)}) %collective-permute-start.1) | collective-permute-done | bytes 23072 | tf_op jit(solution)/shard_map/ppermute | solution.py:1164
  43.9 5.5 %all-gather.16.cloned.1.call-done = bf16[1,2048,1280]{2,1,0:T(8,128)(2,1)} async-done(((bf16[1,128,1280]{2,1,0:T(8,128)(2,1)}), bf16[1,2048,1280]{2,1,0:T(8,128)(2,1)}) %all-gather.16.cloned.1.call-update) | async-done | bytes 5242896 | tf_op jit(solution)/shard_map/all_gather | solution.py:1174
  49.7 1.6 collective-permute-start.4
  51.7 8.0 %project.1 = (bf16[2048,1280]{1,0:T(8,128)(2,1)}, bf16[2048,128]{1,0:T(8,128)(2,1)}, bf16[2048,128]{1,0:T(8,128)(2,1)}, bf16[2048,128]{1,0:T(8,128)(2,1)}) custom-call(s32[1]{0:T(128)} %bitcast.side_ref, bf16[2048,1280]{1,0:T(8,128)(2,1)} %bitcast.46, f32[1,1280]{1,0:T(1,128)} %get-tuple-element.113.gain_ref, bf16[640,384]{1,0:T(8,128)(2,1)} %copy-done.14, ...), custom_call_target="tpu_custom_call" | custom-call | flops 2013265920 | bytes 10485760 | tf_op jit(solution)/shard_map/project/pallas_call | solution.py:289
  59.7 9.5 %attend.1 = (f32[2048,128]{1,0:T(8,128)}, f32[1,2048]{1,0:T(1,128)}, bf16[2048,128]{1,0:T(8,128)(2,1)}) custom-call(bf16[2048,128]{1,0:T(8,128)(2,1)} %get-tuple-element.117.q_ref, bf16[2048,128]{1,0:T(8,128)(2,1)} %get-tuple-element.118.k_ref, bf16[2048,128]{1,0:T(8,128)(2,1)} %get-tuple-element.119.v_ref), custom_call_target="tpu_custom_call" | custom-call | flops 1073741824 | bytes 3145728 | tf_op jit(solution)/shard_map/attend/pallas_call | solution.py:134
  69.3 3.6 all-to-all-start
  72.9 1.6 collective-permute-start.6
  76.5 13.9 %collective-permute-done.5.middle_in_ref = bf16[320,1792]{1,0:T(8,128)(2,1)} collective-permute-done((bf16[320,1792]{1,0:T(8,128)(2,1)}, bf16[320,1792]{1,0:T(8,128)(2,1)}, u32[]{:S(2)}, u32[]{:S(2)}) %collective-permute-start.5) | collective-permute-done | bytes 1146912 | tf_op jit(solution)/shard_map/ppermute | solution.py:1164
  90.4 5.4 %all-to-all-done.got_ref = bf16[16,128,128]{2,1,0:T(8,128)(2,1)S(1)} async-done(((bf16[16,128,128]{2,1,0:T(8,128)(2,1)}), bf16[16,128,128]{2,1,0:T(8,128)(2,1)S(1)}, u32[]{:S(2)}, u32[]{:S(2)}) %all-to-all-start) | async-done | bytes 524320 | tf_op jit(solution)/shard_map/all_to_all | solution.py:1193
  96.6 4.8 %mix.1 = (f32[128,1280]{1,0:T(8,128)}, bf16[128,1408]{1,0:T(8,128)(2,1)}, f32[128,1]{1,0:T(8,128)}, f32[128,128]{1,0:T(8,128)}, bf16[128,1280]{1,0:T(8,128)(2,1)}) custom-call(s32[2]{0:T(128)} %pad_add_fusion.spot_ref, bf16[16,128,128]{2,1,0:T(8,128)(2,1)} %copy-done.12, bf16[640,1280]{1,0:T(8,128)(2,1)} %own_ref.3, bf16[640,640]{1,0:T(8,128)(2,1)} %copy-done.7, ...), custom_call_target="tpu_custom_call" | custom-call | tf_op jit(solution)/shard_map/mix/pallas_call | solution.py:392
  102.1 1.7 collective-permute-start.7
  103.8 1.2 constant_dynamic-slice_fusion.5
  105.2 5.8 %pick_slots.1.grad_slots_ref = bf16[896,1280]{1,0:T(8,128)(2,1)} custom-call(s32[1]{0:T(128)} %bitcast.2.here_ref, bf16[2048,1408]{1,0:T(8,128)(2,1)} %all-gather.10.cloned.1.call-done.g_ref), custom_call_target="tpu_custom_call" | custom-call | flops 1174405120 | bytes 8650752 | tf_op jit(solution)/shard_map/pick_slots/pallas_call | solution.py:747
  111.7 1.4 collective-permute-start.9
  113.1 17.6 %collective-permute-done.7.other_down_ref = bf16[448,1280]{1,0:T(8,128)(2,1)} collective-permute-done((bf16[448,1280]{1,0:T(8,128)(2,1)}, bf16[448,1280]{1,0:T(8,128)(2,1)}, u32[]{:S(2)}, u32[]{:S(2)}) %collective-permute-start.7) | collective-permute-done | bytes 1146912 | tf_op jit(solution)/shard_map/ppermute | solution.py:1164
  130.7 3.4 collective-permute-done.8.other_shared_in_ref
  134.1 1.5 collective-permute-done.9.other_shared_out_ref
  135.6 3.8 all-gather.12.cloned.1.call-done.normed_ref.left_ref
  140.4 1.6 collective-permute-start.10
  142.1 32.6 %experts.1 = (bf16[896,1280]{1,0:T(8,128)(2,1)}, bf16[896,896]{1,0:T(8,128)(2,1)}, bf16[896,1280]{1,0:T(8,128)(2,1)}, bf16[896,1792]{1,0:T(8,128)(2,1)}, bf16[20...) custom-call(s32[3]{0:T(128)} %pad_add_fusion.1.here_ref, ...), custom_call_target="tpu_custom_call" | custom-call | flops 20000000000 | bytes 40000000 | tf_op jit(solution)/shard_map/experts/pallas_call | solution.py:935
  174.7 3.2 all-gather.14.cloned.1.call-done.left_ref
  177.9 7.5 %shared_products.1 = (f32[256,1280]{1,0:T(8,128)}, f32[128,1280]{1,0:T(8,128)}) custom-call(bf16[2048,256]{1,0:T(8,128)(2,1)} %get-tuple-element.151.grad_ref, bf16[2048,1408]{1,0:T(8,128)(2,1)} %all-gather.12.cloned.1.call-done.normed_ref.left_ref, bf16[2048,128]{1,0:T(8,128)(2,1)} %get-tuple-element.152.hidden_ref, ...), custom_call_target="tpu_custom_call" | custom-call | flops 2013265920 | bytes 15728640 | tf_op jit(solution)/shard_map/shared_products/pallas_call | solution.py:1055
  185.4 1.2 fusion.24
  186.7 1.3 collective-permute-start.11
  190.0 1.3 pad_maximum_fusion
  191.3 1.2 collective-permute-start.13
  193.3 1.2 concatenate.65
  194.5 14.4 %slot_grads.2 = (f32[640,1792]{1,0:T(8,128)}, bf16[640,1792]{1,0:T(8,128)(2,1)}) custom-call(s32[1]{0:T(128)} %bitcast.side_ref, bf16[896,1280]{1,0:T(8,128)(2,1)} %get-tuple-element.148.left_ref, bf16[896,1792]{1,0:T(8,128)(2,1)} %get-tuple-element.149.right_ref), custom_call_target="tpu_custom_call" | custom-call | flops 4110417920 | bytes 12386304 | tf_op jit(solution)/shard_map/slot_grads/pallas_call | solution.py:1012
  208.9 9.2 %slot_grads.3 = (f32[448,1280]{1,0:T(8,128)}, bf16[448,1280]{1,0:T(8,128)(2,1)}) custom-call(s32[1]{0:T(128)} %bitcast.side_ref, bf16[896,896]{1,0:T(8,128)(2,1)} %get-tuple-element.169.left_ref, bf16[896,1280]{1,0:T(8,128)(2,1)} %get-tuple-element.170.right_ref), custom_call_target="tpu_custom_call" | custom-call | flops 2055208960 | bytes 7340032 | tf_op jit(solution)/shard_map/slot_grads/pallas_call | solution.py:1012
  220.1 3.5 all-to-all-start.1
  224.4 5.7 %all-to-all-done.1 = f32[16,1,128]{2,1,0:T(1,128)S(1)} async-done(((f32[16,1,128]{2,1,0:T(1,128)}), f32[16,1,128]{2,1,0:T(1,128)S(1)}, u32[]{:S(2)}, u32[]{:S(2)}) %all-to-all-start.1) | async-done | bytes 8224 | tf_op jit(solution)/shard_map/all_to_all | solution.py:1193
  230.2 10.8 %reduce-scatter.2.cloned.1.call-done.sums_ref = bf16[128,2560]{1,0:T(8,128)(2,1)} async-done(((bf16[2048,2560]{1,0:T(8,128)(2,1)}), bf16[128,2560]{1,0:T(8,128)(2,1)}) %reduce-scatter.2.cloned.1.call-update) | async-done | bytes 655376 | tf_op jit(solution)/shard_map/reduce_scatter | solution.py:1302
  241.7 5.2 %mix_back.1 = (bf16[16,128,128]{2,1,0:T(8,128)(2,1)}, bf16[16,144,128]{2,1,0:T(8,128)(2,1)}, f32[128,1280]{1,0:T(8,128)}, bf16[128,1280]{1,0:T(8,128)(2,1)}) custom-call(s32[2]{0:T(128)} %pad_add_fusion.spot_ref, bf16[128,2560]{1,0:T(8,128)(2,1)} %reduce-scatter.2.cloned.1.call-done.sums_ref, f32[128,128]{1,0:T(8,128)} %get-tuple-element.158.gates_ref, ...), custom_call_target="tpu_custom_call" | custom-call | tf_op jit(solution)/shard_map/mix_back/pallas_call | solution.py:479
  246.8 5.2 %all-to-all-start.2 = ((bf16[16,128,128]{2,1,0:T(8,128)(2,1)}), bf16[16,128,128]{2,1,0:T(8,128)(2,1)}, u32[]{:S(2)}, u32[]{:S(2)}) async-start(bf16[16,128,128]{2,1,0:T(8,128)(2,1)} %get-tuple-element.164), calls=%async_computation.3 | async-start | bytes 1048576 | tf_op jit(solution)/shard_map/all_to_all | solution.py:1193
  252.4 1.5 collective-permute-start.15
  253.9 1.5 collective-permute-done.14
  255.4 12.4 %collective-permute-done.15 = bf16[160,1792]{1,0:T(8,128)(2,1)} collective-permute-done((bf16[160,1792]{1,0:T(8,128)(2,1)S(1)}, bf16[160,1792]{1,0:T(8,128)(2,1)}, u32[]{:S(2)}, u32[]{:S(2)}) %collective-permute-start.15) | collective-permute-done | bytes 573472 | tf_op jit(solution)/shard_map/ppermute | solution.py:1164
  267.9 5.7 %all-to-all-start.3 = ((bf16[16,144,128]{2,1,0:T(8,128)(2,1)}), bf16[16,144,128]{2,1,0:T(8,128)(2,1)S(1)}, u32[]{:S(2)}, u32[]{:S(2)}) async-start(bf16[16,144,128]{2,1,0:T(8,128)(2,1)} %get-tuple-element.181), calls=%async_computation.4 | async-start | bytes 1179648 | tf_op jit(solution)/shard_map/all_to_all | solution.py:1355
  274.5 1.4 collective-permute-start.16
  275.9 17.6 %attend_back.1 = (bf16[2048,384]{1,0:T(8,128)(2,1)}, bf16[2048,384]{1,0:T(8,128)(2,1)}) custom-call(bf16[2048,128]{1,0:T(8,128)(2,1)} %get-tuple-element.117.q_ref, bf16[2048,128]{1,0:T(8,128)(2,1)} %get-tuple-element.118.k_ref, bf16[2048,128]{1,0:T(8,128)(2,1)} %get-tuple-element.119.v_ref, bf16[2048,128]{1,0:T(8,128)(2,1)} %bitcast.20.grad_ref, ...), custom_call_target="tpu_custom_call" | custom-call | flops 2684354560 | bytes 5242880 | tf_op jit(solution)/shard_map/attend_back/pallas_call | solution.py:243
  293.5 6.1 %all-to-all-start.4 = ((bf16[16,128,384]{2,1,0:T(8,128)(2,1)}), bf16[16,128,384]{2,1,0:T(8,128)(2,1)S(1)}, u32[]{:S(2)}, u32[]{:S(2)}) async-start(bf16[16,128,384]{2,1,0:T(8,128)(2,1)} %bitcast.57), calls=%async_computation.5 | async-start | bytes 3145728 | tf_op jit(solution)/shard_map/all_to_all | solution.py:1193
  300.6 5.9 %turned_product.2 = f32[1280,128]{1,0:T(8,128)} custom-call(s32[1]{0:T(128)} %bitcast.side_ref, bf16[2048,1280]{1,0:T(8,128)(2,1)} %all-gather.14.cloned.1.call-done.left_ref, bf16[2048,128]{1,0:T(8,128)(2,1)} %bitcast.47), custom_call_target="tpu_custom_call" | custom-call | flops 671088640 | bytes 5242880 | tf_op jit(solution)/shard_map/turned_product/pallas_call | solution.py:1098
  307.6 1.5 collective-permute-start.18
  309.0 5.4 %fusion.27 = f32[1280,384]{1,0:T(8,128)S(1)} fusion(bf16[2048,1280]{1,0:T(8,128)(2,1)} %get-tuple-element.163, bf16[2048,384]{1,0:T(8,128)(2,1)} %get-tuple-element.182), kind=kOutput, calls=%fused_computation.97 | convolution fusion | flops 2013265920 | bytes 8781824 | tf_op jit(solution)/shard_map/dot_general | solution.py:36
  315.3 12.5 %collective-permute-done.17 = bf16[640,384]{1,0:T(8,128)(2,1)S(1)} collective-permute-done((bf16[640,384]{1,0:T(8,128)(2,1)S(1)}, bf16[640,384]{1,0:T(8,128)(2,1)S(1)}, u32[]{:S(2)}, u32[]{:S(2)}) %collective-permute-start.17) | collective-permute-done | bytes 491552 | tf_op jit(solution)/shard_map/ppermute | solution.py:1164
  329.3 10.6 %all-to-all-done.4.got_ref = bf16[16,128,384]{2,1,0:T(8,128)(2,1)S(1)} async-done(((bf16[16,128,384]{2,1,0:T(8,128)(2,1)}), bf16[16,128,384]{2,1,0:T(8,128)(2,1)S(1)}, u32[]{:S(2)}, u32[]{:S(2)}) %all-to-all-start.4) | async-done | bytes 1572896 | tf_op jit(solution)/shard_map/all_to_all | solution.py:1193
  340.7 2.2 slice.235
  343.3 3.2 add_bitcast_fusion
  346.5 1.4 collective-permute-start.22
  347.9 1.5 convert_add_fusion.1
  349.4 6.0 %turned_product.3 = f32[1280,128]{1,0:T(8,128)} custom-call(s32[1]{0:T(128)} %bitcast.side_ref, bf16[2048,1408]{1,0:T(8,128)(2,1)} %all-gather.12.cloned.1.call-done.normed_ref.left_ref, bf16[2048,128]{1,0:T(8,128)(2,1)} %bitcast.48), custom_call_target="tpu_custom_call" | custom-call | flops 671088640 | bytes 5242880 | tf_op jit(solution)/shard_map/turned_product/pallas_call | solution.py:1098
  355.5 1.2 slice.252
  357.1 1.5 convert_add_fusion.2
  358.7 19.4 %collective-permute-done.21 = f32[640,16]{1,0:T(8,128)S(1)} collective-permute-done((f32[640,16]{1,0:T(8,128)S(1)}, f32[640,16]{1,0:T(8,128)S(1)}, u32[]{:S(2)}, u32[]{:S(2)}) %collective-permute-start.21) | collective-permute-done | bytes 40992 | tf_op jit(solution)/shard_map/ppermute | solution.py:1164
  379.0 2.1 convert_add_fusion
  381.1 2.4 maximum_bitcast_fusion
  383.5 9.5 %inputs_back.1 = f32[128,1280]{1,0:T(8,128)} custom-call(s32[1]{0:T(128)} %bitcast.side_ref, s32[1]{0:T(128)} %bitcast.1.core_ref, bf16[16,128,384]{2,1,0:T(8,128)(2,1)} %copy-done.3, bf16[640,1280]{1,0:T(8,128)(2,1)} %wq_ref.1, bf16[640,1280]{1,0:T(8,128)(2,1)} %wk_ref.1, bf16[640,1280]{1,0:T(8,128)(2,1)} %wv_ref.1, ...), custom_call_target="tpu_custom_call" | custom-call | tf_op jit(solution)/shard_map/inputs_back/pallas_call | solution.py:554
  393.0 8.0 %place_shared.1 = (f32[640,1792]{1,0:T(8,128)}, f32[448,1280]{1,0:T(8,128)}) custom-call(s32[1]{0:T(128)} %bitcast.side_ref, bf16[16,224,640]{2,1,0:T(8,128)(2,1)} %bitcast.49), custom_call_target="tpu_custom_call" | custom-call | tf_op jit(solution)/shard_map/place_shared/pallas_call | solution.py:689
  401.0 5.0 %all-gather.18.cloned.1.call-done = bf16[10496,512]{1,0:T(8,128)(2,1)} async-done(((bf16[656,512]{1,0:T(8,128)(2,1)}), bf16[10496,512]{1,0:T(8,128)(2,1)}) %all-gather.18.cloned.1.call-update) | async-done | bytes 10747920 | tf_op jit(solution)/shard_map/all_gather | solution.py:1174
  406.0 11.4 %place_heads.1 = (f32[640,1280]{1,0:T(8,128)}, f32[640,1280]{1,0:T(8,128)}, f32[640,1280]{1,0:T(8,128)}, f32[640,1280]{1,0:T(8,128)}, f32[5,128]{1,0:T(8,128)}, /*index=5*/f32[5,128]{1,0:T(8,128)}) custom-call(s32[1]{0:T(128)} %bitcast.side_ref, bf16[16,656,512]{2,1,0:T(8,128)(2,1)} %bitcast.43, bf16[16,656,512]{2,1,0:T(8,128)(2,1)} %bitcast.44, ...), custom_call_target="tpu_custom_call" | custom-call | tf_op jit(solution)/shard_map/place_heads/pallas_call | solution.py:640
  (187 shorter events, 29.7 us)
Async XLA Ops:
  7.2 98.0 %copy-start = (bf16[448,1280]{1,0:T(8,128)(2,1)S(1)}, bf16[448,1280]{1,0:T(8,128)(2,1)}, u32[]{:S(2)}) copy-start(bf16[448,1280]{1,0:T(8,128)(2,1)} %param.25) | copy-start | bytes 3440644
  7.2 6.7 %copy-start.2 = (bf16[640,1280]{1,0:T(8,128)(2,1)S(1)}, bf16[640,1280]{1,0:T(8,128)(2,1)}, u32[]{:S(2)}) copy-start(bf16[640,1280]{1,0:T(8,128)(2,1)} %own_ref.3) | copy-start | bytes 4915204
  7.2 7.7 %copy-start.27 = (bf16[640]{0:T(1024)(128)(2,1)S(1)}, bf16[640]{0:T(1024)(128)(2,1)}, u32[]{:S(2)}) copy-start(bf16[640]{0:T(1024)(128)(2,1)} %param.17) | copy-start | bytes 3844
  7.2 7.7 %copy-start.30 = (bf16[640]{0:T(1024)(128)(2,1)S(1)}, bf16[640]{0:T(1024)(128)(2,1)}, u32[]{:S(2)}) copy-start(bf16[640]{0:T(1024)(128)(2,1)} %param.22) | copy-start | bytes 3844
  7.2 7.7 %copy-start.26 = (bf16[640,16]{0,1:T(8,128)(2,1)S(1)}, bf16[640,16]{0,1:T(8,128)(2,1)}, u32[]{:S(2)}) copy-start(bf16[640,16]{0,1:T(8,128)(2,1)} %param.23) | copy-start | bytes 61444
  7.2 42.2 %all-gather.16.cloned.1.call-start = ((), (), s32[]{:S(2)}) async-start(), calls=%async_computation.10 | async-start | bytes 5570560 | tf_op jit(solution)/shard_map/all_gather | solution.py:1174
  8.0 9.1 %copy-start.31 = (f32[16]{0:T(128)S(1)}, f32[16]{0:T(128)}, u32[]{:S(2)}) copy-start(f32[16]{0:T(128)} %constant.125) | copy-start | bytes 196
  8.0 94.1 %all-gather.10.cloned.1.call-start = ((), (), s32[]{:S(2)}) async-start(), calls=%async_computation.6 | async-start | bytes 6127616 | tf_op jit(solution)/shard_map/all_gather | solution.py:1174
  9.0 8.4 %copy-start.28 = (s32[1,128,7]{1,0,2:T(1,128)S(1)}, s32[1,128,7]{1,0,2:T(1,128)}, u32[]{:S(2)}) copy-start(s32[1,128,7]{1,0,2:T(1,128)} %param.28) | copy-start | bytes 10756
  9.0 8.5 %copy-start.29 = (s32[1,1,896]{2,1,0:T(1,128)S(1)}, s32[1,1,896]{2,1,0:T(1,128)}, u32[]{:S(2)}) copy-start(s32[1,1,896]{2,1,0:T(1,128)} %param.29) | copy-start | bytes 10756
  10.9 9.3 %copy-start.14 = (bf16[640,384]{1,0:T(8,128)(2,1)}, bf16[640,384]{1,0:T(8,128)(2,1)S(1)}, u32[]{:S(2)}) copy-start(bf16[640,384]{1,0:T(8,128)(2,1)S(1)} %pad_maximum_fusion.2.own_ref) | copy-start | bytes 1474564
  10.9 33.0 %collective-permute-start = (bf16[640,384]{1,0:T(8,128)(2,1)S(1)}, bf16[640,384]{1,0:T(8,128)(2,1)}, u32[]{:S(2)}, u32[]{:S(2)}) collective-permute-start(bf16[640,384]{1,0:T(8,128)(2,1)S(1)} %pad_maximum_fusion.2.own_ref), channel_id=1, source_target_pairs={{0,1},{1,0},{2,3},{3,2},{4,5},{5,4},{6,7},{7,6},{8,9},{9,8},{10,11... | collective-permute-start | bytes 1474568 | tf_op jit(solution)/shard_map/ppermute | solution.py:1164
  14.8 29.1 %collective-permute-start.2 = (bf16[640,640]{1,0:T(8,128)(2,1)}, bf16[640,640]{1,0:T(8,128)(2,1)S(1)}, u32[]{:S(2)}, u32[]{:S(2)}) collective-permute-start(bf16[640,640]{1,0:T(8,128)(2,1)} %constant_dynamic-slice_fusion.6), channel_id=1, source_target_pairs={{0,1},{1,0},{2,3},{3,2},{4,5},{5,4},{6,7},{7,6},{8,9},{9,8},{10,11... | collective-permute-start | bytes 2457608 | tf_op jit(solution)/shard_map/ppermute | solution.py:1164
  15.0 28.3 %collective-permute-start.1 = (bf16[18,640]{1,0:T(8,128)(2,1)S(1)}, bf16[18,640]{1,0:T(8,128)(2,1)S(1)}, u32[]{:S(2)}, u32[]{:S(2)}) collective-permute-start(bf16[18,640]{1,0:T(8,128)(2,1)S(1)} %pad_maximum_fusion.8), channel_id=1, source_target_pairs={{0,1},{1,0},{2,3},{3,2},{4,5},{5,4},{6,7},{7,6},{8,9},{9,8},{10,11... | collective-permute-start | bytes 69128 | tf_op jit(solution)/shard_map/ppermute | solution.py:1164
  18.5 2.4 copy-start.10
  43.9 15.8 %copy-start.7 = (bf16[640,640]{1,0:T(8,128)(2,1)}, bf16[640,640]{1,0:T(8,128)(2,1)S(1)}, u32[]{:S(2)}) copy-start(bf16[640,640]{1,0:T(8,128)(2,1)S(1)} %collective-permute-done.2.near_ref) | copy-start | bytes 2457604
  49.4 19.8 %collective-permute-start.3 = (bf16[640,640]{1,0:T(8,128)(2,1)S(1)}, bf16[640,640]{1,0:T(8,128)(2,1)S(1)}, u32[]{:S(2)}, u32[]{:S(2)}) collective-permute-start(bf16[640,640]{1,0:T(8,128)(2,1)S(1)} %collective-permute-done.2.near_ref), channel_id=1, source_target_pairs={{0,2},{2,0},{4,6},{6,4},{8,10},{10,8},{12,14},{14,12},{16,18},{18,... | collective-permute-start | bytes 2457608 | tf_op jit(solution)/shard_map/ppermute | solution.py:1232
  49.7 19.5 %collective-permute-start.4 = (bf16[160,1792]{1,0:T(8,128)(2,1)}, bf16[160,1792]{1,0:T(8,128)(2,1)}, u32[]{:S(2)}, u32[]{:S(2)}) collective-permute-start(bf16[160,1792]{1,0:T(8,128)(2,1)} %get-tuple-element.122), channel_id=1, source_target_pairs={{0,1},{1,0},{2,3},{3,2},{4,5},{5,4},{6,7},{7,6},{8,9},{9,8},{10,11... | collective-permute-start | bytes 1720328 | tf_op jit(solution)/shard_map/ppermute | solution.py:1164
  51.3 39.1 %collective-permute-start.5 = (bf16[320,1792]{1,0:T(8,128)(2,1)}, bf16[320,1792]{1,0:T(8,128)(2,1)}, u32[]{:S(2)}, u32[]{:S(2)}) collective-permute-start(bf16[320,1792]{1,0:T(8,128)(2,1)} %slice_bitcast_fusion), channel_id=1, source_target_pairs={{0,1},{1,0},{2,3},{3,2},{4,5},{5,4},{6,7},{7,6},{8,9},{9,8},{10,11... | collective-permute-start | bytes 3440648 | tf_op jit(solution)/shard_map/ppermute | solution.py:1164
  69.3 26.6 %copy-start.8 = (bf16[640,640]{1,0:T(8,128)(2,1)}, bf16[640,640]{1,0:T(8,128)(2,1)S(1)}, u32[]{:S(2)}) copy-start(bf16[640,640]{1,0:T(8,128)(2,1)S(1)} %collective-permute-done.3.far_ref) | copy-start | bytes 2457604
  69.3 26.6 %all-to-all-start = ((bf16[16,128,128]{2,1,0:T(8,128)(2,1)}), bf16[16,128,128]{2,1,0:T(8,128)(2,1)S(1)}, u32[]{:S(2)}, u32[]{:S(2)}) async-start(bf16[16,128,128]{2,1,0:T(8,128)(2,1)} %bitcast.61), calls=%async_computation | async-start | bytes 1048576 | tf_op jit(solution)/shard_map/all_to_all | solution.py:1193
  72.9 66.6 %all-gather.12.cloned.1.call-start = ((), (), s32[]{:S(2)}) async-start(), calls=%async_computation.7 | async-start | bytes 6127616 | tf_op jit(solution)/shard_map/all_gather | solution.py:1174
  72.9 29.1 %collective-permute-start.6 = (bf16[160,1792]{1,0:T(8,128)(2,1)}, bf16[160,1792]{1,0:T(8,128)(2,1)}, u32[]{:S(2)}, u32[]{:S(2)}) collective-permute-start(bf16[160,1792]{1,0:T(8,128)(2,1)} %get-tuple-element.129), channel_id=1, source_target_pairs={{0,1},{1,0},{2,3},{3,2},{4,5},{5,4},{6,7},{7,6},{8,9},{9,8},{10,11... | collective-permute-start | bytes 1720328 | tf_op jit(solution)/shard_map/ppermute | solution.py:1164
  102.1 75.8 %all-gather.14.cloned.1.call-start = ((), (), s32[]{:S(2)}) async-start(), calls=%async_computation.8 | async-start | bytes 5570560 | tf_op jit(solution)/shard_map/all_gather | solution.py:1174
  102.1 28.6 %collective-permute-start.7 = (bf16[448,1280]{1,0:T(8,128)(2,1)}, bf16[448,1280]{1,0:T(8,128)(2,1)}, u32[]{:S(2)}, u32[]{:S(2)}) collective-permute-start(bf16[448,1280]{1,0:T(8,128)(2,1)} %bitcast.71), channel_id=1, source_target_pairs={{0,1},{1,0},{2,3},{3,2},{4,5},{5,4},{6,7},{7,6},{8,9},{9,8},{10,11... | collective-permute-start | bytes 3440648 | tf_op jit(solution)/shard_map/ppermute | solution.py:1164
  105.1 5.9 %copy-start.24 = (bf16[640,112]{1,0:T(8,128)(2,1)}, bf16[640,112]{1,0:T(8,128)(2,1)S(1)}, u32[]{:S(2)}) copy-start(bf16[640,112]{1,0:T(8,128)(2,1)S(1)} %pad_maximum_fusion.6.own_shared_in_ref) | copy-start | bytes 430084
  105.2 6.5 %copy-start.25 = (bf16[56,1280]{1,0:T(8,128)(2,1)}, bf16[56,1280]{1,0:T(8,128)(2,1)S(1)}, u32[]{:S(2)}) copy-start(bf16[56,1280]{1,0:T(8,128)(2,1)S(1)} %constant_dynamic-slice_fusion.3.own_shared_out_ref) | copy-start | bytes 430084
  105.2 35.1 %copy-start.6 = (bf16[640,1280]{1,0:T(8,128)(2,1)S(1)}, bf16[640,1280]{1,0:T(8,128)(2,1)}, u32[]{:S(2)}) copy-start(bf16[640,1280]{1,0:T(8,128)(2,1)} %wq_ref.1) | copy-start | bytes 4915204
  111.1 23.0 %collective-permute-start.8 = (bf16[640,112]{1,0:T(8,128)(2,1)S(1)}, bf16[640,112]{1,0:T(8,128)(2,1)S(1)}, u32[]{:S(2)}, u32[]{:S(2)}) collective-permute-start(bf16[640,112]{1,0:T(8,128)(2,1)S(1)} %pad_maximum_fusion.6.own_shared_in_ref), channel_id=1, source_target_pairs={{0,1},{1,0},{2,3},{3,2},{4,5},{5,4},{6,7},{7,6},{8,9},{9,8},{10,11... | collective-permute-start | bytes 430088 | tf_op jit(solution)/shard_map/ppermute | solution.py:1164
  111.7 23.9 %collective-permute-start.9 = (bf16[56,1280]{1,0:T(8,128)(2,1)S(1)}, bf16[56,1280]{1,0:T(8,128)(2,1)S(1)}, u32[]{:S(2)}, u32[]{:S(2)}) collective-permute-start(bf16[56,1280]{1,0:T(8,128)(2,1)S(1)} %constant_dynamic-slice_fusion.3.own_shared_out_ref), channel_id=1, source_target_pairs={{0,1},{1,0},{2,3},{3,2},{4,5},{5,4},{6,7},{7,6},{8,9},{9,8},{10,11... | collective-permute-start | bytes 430088 | tf_op jit(solution)/shard_map/ppermute | solution.py:1164
  134.1 8.0 %copy-start.32 = (bf16[640,112]{1,0:T(8,128)(2,1)}, bf16[640,112]{1,0:T(8,128)(2,1)S(1)}, u32[]{:S(2)}) copy-start(bf16[640,112]{1,0:T(8,128)(2,1)S(1)} %collective-permute-done.8.other_shared_in_ref) | copy-start | bytes 430084
  135.6 6.5 %copy-start.33 = (bf16[56,1280]{1,0:T(8,128)(2,1)}, bf16[56,1280]{1,0:T(8,128)(2,1)S(1)}, u32[]{:S(2)}) copy-start(bf16[56,1280]{1,0:T(8,128)(2,1)S(1)} %collective-permute-done.9.other_shared_out_ref) | copy-start | bytes 430084
  139.5 101.6 %reduce-scatter.2.cloned.1.call-start = ((), (), s32[]{:S(2)}) async-start(), calls=%async_computation.9 | async-start | bytes 11141120 | tf_op jit(solution)/shard_map/reduce_scatter | solution.py:1302
  140.4 34.2 %collective-permute-start.10 = (bf16[640,640]{1,0:T(8,128)(2,1)S(1)}, bf16[640,640]{1,0:T(8,128)(2,1)}, u32[]{:S(2)}, u32[]{:S(2)}) collective-permute-start(bf16[640,640]{1,0:T(8,128)(2,1)S(1)} %constant_dynamic-slice_fusion.2), channel_id=1, source_target_pairs={{0,1},{1,0},{2,3},{3,2},{4,5},{5,4},{6,7},{7,6},{8,9},{9,8},{10,11... | collective-permute-start | bytes 2457608 | tf_op jit(solution)/shard_map/ppermute | solution.py:1164
  185.4 4.4 %copy-start.4 = (bf16[640,1280]{1,0:T(8,128)(2,1)S(1)}, bf16[640,1280]{1,0:T(8,128)(2,1)}, u32[]{:S(2)}) copy-start(bf16[640,1280]{1,0:T(8,128)(2,1)} %wv_ref.1) | copy-start | bytes 4915204
  185.4 4.5 %copy-start.5 = (bf16[640,1280]{1,0:T(8,128)(2,1)S(1)}, bf16[640,1280]{1,0:T(8,128)(2,1)}, u32[]{:S(2)}) copy-start(bf16[640,1280]{1,0:T(8,128)(2,1)} %wk_ref.1) | copy-start | bytes 4915204
  186.7 32.4 %collective-permute-start.11 = (bf16[112,640]{1,0:T(8,128)(2,1)S(1)}, bf16[112,640]{1,0:T(8,128)(2,1)S(1)}, u32[]{:S(2)}, u32[]{:S(2)}) collective-permute-start(bf16[112,640]{1,0:T(8,128)(2,1)S(1)} %fusion.5), channel_id=1, source_target_pairs={{0,1},{1,0},{2,3},{3,2},{4,5},{5,4},{6,7},{7,6},{8,9},{9,8},{10,11... | collective-permute-start | bytes 430088 | tf_op jit(solution)/shard_map/ppermute | solution.py:1164
  188.9 29.2 %collective-permute-start.12 = (bf16[56,1280]{1,0:T(8,128)(2,1)S(1)}, bf16[56,1280]{1,0:T(8,128)(2,1)S(1)}, u32[]{:S(2)}, u32[]{:S(2)}) collective-permute-start(bf16[56,1280]{1,0:T(8,128)(2,1)S(1)} %slice.283), channel_id=1, source_target_pairs={{0,1},{1,0},{2,3},{3,2},{4,5},{5,4},{6,7},{7,6},{8,9},{9,8},{10,11... | collective-permute-start | bytes 430088 | tf_op jit(solution)/shard_map/ppermute | solution.py:1164
  191.3 62.6 %collective-permute-start.13 = (bf16[1280,640]{1,0:T(8,128)(2,1)}, bf16[1280,640]{1,0:T(8,128)(2,1)}, u32[]{:S(2)}, u32[]{:S(2)}) collective-permute-start(bf16[1280,640]{1,0:T(8,128)(2,1)} %pad_maximum_fusion), channel_id=1, source_target_pairs={{0,1},{1,0},{2,3},{3,2},{4,5},{5,4},{6,7},{7,6},{8,9},{9,8},{10,11... | collective-permute-start | bytes 4915208 | tf_op jit(solution)/shard_map/ppermute | solution.py:1164
  219.2 36.2 %collective-permute-start.14 = (bf16[448,1280]{1,0:T(8,128)(2,1)}, bf16[448,1280]{1,0:T(8,128)(2,1)S(1)}, u32[]{:S(2)}, u32[]{:S(2)}) collective-permute-start(bf16[448,1280]{1,0:T(8,128)(2,1)} %get-tuple-element.172), channel_id=1, source_target_pairs={{0,1},{1,0},{2,3},{3,2},{4,5},{5,4},{6,7},{7,6},{8,9},{9,8},{10,11... | collective-permute-start | bytes 3440648 | tf_op jit(solution)/shard_map/ppermute | solution.py:1164
  220.1 10.0 %all-to-all-start.1 = ((f32[16,1,128]{2,1,0:T(1,128)}), f32[16,1,128]{2,1,0:T(1,128)S(1)}, u32[]{:S(2)}, u32[]{:S(2)}) async-start(f32[16,1,128]{2,1,0:T(1,128)} %bitcast.16), calls=%async_computation.2 | async-start | bytes 16384 | tf_op jit(solution)/shard_map/all_to_all | solution.py:1193
  241.7 10.6 %copy-start.11 = (bf16[640,1792]{1,0:T(8,128)(2,1)S(1)}, bf16[640,1792]{1,0:T(8,128)(2,1)}, u32[]{:S(2)}) copy-start(bf16[640,1792]{1,0:T(8,128)(2,1)} %get-tuple-element.173) | copy-start | bytes 6881284
  246.8 21.0 %all-to-all-start.2 = ((bf16[16,128,128]{2,1,0:T(8,128)(2,1)}), bf16[16,128,128]{2,1,0:T(8,128)(2,1)}, u32[]{:S(2)}, u32[]{:S(2)}) async-start(bf16[16,128,128]{2,1,0:T(8,128)(2,1)} %get-tuple-element.164), calls=%async_computation.3 | async-start | bytes 1048576 | tf_op jit(solution)/shard_map/all_to_all | solution.py:1193
  252.0 141.0 %all-gather.20.cloned.1.call-start = ((), (), s32[]{:S(2)}) async-start(), calls=%async_computation.12 | async-start | bytes 4874240 | tf_op jit(solution)/shard_map/all_gather | solution.py:1174
  252.4 15.4 %collective-permute-start.15 = (bf16[160,1792]{1,0:T(8,128)(2,1)S(1)}, bf16[160,1792]{1,0:T(8,128)(2,1)}, u32[]{:S(2)}, u32[]{:S(2)}) collective-permute-start(bf16[160,1792]{1,0:T(8,128)(2,1)S(1)} %slice.218), channel_id=1, source_target_pairs={{0,1},{1,0},{2,3},{3,2},{4,5},{5,4},{6,7},{7,6},{8,9},{9,8},{10,11... | collective-permute-start | bytes 1720328 | tf_op jit(solution)/shard_map/ppermute | solution.py:1164
  255.4 12.4 %copy-start.22 = (bf16[448,1280]{1,0:T(8,128)(2,1)}, bf16[448,1280]{1,0:T(8,128)(2,1)S(1)}, u32[]{:S(2)}) copy-start(bf16[448,1280]{1,0:T(8,128)(2,1)S(1)} %collective-permute-done.14) | copy-start | bytes 3440644
  267.9 25.6 %all-to-all-start.3 = ((bf16[16,144,128]{2,1,0:T(8,128)(2,1)}), bf16[16,144,128]{2,1,0:T(8,128)(2,1)S(1)}, u32[]{:S(2)}, u32[]{:S(2)}) async-start(bf16[16,144,128]{2,1,0:T(8,128)(2,1)} %get-tuple-element.181), calls=%async_computation.4 | async-start | bytes 1179648 | tf_op jit(solution)/shard_map/all_to_all | solution.py:1355
  274.5 19.0 %collective-permute-start.16 = (bf16[200,1792]{1,0:T(8,128)(2,1)}, bf16[200,1792]{1,0:T(8,128)(2,1)S(1)}, u32[]{:S(2)}, u32[]{:S(2)}) collective-permute-start(bf16[200,1792]{1,0:T(8,128)(2,1)} %slice.219), channel_id=1, source_target_pairs={{0,1},{1,0},{2,3},{3,2},{4,5},{5,4},{6,7},{7,6},{8,9},{9,8},{10,11... | collective-permute-start | bytes 2150408 | tf_op jit(solution)/shard_map/ppermute | solution.py:1164
  293.5 46.4 %all-to-all-start.4 = ((bf16[16,128,384]{2,1,0:T(8,128)(2,1)}), bf16[16,128,384]{2,1,0:T(8,128)(2,1)S(1)}, u32[]{:S(2)}, u32[]{:S(2)}) async-start(bf16[16,128,384]{2,1,0:T(8,128)(2,1)} %bitcast.57), calls=%async_computation.5 | async-start | bytes 3145728 | tf_op jit(solution)/shard_map/all_to_all | solution.py:1193
  299.6 106.4 %all-gather.18.cloned.1.call-start = ((), (), s32[]{:S(2)}) async-start(), calls=%async_computation.11 | async-start | bytes 11419648 | tf_op jit(solution)/shard_map/all_gather | solution.py:1174
  307.6 7.7 %collective-permute-start.18 = (bf16[656,128]{1,0:T(8,128)(2,1)S(1)}, bf16[656,128]{1,0:T(8,128)(2,1)S(1)}, u32[]{:S(2)}, u32[]{:S(2)}) collective-permute-start(bf16[656,128]{1,0:T(8,128)(2,1)S(1)} %pad_maximum_fusion.5), channel_id=1, source_target_pairs={{0,1},{1,0},{2,3},{3,2},{4,5},{5,4},{6,7},{7,6},{8,9},{9,8},{10,11... | collective-permute-start | bytes 503816 | tf_op jit(solution)/shard_map/ppermute | solution.py:1164
  309.0 18.8 %copy-start.16 = (bf16[640,128]{1,0:T(8,128)(2,1)S(1)}, bf16[640,128]{1,0:T(8,128)(2,1)}, u32[]{:S(2)}) copy-start(bf16[640,128]{1,0:T(8,128)(2,1)} %copy-done.15) | copy-start | bytes 491524
  309.0 18.8 %copy-start.18 = (bf16[640,128]{1,0:T(8,128)(2,1)S(1)}, bf16[640,128]{1,0:T(8,128)(2,1)}, u32[]{:S(2)}) copy-start(bf16[640,128]{1,0:T(8,128)(2,1)} %copy-done.17) | copy-start | bytes 491524
  309.0 18.8 %copy-start.20 = (bf16[640,128]{1,0:T(8,128)(2,1)S(1)}, bf16[640,128]{1,0:T(8,128)(2,1)}, u32[]{:S(2)}) copy-start(bf16[640,128]{1,0:T(8,128)(2,1)} %copy-done.19) | copy-start | bytes 491524
  314.4 13.7 %copy-start.13 = (f32[1280,128]{1,0:T(8,128)S(1)}, f32[1280,128]{1,0:T(8,128)}, u32[]{:S(2)}) copy-start(f32[1280,128]{1,0:T(8,128)} %turned_product.2) | copy-start | bytes 1966084
  314.5 13.3 %collective-permute-start.17 = (bf16[640,384]{1,0:T(8,128)(2,1)S(1)}, bf16[640,384]{1,0:T(8,128)(2,1)S(1)}, u32[]{:S(2)}, u32[]{:S(2)}) collective-permute-start(bf16[640,384]{1,0:T(8,128)(2,1)S(1)} %dynamic-slice_convert_fusion), channel_id=1, source_target_pairs={{0,1},{1,0},{2,3},{3,2},{4,5},{5,4},{6,7},{7,6},{8,9},{9,8},{10,11... | collective-permute-start | bytes 1474568 | tf_op jit(solution)/shard_map/ppermute | solution.py:1164
  329.3 14.0 %copy-start.23 = (bf16[448,1280]{1,0:T(8,128)(2,1)S(1)}, bf16[448,1280]{1,0:T(8,128)(2,1)}, u32[]{:S(2)}) copy-start(bf16[448,1280]{1,0:T(8,128)(2,1)} %copy-done.22) | copy-start | bytes 3440644
  339.9 6.7 %copy-start.3 = (bf16[16,128,384]{2,1,0:T(8,128)(2,1)}, bf16[16,128,384]{2,1,0:T(8,128)(2,1)S(1)}, u32[]{:S(2)}) copy-start(bf16[16,128,384]{2,1,0:T(8,128)(2,1)S(1)} %all-to-all-done.4.got_ref) | copy-start | bytes 4718596
  340.5 43.0 %collective-permute-start.19 = (bf16[640,640]{1,0:T(8,128)(2,1)}, bf16[640,640]{1,0:T(8,128)(2,1)}, u32[]{:S(2)}, u32[]{:S(2)}) collective-permute-start(bf16[640,640]{1,0:T(8,128)(2,1)} %collective-permute-done.10.near_q_ref), channel_id=1, source_target_pairs={{0,2},{2,0},{4,6},{6,4},{8,10},{10,8},{12,14},{14,12},{16,18},{18,... | collective-permute-start | bytes 2457608 | tf_op jit(solution)/shard_map/ppermute | solution.py:1400
  343.0 40.6 %collective-permute-start.20 = (bf16[1280,640]{1,0:T(8,128)(2,1)}, bf16[1280,640]{1,0:T(8,128)(2,1)}, u32[]{:S(2)}, u32[]{:S(2)}) collective-permute-start(bf16[1280,640]{1,0:T(8,128)(2,1)} %collective-permute-done.13.near_rest_ref), channel_id=1, source_target_pairs={{0,2},{2,0},{4,6},{6,4},{8,10},{10,8},{12,14},{14,12},{16,18},{18,... | collective-permute-start | bytes 4915208 | tf_op jit(solution)/shard_map/ppermute | solution.py:1400
  346.5 32.5 %collective-permute-start.22 = (bf16[280,1792]{1,0:T(8,128)(2,1)}, bf16[280,1792]{1,0:T(8,128)(2,1)}, u32[]{:S(2)}, u32[]{:S(2)}) collective-permute-start(bf16[280,1792]{1,0:T(8,128)(2,1)} %slice.235), channel_id=1, source_target_pairs={{0,1},{1,0},{2,3},{3,2},{4,5},{5,4},{6,7},{7,6},{8,9},{9,8},{10,11... | collective-permute-start | bytes 3010568 | tf_op jit(solution)/shard_map/ppermute | solution.py:1164
  355.5 22.6 %copy-start.9 = (f32[1280,128]{1,0:T(8,128)S(1)}, f32[1280,128]{1,0:T(8,128)}, u32[]{:S(2)}) copy-start(f32[1280,128]{1,0:T(8,128)} %turned_product.3) | copy-start | bytes 1966084
  356.7 21.4 %collective-permute-start.21 = (f32[640,16]{1,0:T(8,128)S(1)}, f32[640,16]{1,0:T(8,128)S(1)}, u32[]{:S(2)}, u32[]{:S(2)}) collective-permute-start(f32[640,16]{1,0:T(8,128)S(1)} %slice.252), channel_id=1, source_target_pairs={{0,1},{1,0},{2,3},{3,2},{4,5},{5,4},{6,7},{7,6},{8,9},{9,8},{10,11... | collective-permute-start | bytes 122888 | tf_op jit(solution)/shard_map/ppermute | solution.py:1164
  406.0 11.4 %copy-start.1 = (bf16[448,1280]{1,0:T(8,128)(2,1)S(1)}, bf16[448,1280]{1,0:T(8,128)(2,1)}, u32[]{:S(2)}) copy-start(bf16[448,1280]{1,0:T(8,128)(2,1)} %param.25) | copy-start | bytes 3440644
  (5 other events, 5.5 us)
Sparse Core Ops, SparseCore 0:
  9.7 39.6 all-gather.15
  51.6 48.6 all-gather.9
  102.4 37.0 all-gather.11
  141.5 36.3 all-gather.13
  180.0 60.9 reduce-scatter.1
  268.0 66.2 all-gather.19
  340.0 65.9 all-gather.17

commit v3 on v2

--- a/solution.py
+++ b/solution.py
@@ -634,12 +634,12 @@
     spans, _, packed = got.shape
     half = width // 2
     cut = width // spans
-    block = half // 8
+    block = half // 5
     part = pl.BlockSpec((block, width), lambda r: (r, 0))
     line = pl.BlockSpec((1, half), lambda r: (0, 0))
     return pl.pallas_call(
         functools.partial(place_heads_kernel, cut),
-        grid=(8,),
+        grid=(5,),
         in_specs=[
             pl.BlockSpec(memory_space=pltpu.SMEM),
             pl.BlockSpec((HEADS, block, 3 * HEAD_DIM), lambda r: (0, r, 0)),
@@ -1349,8 +1349,8 @@
         spans,
     )
     arrived = swapped(sent).reshape(length, HEAD_DIM)
-    arrived, shared_grads, cuts, near[1], down_theirs, in_parts[0] = tied(
-        arrived, shared_grads, cuts, near[1], down_theirs, in_parts[0]
+    arrived, shared_grads, near[1], down_theirs, in_parts[0] = tied(
+        arrived, shared_grads, near[1], down_theirs, in_parts[0]
     )
     cuts = lax.all_to_all(
         cuts, "ctx", split_axis=0, concat_axis=0, tiled=True, axis_index_groups=groups

time: 426 us -> 425 us (level)
  no operation moved by 1% of the time
where the time goes in v3:
time: 425 us; the launch traced here: 423 us
  Pallas kernels  154 us (36%)
  waiting for transfers between devices  153 us (36%)
  starting transfers between devices  50.9 us (12%)
  local copies, waits for them, and re-layouts  22.9 us (5%)
  other arithmetic  21.7 us (5%)
  between operations  14.9 us (4%)
  matrix products  5.37 us (1%)
    ppermute x20, waiting for transfers between devices, across(): return lax.ppermute(value, 'fsdp', [(0, 1), (1, 0)])  102 us
    pallas_call x1, Pallas kernels, run_experts(): pl.pallas_call(functools.partial(experts_kernel, capacity, tokens, expert...  32.6 us
    ppermute x20, starting transfers between devices, across(): return lax.ppermute(value, 'fsdp', [(0, 1), (1, 0)])  25.2 us
    pallas_call x2, Pallas kernels, slot_grads(): pl.pallas_call(slot_grads_kernel, grid=(wide // (2 * HEAD_DIM),), in_spec...  23.6 us
    all_to_all x4, waiting for transfers between devices, swapped(): return lax.all_to_all(value, 'ctx', split_axis=0, concat_axis=0, tiled=True)  21.7 us
    all_to_all x4, starting transfers between devices, swapped(): return lax.all_to_all(value, 'ctx', split_axis=0, concat_axis=0, tiled=True)  18.4 us
    pallas_call x1, Pallas kernels, attend_back(): pl.pallas_call(functools.partial(attend_back_kernel, ring), grid=(length...  17.6 us
    all_gather x6, waiting for transfers between devices, everyone(): lax.all_gather(value, 'ctx', axis=0, tiled=True, axis_index_groups=groups)  17.5 us
  transfers between devices with their start and end apart: 35, of which 18 were waited for; matrix products, arithmetic and copies ran while one was open for 11% of the time, Pallas kernels for 34%

profile of v3, /device:TPU:0, one launch (start us, length us, event | category | flops | bytes accessed | tf_op | source)
XLA Modules:
  0.0 423.0 jit_solution(1639832076124560373)
XLA Ops:
  9.1 1.1 constant_dynamic-slice_fusion.7
  10.9 3.0 collective-permute-start
  15.0 2.0 collective-permute-start.1
  18.6 1.6 multiply_add_fusion
  23.9 19.4 %collective-permute-done.1 = bf16[18,640]{1,0:T(8,128)(2,1)S(1)} collective-permute-done((bf16[18,640]{1,0:T(8,128)(2,1)S(1)}, bf16[18,640]{1,0:T(8,128)(2,1)S(1)}, u32[]{:S(2)}, u32[]{:S(2)}) %collective-permute-start.1) | collective-permute-done | bytes 23072 | tf_op jit(solution)/shard_map/ppermute | solution.py:1164
  43.9 5.5 %all-gather.16.cloned.1.call-done = bf16[1,2048,1280]{2,1,0:T(8,128)(2,1)} async-done(((bf16[1,128,1280]{2,1,0:T(8,128)(2,1)}), bf16[1,2048,1280]{2,1,0:T(8,128)(2,1)}) %all-gather.16.cloned.1.call-update) | async-done | bytes 5242896 | tf_op jit(solution)/shard_map/all_gather | solution.py:1174
  49.7 1.6 collective-permute-start.4
  51.7 8.0 %project.1 = (bf16[2048,1280]{1,0:T(8,128)(2,1)}, bf16[2048,128]{1,0:T(8,128)(2,1)}, bf16[2048,128]{1,0:T(8,128)(2,1)}, bf16[2048,128]{1,0:T(8,128)(2,1)}) custom-call(s32[1]{0:T(128)} %bitcast.side_ref, bf16[2048,1280]{1,0:T(8,128)(2,1)} %bitcast.46, f32[1,1280]{1,0:T(1,128)} %get-tuple-element.112.gain_ref, bf16[640,384]{1,0:T(8,128)(2,1)} %copy-done.14, ...), custom_call_target="tpu_custom_call" | custom-call | flops 2013265920 | bytes 10485760 | tf_op jit(solution)/shard_map/project/pallas_call | solution.py:289
  59.7 9.5 %attend.1 = (f32[2048,128]{1,0:T(8,128)}, f32[1,2048]{1,0:T(1,128)}, bf16[2048,128]{1,0:T(8,128)(2,1)}) custom-call(bf16[2048,128]{1,0:T(8,128)(2,1)} %get-tuple-element.116.q_ref, bf16[2048,128]{1,0:T(8,128)(2,1)} %get-tuple-element.117.k_ref, bf16[2048,128]{1,0:T(8,128)(2,1)} %get-tuple-element.118.v_ref), custom_call_target="tpu_custom_call" | custom-call | flops 1073741824 | bytes 3145728 | tf_op jit(solution)/shard_map/attend/pallas_call | solution.py:134
  69.3 3.6 all-to-all-start
  72.9 1.6 collective-permute-start.6
  76.5 13.9 %collective-permute-done.5.middle_in_ref = bf16[320,1792]{1,0:T(8,128)(2,1)} collective-permute-done((bf16[320,1792]{1,0:T(8,128)(2,1)}, bf16[320,1792]{1,0:T(8,128)(2,1)}, u32[]{:S(2)}, u32[]{:S(2)}) %collective-permute-start.5) | collective-permute-done | bytes 1146912 | tf_op jit(solution)/shard_map/ppermute | solution.py:1164
  90.4 5.4 %all-to-all-done.got_ref = bf16[16,128,128]{2,1,0:T(8,128)(2,1)S(1)} async-done(((bf16[16,128,128]{2,1,0:T(8,128)(2,1)}), bf16[16,128,128]{2,1,0:T(8,128)(2,1)S(1)}, u32[]{:S(2)}, u32[]{:S(2)}) %all-to-all-start) | async-done | bytes 524320 | tf_op jit(solution)/shard_map/all_to_all | solution.py:1193
  96.6 4.8 %mix.1 = (f32[128,1280]{1,0:T(8,128)}, bf16[128,1408]{1,0:T(8,128)(2,1)}, f32[128,1]{1,0:T(8,128)}, f32[128,128]{1,0:T(8,128)}, bf16[128,1280]{1,0:T(8,128)(2,1)}) custom-call(s32[2]{0:T(128)} %pad_add_fusion.spot_ref, bf16[16,128,128]{2,1,0:T(8,128)(2,1)} %copy-done.12, bf16[640,1280]{1,0:T(8,128)(2,1)} %own_ref.3, bf16[640,640]{1,0:T(8,128)(2,1)} %copy-done.7, ...), custom_call_target="tpu_custom_call" | custom-call | tf_op jit(solution)/shard_map/mix/pallas_call | solution.py:392
  102.1 1.7 collective-permute-start.7
  103.8 1.2 constant_dynamic-slice_fusion.5
  105.2 5.8 %pick_slots.1.grad_slots_ref = bf16[896,1280]{1,0:T(8,128)(2,1)} custom-call(s32[1]{0:T(128)} %bitcast.2.here_ref, bf16[2048,1408]{1,0:T(8,128)(2,1)} %all-gather.10.cloned.1.call-done.g_ref), custom_call_target="tpu_custom_call" | custom-call | flops 1174405120 | bytes 8650752 | tf_op jit(solution)/shard_map/pick_slots/pallas_call | solution.py:747
  111.7 1.4 collective-permute-start.9
  113.1 17.6 %collective-permute-done.7.other_down_ref = bf16[448,1280]{1,0:T(8,128)(2,1)} collective-permute-done((bf16[448,1280]{1,0:T(8,128)(2,1)}, bf16[448,1280]{1,0:T(8,128)(2,1)}, u32[]{:S(2)}, u32[]{:S(2)}) %collective-permute-start.7) | collective-permute-done | bytes 1146912 | tf_op jit(solution)/shard_map/ppermute | solution.py:1164
  130.7 3.4 collective-permute-done.8.other_shared_in_ref
  134.1 1.5 collective-permute-done.9.other_shared_out_ref
  135.6 3.8 all-gather.12.cloned.1.call-done.normed_ref.left_ref
  140.4 1.6 collective-permute-start.10
  142.1 32.6 %experts.1 = (bf16[896,1280]{1,0:T(8,128)(2,1)}, bf16[896,896]{1,0:T(8,128)(2,1)}, bf16[896,1280]{1,0:T(8,128)(2,1)}, bf16[896,1792]{1,0:T(8,128)(2,1)}, bf16[20...) custom-call(s32[3]{0:T(128)} %pad_add_fusion.1.here_ref, ...), custom_call_target="tpu_custom_call" | custom-call | flops 20000000000 | bytes 40000000 | tf_op jit(solution)/shard_map/experts/pallas_call | solution.py:935
  174.7 3.2 all-gather.14.cloned.1.call-done.left_ref
  177.9 7.5 %shared_products.1 = (f32[256,1280]{1,0:T(8,128)}, f32[128,1280]{1,0:T(8,128)}) custom-call(bf16[2048,256]{1,0:T(8,128)(2,1)} %get-tuple-element.150.grad_ref, bf16[2048,1408]{1,0:T(8,128)(2,1)} %all-gather.12.cloned.1.call-done.normed_ref.left_ref, bf16[2048,128]{1,0:T(8,128)(2,1)} %get-tuple-element.151.hidden_ref, ...), custom_call_target="tpu_custom_call" | custom-call | flops 2013265920 | bytes 15728640 | tf_op jit(solution)/shard_map/shared_products/pallas_call | solution.py:1055
  185.4 1.2 fusion.24
  186.7 1.3 collective-permute-start.11
  190.0 1.3 pad_maximum_fusion
  191.3 1.2 collective-permute-start.13
  193.3 1.2 concatenate.65
  194.5 14.4 %slot_grads.2 = (f32[640,1792]{1,0:T(8,128)}, bf16[640,1792]{1,0:T(8,128)(2,1)}) custom-call(s32[1]{0:T(128)} %bitcast.side_ref, bf16[896,1280]{1,0:T(8,128)(2,1)} %get-tuple-element.147.left_ref, bf16[896,1792]{1,0:T(8,128)(2,1)} %get-tuple-element.148.right_ref), custom_call_target="tpu_custom_call" | custom-call | flops 4110417920 | bytes 12386304 | tf_op jit(solution)/shard_map/slot_grads/pallas_call | solution.py:1012
  208.9 9.2 %slot_grads.3 = (f32[448,1280]{1,0:T(8,128)}, bf16[448,1280]{1,0:T(8,128)(2,1)}) custom-call(s32[1]{0:T(128)} %bitcast.side_ref, bf16[896,896]{1,0:T(8,128)(2,1)} %get-tuple-element.167.left_ref, bf16[896,1280]{1,0:T(8,128)(2,1)} %get-tuple-element.168.right_ref), custom_call_target="tpu_custom_call" | custom-call | flops 2055208960 | bytes 7340032 | tf_op jit(solution)/shard_map/slot_grads/pallas_call | solution.py:1012
  220.1 3.5 all-to-all-start.1
  224.4 5.7 %all-to-all-done.1 = f32[16,1,128]{2,1,0:T(1,128)S(1)} async-done(((f32[16,1,128]{2,1,0:T(1,128)}), f32[16,1,128]{2,1,0:T(1,128)S(1)}, u32[]{:S(2)}, u32[]{:S(2)}) %all-to-all-start.1) | async-done | bytes 8224 | tf_op jit(solution)/shard_map/all_to_all | solution.py:1193
  230.2 10.8 %reduce-scatter.2.cloned.1.call-done.sums_ref = bf16[128,2560]{1,0:T(8,128)(2,1)} async-done(((bf16[2048,2560]{1,0:T(8,128)(2,1)}), bf16[128,2560]{1,0:T(8,128)(2,1)}) %reduce-scatter.2.cloned.1.call-update) | async-done | bytes 655376 | tf_op jit(solution)/shard_map/reduce_scatter | solution.py:1302
  241.7 5.2 %mix_back.1 = (bf16[16,128,128]{2,1,0:T(8,128)(2,1)}, bf16[16,144,128]{2,1,0:T(8,128)(2,1)}, f32[128,1280]{1,0:T(8,128)}, bf16[128,1280]{1,0:T(8,128)(2,1)}) custom-call(s32[2]{0:T(128)} %pad_add_fusion.spot_ref, bf16[128,2560]{1,0:T(8,128)(2,1)} %reduce-scatter.2.cloned.1.call-done.sums_ref, f32[128,128]{1,0:T(8,128)} %get-tuple-element.157.gates_ref, ...), custom_call_target="tpu_custom_call" | custom-call | tf_op jit(solution)/shard_map/mix_back/pallas_call | solution.py:479
  246.8 5.2 %all-to-all-start.2 = ((bf16[16,128,128]{2,1,0:T(8,128)(2,1)}), bf16[16,128,128]{2,1,0:T(8,128)(2,1)}, u32[]{:S(2)}, u32[]{:S(2)}) async-start(bf16[16,128,128]{2,1,0:T(8,128)(2,1)} %get-tuple-element.163), calls=%async_computation.3 | async-start | bytes 1048576 | tf_op jit(solution)/shard_map/all_to_all | solution.py:1193
  252.4 1.5 collective-permute-start.15
  253.9 1.5 collective-permute-done.14
  255.4 12.4 %collective-permute-done.15 = bf16[160,1792]{1,0:T(8,128)(2,1)} collective-permute-done((bf16[160,1792]{1,0:T(8,128)(2,1)S(1)}, bf16[160,1792]{1,0:T(8,128)(2,1)}, u32[]{:S(2)}, u32[]{:S(2)}) %collective-permute-start.15) | collective-permute-done | bytes 573472 | tf_op jit(solution)/shard_map/ppermute | solution.py:1164
  267.9 5.7 %all-to-all-start.3 = ((bf16[16,144,128]{2,1,0:T(8,128)(2,1)}), bf16[16,144,128]{2,1,0:T(8,128)(2,1)S(1)}, u32[]{:S(2)}, u32[]{:S(2)}) async-start(bf16[16,144,128]{2,1,0:T(8,128)(2,1)} %get-tuple-element.179), calls=%async_computation.4 | async-start | bytes 1179648 | tf_op jit(solution)/shard_map/all_to_all | solution.py:1355
  274.5 1.4 collective-permute-start.16
  275.9 17.6 %attend_back.1 = (bf16[2048,384]{1,0:T(8,128)(2,1)}, bf16[2048,384]{1,0:T(8,128)(2,1)}) custom-call(bf16[2048,128]{1,0:T(8,128)(2,1)} %get-tuple-element.116.q_ref, bf16[2048,128]{1,0:T(8,128)(2,1)} %get-tuple-element.117.k_ref, bf16[2048,128]{1,0:T(8,128)(2,1)} %get-tuple-element.118.v_ref, bf16[2048,128]{1,0:T(8,128)(2,1)} %bitcast.20.grad_ref, ...), custom_call_target="tpu_custom_call" | custom-call | flops 2684354560 | bytes 5242880 | tf_op jit(solution)/shard_map/attend_back/pallas_call | solution.py:243
  293.5 6.1 %all-to-all-start.4 = ((bf16[16,128,384]{2,1,0:T(8,128)(2,1)}), bf16[16,128,384]{2,1,0:T(8,128)(2,1)S(1)}, u32[]{:S(2)}, u32[]{:S(2)}) async-start(bf16[16,128,384]{2,1,0:T(8,128)(2,1)} %bitcast.57), calls=%async_computation.5 | async-start | bytes 3145728 | tf_op jit(solution)/shard_map/all_to_all | solution.py:1193
  300.6 5.9 %turned_product.2 = f32[1280,128]{1,0:T(8,128)} custom-call(s32[1]{0:T(128)} %bitcast.side_ref, bf16[2048,1280]{1,0:T(8,128)(2,1)} %all-gather.14.cloned.1.call-done.left_ref, bf16[2048,128]{1,0:T(8,128)(2,1)} %bitcast.47), custom_call_target="tpu_custom_call" | custom-call | flops 671088640 | bytes 5242880 | tf_op jit(solution)/shard_map/turned_product/pallas_call | solution.py:1098
  307.6 1.5 collective-permute-start.18
  309.0 5.4 %fusion.27 = f32[1280,384]{1,0:T(8,128)S(1)} fusion(bf16[2048,1280]{1,0:T(8,128)(2,1)} %get-tuple-element.162, bf16[2048,384]{1,0:T(8,128)(2,1)} %get-tuple-element.180), kind=kOutput, calls=%fused_computation.97 | convolution fusion | flops 2013265920 | bytes 8781824 | tf_op jit(solution)/shard_map/dot_general | solution.py:36
  315.3 12.5 %collective-permute-done.17 = bf16[640,384]{1,0:T(8,128)(2,1)S(1)} collective-permute-done((bf16[640,384]{1,0:T(8,128)(2,1)S(1)}, bf16[640,384]{1,0:T(8,128)(2,1)S(1)}, u32[]{:S(2)}, u32[]{:S(2)}) %collective-permute-start.17) | collective-permute-done | bytes 491552 | tf_op jit(solution)/shard_map/ppermute | solution.py:1164
  329.3 10.6 %all-to-all-done.4.got_ref = bf16[16,128,384]{2,1,0:T(8,128)(2,1)S(1)} async-done(((bf16[16,128,384]{2,1,0:T(8,128)(2,1)}), bf16[16,128,384]{2,1,0:T(8,128)(2,1)S(1)}, u32[]{:S(2)}, u32[]{:S(2)}) %all-to-all-start.4) | async-done | bytes 1572896 | tf_op jit(solution)/shard_map/all_to_all | solution.py:1193
  340.7 2.2 slice.235
  343.3 3.2 add_bitcast_fusion
  346.5 1.4 collective-permute-start.22
  347.9 1.5 convert_add_fusion.1
  349.4 6.0 %turned_product.3 = f32[1280,128]{1,0:T(8,128)} custom-call(s32[1]{0:T(128)} %bitcast.side_ref, bf16[2048,1408]{1,0:T(8,128)(2,1)} %all-gather.12.cloned.1.call-done.normed_ref.left_ref, bf16[2048,128]{1,0:T(8,128)(2,1)} %bitcast.48), custom_call_target="tpu_custom_call" | custom-call | flops 671088640 | bytes 5242880 | tf_op jit(solution)/shard_map/turned_product/pallas_call | solution.py:1098
  355.5 1.2 slice.252
  357.1 1.5 convert_add_fusion.2
  358.7 19.4 %collective-permute-done.21 = f32[640,16]{1,0:T(8,128)S(1)} collective-permute-done((f32[640,16]{1,0:T(8,128)S(1)}, f32[640,16]{1,0:T(8,128)S(1)}, u32[]{:S(2)}, u32[]{:S(2)}) %collective-permute-start.21) | collective-permute-done | bytes 40992 | tf_op jit(solution)/shard_map/ppermute | solution.py:1164
  379.0 2.1 convert_add_fusion
  381.1 2.4 maximum_bitcast_fusion
  383.5 9.5 %inputs_back.1 = f32[128,1280]{1,0:T(8,128)} custom-call(s32[1]{0:T(128)} %bitcast.side_ref, s32[1]{0:T(128)} %bitcast.1.core_ref, bf16[16,128,384]{2,1,0:T(8,128)(2,1)} %copy-done.3, bf16[640,1280]{1,0:T(8,128)(2,1)} %wq_ref.1, bf16[640,1280]{1,0:T(8,128)(2,1)} %wk_ref.1, bf16[640,1280]{1,0:T(8,128)(2,1)} %wv_ref.1, ...), custom_call_target="tpu_custom_call" | custom-call | tf_op jit(solution)/shard_map/inputs_back/pallas_call | solution.py:554
  393.0 8.0 %place_shared.1 = (f32[640,1792]{1,0:T(8,128)}, f32[448,1280]{1,0:T(8,128)}) custom-call(s32[1]{0:T(128)} %bitcast.side_ref, bf16[16,224,640]{2,1,0:T(8,128)(2,1)} %bitcast.49), custom_call_target="tpu_custom_call" | custom-call | tf_op jit(solution)/shard_map/place_shared/pallas_call | solution.py:689
  401.0 5.0 %all-gather.18.cloned.1.call-done = bf16[10496,512]{1,0:T(8,128)(2,1)} async-done(((bf16[656,512]{1,0:T(8,128)(2,1)}), bf16[10496,512]{1,0:T(8,128)(2,1)}) %all-gather.18.cloned.1.call-update) | async-done | bytes 10747920 | tf_op jit(solution)/shard_map/all_gather | solution.py:1174
  406.0 10.1 %place_heads.1 = (f32[640,1280]{1,0:T(8,128)}, f32[640,1280]{1,0:T(8,128)}, f32[640,1280]{1,0:T(8,128)}, f32[640,1280]{1,0:T(8,128)}, f32[5,128]{1,0:T(8,128)}, /*index=5*/f32[5,128]{1,0:T(8,128)}) custom-call(s32[1]{0:T(128)} %bitcast.side_ref, bf16[16,656,512]{2,1,0:T(8,128)(2,1)} %bitcast.43, bf16[16,656,512]{2,1,0:T(8,128)(2,1)} %bitcast.44, ...), custom_call_target="tpu_custom_call" | custom-call | tf_op jit(solution)/shard_map/place_heads/pallas_call | solution.py:640
  (187 shorter events, 29.7 us)
Async XLA Ops:
  7.2 98.0 %copy-start = (bf16[448,1280]{1,0:T(8,128)(2,1)S(1)}, bf16[448,1280]{1,0:T(8,128)(2,1)}, u32[]{:S(2)}) copy-start(bf16[448,1280]{1,0:T(8,128)(2,1)} %param.25) | copy-start | bytes 3440644
  7.2 6.7 %copy-start.2 = (bf16[640,1280]{1,0:T(8,128)(2,1)S(1)}, bf16[640,1280]{1,0:T(8,128)(2,1)}, u32[]{:S(2)}) copy-start(bf16[640,1280]{1,0:T(8,128)(2,1)} %own_ref.3) | copy-start | bytes 4915204
  7.2 7.7 %copy-start.27 = (bf16[640]{0:T(1024)(128)(2,1)S(1)}, bf16[640]{0:T(1024)(128)(2,1)}, u32[]{:S(2)}) copy-start(bf16[640]{0:T(1024)(128)(2,1)} %param.17) | copy-start | bytes 3844
  7.2 7.7 %copy-start.30 = (bf16[640]{0:T(1024)(128)(2,1)S(1)}, bf16[640]{0:T(1024)(128)(2,1)}, u32[]{:S(2)}) copy-start(bf16[640]{0:T(1024)(128)(2,1)} %param.22) | copy-start | bytes 3844
  7.2 7.7 %copy-start.26 = (bf16[640,16]{0,1:T(8,128)(2,1)S(1)}, bf16[640,16]{0,1:T(8,128)(2,1)}, u32[]{:S(2)}) copy-start(bf16[640,16]{0,1:T(8,128)(2,1)} %param.23) | copy-start | bytes 61444
  7.2 42.2 %all-gather.16.cloned.1.call-start = ((), (), s32[]{:S(2)}) async-start(), calls=%async_computation.10 | async-start | bytes 5570560 | tf_op jit(solution)/shard_map/all_gather | solution.py:1174
  8.0 9.1 %copy-start.31 = (f32[16]{0:T(128)S(1)}, f32[16]{0:T(128)}, u32[]{:S(2)}) copy-start(f32[16]{0:T(128)} %constant.125) | copy-start | bytes 196
  8.0 94.1 %all-gather.10.cloned.1.call-start = ((), (), s32[]{:S(2)}) async-start(), calls=%async_computation.6 | async-start | bytes 6127616 | tf_op jit(solution)/shard_map/all_gather | solution.py:1174
  9.0 8.4 %copy-start.28 = (s32[1,128,7]{1,0,2:T(1,128)S(1)}, s32[1,128,7]{1,0,2:T(1,128)}, u32[]{:S(2)}) copy-start(s32[1,128,7]{1,0,2:T(1,128)} %param.28) | copy-start | bytes 10756
  9.0 8.5 %copy-start.29 = (s32[1,1,896]{2,1,0:T(1,128)S(1)}, s32[1,1,896]{2,1,0:T(1,128)}, u32[]{:S(2)}) copy-start(s32[1,1,896]{2,1,0:T(1,128)} %param.29) | copy-start | bytes 10756
  10.9 9.3 %copy-start.14 = (bf16[640,384]{1,0:T(8,128)(2,1)}, bf16[640,384]{1,0:T(8,128)(2,1)S(1)}, u32[]{:S(2)}) copy-start(bf16[640,384]{1,0:T(8,128)(2,1)S(1)} %pad_maximum_fusion.2.own_ref) | copy-start | bytes 1474564
  10.9 33.0 %collective-permute-start = (bf16[640,384]{1,0:T(8,128)(2,1)S(1)}, bf16[640,384]{1,0:T(8,128)(2,1)}, u32[]{:S(2)}, u32[]{:S(2)}) collective-permute-start(bf16[640,384]{1,0:T(8,128)(2,1)S(1)} %pad_maximum_fusion.2.own_ref), channel_id=1, source_target_pairs={{0,1},{1,0},{2,3},{3,2},{4,5},{5,4},{6,7},{7,6},{8,9},{9,8},{10,11... | collective-permute-start | bytes 1474568 | tf_op jit(solution)/shard_map/ppermute | solution.py:1164
  14.8 29.1 %collective-permute-start.2 = (bf16[640,640]{1,0:T(8,128)(2,1)}, bf16[640,640]{1,0:T(8,128)(2,1)S(1)}, u32[]{:S(2)}, u32[]{:S(2)}) collective-permute-start(bf16[640,640]{1,0:T(8,128)(2,1)} %constant_dynamic-slice_fusion.6), channel_id=1, source_target_pairs={{0,1},{1,0},{2,3},{3,2},{4,5},{5,4},{6,7},{7,6},{8,9},{9,8},{10,11... | collective-permute-start | bytes 2457608 | tf_op jit(solution)/shard_map/ppermute | solution.py:1164
  15.0 28.3 %collective-permute-start.1 = (bf16[18,640]{1,0:T(8,128)(2,1)S(1)}, bf16[18,640]{1,0:T(8,128)(2,1)S(1)}, u32[]{:S(2)}, u32[]{:S(2)}) collective-permute-start(bf16[18,640]{1,0:T(8,128)(2,1)S(1)} %pad_maximum_fusion.8), channel_id=1, source_target_pairs={{0,1},{1,0},{2,3},{3,2},{4,5},{5,4},{6,7},{7,6},{8,9},{9,8},{10,11... | collective-permute-start | bytes 69128 | tf_op jit(solution)/shard_map/ppermute | solution.py:1164
  18.5 2.4 copy-start.10
  43.9 15.8 %copy-start.7 = (bf16[640,640]{1,0:T(8,128)(2,1)}, bf16[640,640]{1,0:T(8,128)(2,1)S(1)}, u32[]{:S(2)}) copy-start(bf16[640,640]{1,0:T(8,128)(2,1)S(1)} %collective-permute-done.2.near_ref) | copy-start | bytes 2457604
  49.4 19.8 %collective-permute-start.3 = (bf16[640,640]{1,0:T(8,128)(2,1)S(1)}, bf16[640,640]{1,0:T(8,128)(2,1)S(1)}, u32[]{:S(2)}, u32[]{:S(2)}) collective-permute-start(bf16[640,640]{1,0:T(8,128)(2,1)S(1)} %collective-permute-done.2.near_ref), channel_id=1, source_target_pairs={{0,2},{2,0},{4,6},{6,4},{8,10},{10,8},{12,14},{14,12},{16,18},{18,... | collective-permute-start | bytes 2457608 | tf_op jit(solution)/shard_map/ppermute | solution.py:1232
  49.7 19.5 %collective-permute-start.4 = (bf16[160,1792]{1,0:T(8,128)(2,1)}, bf16[160,1792]{1,0:T(8,128)(2,1)}, u32[]{:S(2)}, u32[]{:S(2)}) collective-permute-start(bf16[160,1792]{1,0:T(8,128)(2,1)} %get-tuple-element.121), channel_id=1, source_target_pairs={{0,1},{1,0},{2,3},{3,2},{4,5},{5,4},{6,7},{7,6},{8,9},{9,8},{10,11... | collective-permute-start | bytes 1720328 | tf_op jit(solution)/shard_map/ppermute | solution.py:1164
  51.3 39.1 %collective-permute-start.5 = (bf16[320,1792]{1,0:T(8,128)(2,1)}, bf16[320,1792]{1,0:T(8,128)(2,1)}, u32[]{:S(2)}, u32[]{:S(2)}) collective-permute-start(bf16[320,1792]{1,0:T(8,128)(2,1)} %slice_bitcast_fusion), channel_id=1, source_target_pairs={{0,1},{1,0},{2,3},{3,2},{4,5},{5,4},{6,7},{7,6},{8,9},{9,8},{10,11... | collective-permute-start | bytes 3440648 | tf_op jit(solution)/shard_map/ppermute | solution.py:1164
  69.3 26.6 %copy-start.8 = (bf16[640,640]{1,0:T(8,128)(2,1)}, bf16[640,640]{1,0:T(8,128)(2,1)S(1)}, u32[]{:S(2)}) copy-start(bf16[640,640]{1,0:T(8,128)(2,1)S(1)} %collective-permute-done.3.far_ref) | copy-start | bytes 2457604
  69.3 26.6 %all-to-all-start = ((bf16[16,128,128]{2,1,0:T(8,128)(2,1)}), bf16[16,128,128]{2,1,0:T(8,128)(2,1)S(1)}, u32[]{:S(2)}, u32[]{:S(2)}) async-start(bf16[16,128,128]{2,1,0:T(8,128)(2,1)} %bitcast.61), calls=%async_computation | async-start | bytes 1048576 | tf_op jit(solution)/shard_map/all_to_all | solution.py:1193
  72.9 66.6 %all-gather.12.cloned.1.call-start = ((), (), s32[]{:S(2)}) async-start(), calls=%async_computation.7 | async-start | bytes 6127616 | tf_op jit(solution)/shard_map/all_gather | solution.py:1174
  72.9 29.1 %collective-permute-start.6 = (bf16[160,1792]{1,0:T(8,128)(2,1)}, bf16[160,1792]{1,0:T(8,128)(2,1)}, u32[]{:S(2)}, u32[]{:S(2)}) collective-permute-start(bf16[160,1792]{1,0:T(8,128)(2,1)} %get-tuple-element.128), channel_id=1, source_target_pairs={{0,1},{1,0},{2,3},{3,2},{4,5},{5,4},{6,7},{7,6},{8,9},{9,8},{10,11... | collective-permute-start | bytes 1720328 | tf_op jit(solution)/shard_map/ppermute | solution.py:1164
  102.1 75.8 %all-gather.14.cloned.1.call-start = ((), (), s32[]{:S(2)}) async-start(), calls=%async_computation.8 | async-start | bytes 5570560 | tf_op jit(solution)/shard_map/all_gather | solution.py:1174
  102.1 28.6 %collective-permute-start.7 = (bf16[448,1280]{1,0:T(8,128)(2,1)}, bf16[448,1280]{1,0:T(8,128)(2,1)}, u32[]{:S(2)}, u32[]{:S(2)}) collective-permute-start(bf16[448,1280]{1,0:T(8,128)(2,1)} %bitcast.71), channel_id=1, source_target_pairs={{0,1},{1,0},{2,3},{3,2},{4,5},{5,4},{6,7},{7,6},{8,9},{9,8},{10,11... | collective-permute-start | bytes 3440648 | tf_op jit(solution)/shard_map/ppermute | solution.py:1164
  105.1 5.9 %copy-start.24 = (bf16[640,112]{1,0:T(8,128)(2,1)}, bf16[640,112]{1,0:T(8,128)(2,1)S(1)}, u32[]{:S(2)}) copy-start(bf16[640,112]{1,0:T(8,128)(2,1)S(1)} %pad_maximum_fusion.6.own_shared_in_ref) | copy-start | bytes 430084
  105.2 6.5 %copy-start.25 = (bf16[56,1280]{1,0:T(8,128)(2,1)}, bf16[56,1280]{1,0:T(8,128)(2,1)S(1)}, u32[]{:S(2)}) copy-start(bf16[56,1280]{1,0:T(8,128)(2,1)S(1)} %constant_dynamic-slice_fusion.3.own_shared_out_ref) | copy-start | bytes 430084
  105.2 35.1 %copy-start.6 = (bf16[640,1280]{1,0:T(8,128)(2,1)S(1)}, bf16[640,1280]{1,0:T(8,128)(2,1)}, u32[]{:S(2)}) copy-start(bf16[640,1280]{1,0:T(8,128)(2,1)} %wq_ref.1) | copy-start | bytes 4915204
  111.1 23.0 %collective-permute-start.8 = (bf16[640,112]{1,0:T(8,128)(2,1)S(1)}, bf16[640,112]{1,0:T(8,128)(2,1)S(1)}, u32[]{:S(2)}, u32[]{:S(2)}) collective-permute-start(bf16[640,112]{1,0:T(8,128)(2,1)S(1)} %pad_maximum_fusion.6.own_shared_in_ref), channel_id=1, source_target_pairs={{0,1},{1,0},{2,3},{3,2},{4,5},{5,4},{6,7},{7,6},{8,9},{9,8},{10,11... | collective-permute-start | bytes 430088 | tf_op jit(solution)/shard_map/ppermute | solution.py:1164
  111.7 23.9 %collective-permute-start.9 = (bf16[56,1280]{1,0:T(8,128)(2,1)S(1)}, bf16[56,1280]{1,0:T(8,128)(2,1)S(1)}, u32[]{:S(2)}, u32[]{:S(2)}) collective-permute-start(bf16[56,1280]{1,0:T(8,128)(2,1)S(1)} %constant_dynamic-slice_fusion.3.own_shared_out_ref), channel_id=1, source_target_pairs={{0,1},{1,0},{2,3},{3,2},{4,5},{5,4},{6,7},{7,6},{8,9},{9,8},{10,11... | collective-permute-start | bytes 430088 | tf_op jit(solution)/shard_map/ppermute | solution.py:1164
  134.1 8.0 %copy-start.32 = (bf16[640,112]{1,0:T(8,128)(2,1)}, bf16[640,112]{1,0:T(8,128)(2,1)S(1)}, u32[]{:S(2)}) copy-start(bf16[640,112]{1,0:T(8,128)(2,1)S(1)} %collective-permute-done.8.other_shared_in_ref) | copy-start | bytes 430084
  135.6 6.5 %copy-start.33 = (bf16[56,1280]{1,0:T(8,128)(2,1)}, bf16[56,1280]{1,0:T(8,128)(2,1)S(1)}, u32[]{:S(2)}) copy-start(bf16[56,1280]{1,0:T(8,128)(2,1)S(1)} %collective-permute-done.9.other_shared_out_ref) | copy-start | bytes 430084
  139.5 101.6 %reduce-scatter.2.cloned.1.call-start = ((), (), s32[]{:S(2)}) async-start(), calls=%async_computation.9 | async-start | bytes 11141120 | tf_op jit(solution)/shard_map/reduce_scatter | solution.py:1302
  140.4 34.2 %collective-permute-start.10 = (bf16[640,640]{1,0:T(8,128)(2,1)S(1)}, bf16[640,640]{1,0:T(8,128)(2,1)}, u32[]{:S(2)}, u32[]{:S(2)}) collective-permute-start(bf16[640,640]{1,0:T(8,128)(2,1)S(1)} %constant_dynamic-slice_fusion.2), channel_id=1, source_target_pairs={{0,1},{1,0},{2,3},{3,2},{4,5},{5,4},{6,7},{7,6},{8,9},{9,8},{10,11... | collective-permute-start | bytes 2457608 | tf_op jit(solution)/shard_map/ppermute | solution.py:1164
  185.4 4.4 %copy-start.4 = (bf16[640,1280]{1,0:T(8,128)(2,1)S(1)}, bf16[640,1280]{1,0:T(8,128)(2,1)}, u32[]{:S(2)}) copy-start(bf16[640,1280]{1,0:T(8,128)(2,1)} %wv_ref.1) | copy-start | bytes 4915204
  185.4 4.5 %copy-start.5 = (bf16[640,1280]{1,0:T(8,128)(2,1)S(1)}, bf16[640,1280]{1,0:T(8,128)(2,1)}, u32[]{:S(2)}) copy-start(bf16[640,1280]{1,0:T(8,128)(2,1)} %wk_ref.1) | copy-start | bytes 4915204
  186.7 32.4 %collective-permute-start.11 = (bf16[112,640]{1,0:T(8,128)(2,1)S(1)}, bf16[112,640]{1,0:T(8,128)(2,1)S(1)}, u32[]{:S(2)}, u32[]{:S(2)}) collective-permute-start(bf16[112,640]{1,0:T(8,128)(2,1)S(1)} %fusion.5), channel_id=1, source_target_pairs={{0,1},{1,0},{2,3},{3,2},{4,5},{5,4},{6,7},{7,6},{8,9},{9,8},{10,11... | collective-permute-start | bytes 430088 | tf_op jit(solution)/shard_map/ppermute | solution.py:1164
  188.9 29.2 %collective-permute-start.12 = (bf16[56,1280]{1,0:T(8,128)(2,1)S(1)}, bf16[56,1280]{1,0:T(8,128)(2,1)S(1)}, u32[]{:S(2)}, u32[]{:S(2)}) collective-permute-start(bf16[56,1280]{1,0:T(8,128)(2,1)S(1)} %slice.283), channel_id=1, source_target_pairs={{0,1},{1,0},{2,3},{3,2},{4,5},{5,4},{6,7},{7,6},{8,9},{9,8},{10,11... | collective-permute-start | bytes 430088 | tf_op jit(solution)/shard_map/ppermute | solution.py:1164
  191.3 62.6 %collective-permute-start.13 = (bf16[1280,640]{1,0:T(8,128)(2,1)}, bf16[1280,640]{1,0:T(8,128)(2,1)}, u32[]{:S(2)}, u32[]{:S(2)}) collective-permute-start(bf16[1280,640]{1,0:T(8,128)(2,1)} %pad_maximum_fusion), channel_id=1, source_target_pairs={{0,1},{1,0},{2,3},{3,2},{4,5},{5,4},{6,7},{7,6},{8,9},{9,8},{10,11... | collective-permute-start | bytes 4915208 | tf_op jit(solution)/shard_map/ppermute | solution.py:1164
  219.2 36.2 %collective-permute-start.14 = (bf16[448,1280]{1,0:T(8,128)(2,1)}, bf16[448,1280]{1,0:T(8,128)(2,1)S(1)}, u32[]{:S(2)}, u32[]{:S(2)}) collective-permute-start(bf16[448,1280]{1,0:T(8,128)(2,1)} %get-tuple-element.170), channel_id=1, source_target_pairs={{0,1},{1,0},{2,3},{3,2},{4,5},{5,4},{6,7},{7,6},{8,9},{9,8},{10,11... | collective-permute-start | bytes 3440648 | tf_op jit(solution)/shard_map/ppermute | solution.py:1164
  220.1 10.0 %all-to-all-start.1 = ((f32[16,1,128]{2,1,0:T(1,128)}), f32[16,1,128]{2,1,0:T(1,128)S(1)}, u32[]{:S(2)}, u32[]{:S(2)}) async-start(f32[16,1,128]{2,1,0:T(1,128)} %bitcast.16), calls=%async_computation.2 | async-start | bytes 16384 | tf_op jit(solution)/shard_map/all_to_all | solution.py:1193
  241.7 10.6 %copy-start.11 = (bf16[640,1792]{1,0:T(8,128)(2,1)S(1)}, bf16[640,1792]{1,0:T(8,128)(2,1)}, u32[]{:S(2)}) copy-start(bf16[640,1792]{1,0:T(8,128)(2,1)} %get-tuple-element.171) | copy-start | bytes 6881284
  246.8 21.0 %all-to-all-start.2 = ((bf16[16,128,128]{2,1,0:T(8,128)(2,1)}), bf16[16,128,128]{2,1,0:T(8,128)(2,1)}, u32[]{:S(2)}, u32[]{:S(2)}) async-start(bf16[16,128,128]{2,1,0:T(8,128)(2,1)} %get-tuple-element.163), calls=%async_computation.3 | async-start | bytes 1048576 | tf_op jit(solution)/shard_map/all_to_all | solution.py:1193
  252.0 141.0 %all-gather.20.cloned.1.call-start = ((), (), s32[]{:S(2)}) async-start(), calls=%async_computation.12 | async-start | bytes 4874240 | tf_op jit(solution)/shard_map/all_gather | solution.py:1174
  252.4 15.4 %collective-permute-start.15 = (bf16[160,1792]{1,0:T(8,128)(2,1)S(1)}, bf16[160,1792]{1,0:T(8,128)(2,1)}, u32[]{:S(2)}, u32[]{:S(2)}) collective-permute-start(bf16[160,1792]{1,0:T(8,128)(2,1)S(1)} %slice.218), channel_id=1, source_target_pairs={{0,1},{1,0},{2,3},{3,2},{4,5},{5,4},{6,7},{7,6},{8,9},{9,8},{10,11... | collective-permute-start | bytes 1720328 | tf_op jit(solution)/shard_map/ppermute | solution.py:1164
  255.4 12.4 %copy-start.22 = (bf16[448,1280]{1,0:T(8,128)(2,1)}, bf16[448,1280]{1,0:T(8,128)(2,1)S(1)}, u32[]{:S(2)}) copy-start(bf16[448,1280]{1,0:T(8,128)(2,1)S(1)} %collective-permute-done.14) | copy-start | bytes 3440644
  267.9 25.6 %all-to-all-start.3 = ((bf16[16,144,128]{2,1,0:T(8,128)(2,1)}), bf16[16,144,128]{2,1,0:T(8,128)(2,1)S(1)}, u32[]{:S(2)}, u32[]{:S(2)}) async-start(bf16[16,144,128]{2,1,0:T(8,128)(2,1)} %get-tuple-element.179), calls=%async_computation.4 | async-start | bytes 1179648 | tf_op jit(solution)/shard_map/all_to_all | solution.py:1355
  274.5 19.0 %collective-permute-start.16 = (bf16[200,1792]{1,0:T(8,128)(2,1)}, bf16[200,1792]{1,0:T(8,128)(2,1)S(1)}, u32[]{:S(2)}, u32[]{:S(2)}) collective-permute-start(bf16[200,1792]{1,0:T(8,128)(2,1)} %slice.219), channel_id=1, source_target_pairs={{0,1},{1,0},{2,3},{3,2},{4,5},{5,4},{6,7},{7,6},{8,9},{9,8},{10,11... | collective-permute-start | bytes 2150408 | tf_op jit(solution)/shard_map/ppermute | solution.py:1164
  293.5 46.4 %all-to-all-start.4 = ((bf16[16,128,384]{2,1,0:T(8,128)(2,1)}), bf16[16,128,384]{2,1,0:T(8,128)(2,1)S(1)}, u32[]{:S(2)}, u32[]{:S(2)}) async-start(bf16[16,128,384]{2,1,0:T(8,128)(2,1)} %bitcast.57), calls=%async_computation.5 | async-start | bytes 3145728 | tf_op jit(solution)/shard_map/all_to_all | solution.py:1193
  299.6 106.4 %all-gather.18.cloned.1.call-start = ((), (), s32[]{:S(2)}) async-start(), calls=%async_computation.11 | async-start | bytes 11419648 | tf_op jit(solution)/shard_map/all_gather | solution.py:1174
  307.6 7.7 %collective-permute-start.18 = (bf16[656,128]{1,0:T(8,128)(2,1)S(1)}, bf16[656,128]{1,0:T(8,128)(2,1)S(1)}, u32[]{:S(2)}, u32[]{:S(2)}) collective-permute-start(bf16[656,128]{1,0:T(8,128)(2,1)S(1)} %pad_maximum_fusion.5), channel_id=1, source_target_pairs={{0,1},{1,0},{2,3},{3,2},{4,5},{5,4},{6,7},{7,6},{8,9},{9,8},{10,11... | collective-permute-start | bytes 503816 | tf_op jit(solution)/shard_map/ppermute | solution.py:1164
  309.0 18.8 %copy-start.16 = (bf16[640,128]{1,0:T(8,128)(2,1)S(1)}, bf16[640,128]{1,0:T(8,128)(2,1)}, u32[]{:S(2)}) copy-start(bf16[640,128]{1,0:T(8,128)(2,1)} %copy-done.15) | copy-start | bytes 491524
  309.0 18.8 %copy-start.18 = (bf16[640,128]{1,0:T(8,128)(2,1)S(1)}, bf16[640,128]{1,0:T(8,128)(2,1)}, u32[]{:S(2)}) copy-start(bf16[640,128]{1,0:T(8,128)(2,1)} %copy-done.17) | copy-start | bytes 491524
  309.0 18.8 %copy-start.20 = (bf16[640,128]{1,0:T(8,128)(2,1)S(1)}, bf16[640,128]{1,0:T(8,128)(2,1)}, u32[]{:S(2)}) copy-start(bf16[640,128]{1,0:T(8,128)(2,1)} %copy-done.19) | copy-start | bytes 491524
  314.4 13.7 %copy-start.13 = (f32[1280,128]{1,0:T(8,128)S(1)}, f32[1280,128]{1,0:T(8,128)}, u32[]{:S(2)}) copy-start(f32[1280,128]{1,0:T(8,128)} %turned_product.2) | copy-start | bytes 1966084
  314.5 13.3 %collective-permute-start.17 = (bf16[640,384]{1,0:T(8,128)(2,1)S(1)}, bf16[640,384]{1,0:T(8,128)(2,1)S(1)}, u32[]{:S(2)}, u32[]{:S(2)}) collective-permute-start(bf16[640,384]{1,0:T(8,128)(2,1)S(1)} %dynamic-slice_convert_fusion), channel_id=1, source_target_pairs={{0,1},{1,0},{2,3},{3,2},{4,5},{5,4},{6,7},{7,6},{8,9},{9,8},{10,11... | collective-permute-start | bytes 1474568 | tf_op jit(solution)/shard_map/ppermute | solution.py:1164
  329.3 14.0 %copy-start.23 = (bf16[448,1280]{1,0:T(8,128)(2,1)S(1)}, bf16[448,1280]{1,0:T(8,128)(2,1)}, u32[]{:S(2)}) copy-start(bf16[448,1280]{1,0:T(8,128)(2,1)} %copy-done.22) | copy-start | bytes 3440644
  339.9 6.7 %copy-start.3 = (bf16[16,128,384]{2,1,0:T(8,128)(2,1)}, bf16[16,128,384]{2,1,0:T(8,128)(2,1)S(1)}, u32[]{:S(2)}) copy-start(bf16[16,128,384]{2,1,0:T(8,128)(2,1)S(1)} %all-to-all-done.4.got_ref) | copy-start | bytes 4718596
  340.5 43.0 %collective-permute-start.19 = (bf16[640,640]{1,0:T(8,128)(2,1)}, bf16[640,640]{1,0:T(8,128)(2,1)}, u32[]{:S(2)}, u32[]{:S(2)}) collective-permute-start(bf16[640,640]{1,0:T(8,128)(2,1)} %collective-permute-done.10.near_q_ref), channel_id=1, source_target_pairs={{0,2},{2,0},{4,6},{6,4},{8,10},{10,8},{12,14},{14,12},{16,18},{18,... | collective-permute-start | bytes 2457608 | tf_op jit(solution)/shard_map/ppermute | solution.py:1400
  343.0 40.6 %collective-permute-start.20 = (bf16[1280,640]{1,0:T(8,128)(2,1)}, bf16[1280,640]{1,0:T(8,128)(2,1)}, u32[]{:S(2)}, u32[]{:S(2)}) collective-permute-start(bf16[1280,640]{1,0:T(8,128)(2,1)} %collective-permute-done.13.near_rest_ref), channel_id=1, source_target_pairs={{0,2},{2,0},{4,6},{6,4},{8,10},{10,8},{12,14},{14,12},{16,18},{18,... | collective-permute-start | bytes 4915208 | tf_op jit(solution)/shard_map/ppermute | solution.py:1400
  346.5 32.5 %collective-permute-start.22 = (bf16[280,1792]{1,0:T(8,128)(2,1)}, bf16[280,1792]{1,0:T(8,128)(2,1)}, u32[]{:S(2)}, u32[]{:S(2)}) collective-permute-start(bf16[280,1792]{1,0:T(8,128)(2,1)} %slice.235), channel_id=1, source_target_pairs={{0,1},{1,0},{2,3},{3,2},{4,5},{5,4},{6,7},{7,6},{8,9},{9,8},{10,11... | collective-permute-start | bytes 3010568 | tf_op jit(solution)/shard_map/ppermute | solution.py:1164
  355.5 22.6 %copy-start.9 = (f32[1280,128]{1,0:T(8,128)S(1)}, f32[1280,128]{1,0:T(8,128)}, u32[]{:S(2)}) copy-start(f32[1280,128]{1,0:T(8,128)} %turned_product.3) | copy-start | bytes 1966084
  356.7 21.4 %collective-permute-start.21 = (f32[640,16]{1,0:T(8,128)S(1)}, f32[640,16]{1,0:T(8,128)S(1)}, u32[]{:S(2)}, u32[]{:S(2)}) collective-permute-start(f32[640,16]{1,0:T(8,128)S(1)} %slice.252), channel_id=1, source_target_pairs={{0,1},{1,0},{2,3},{3,2},{4,5},{5,4},{6,7},{7,6},{8,9},{9,8},{10,11... | collective-permute-start | bytes 122888 | tf_op jit(solution)/shard_map/ppermute | solution.py:1164
  406.0 10.1 %copy-start.1 = (bf16[448,1280]{1,0:T(8,128)(2,1)S(1)}, bf16[448,1280]{1,0:T(8,128)(2,1)}, u32[]{:S(2)}) copy-start(bf16[448,1280]{1,0:T(8,128)(2,1)} %param.25) | copy-start | bytes 3440644
  (5 other events, 5.5 us)
Sparse Core Ops, SparseCore 0:
  9.7 39.6 all-gather.15
  51.6 48.6 all-gather.9
  102.4 37.0 all-gather.11
  141.5 36.3 all-gather.13
  180.0 60.9 reduce-scatter.1
  268.0 66.2 all-gather.19
  340.0 65.9 all-gather.17
